TPU v7x, 256 devices: a whole 4x4x8 slice. The times are simulated.
256 devices in a mesh: particle: 4 (over z_hi), slab: 32 (over y, x, z_lo), half: 2 (over core).
Axes of the slice: x: 4, y: 4, z: 8 (z_hi: 4, z_lo: 2; z = z_hi * 2 + z_lo), core: 2. Of those that a mesh axis runs over, the one named last changes fastest.
Arguments:
- tiles: bfloat16 [2, 256, 128, 4096], P('half', 'particle', 'slab'), may hold values from -1.5 to 1.5
- tile_index: int32 [2, 256, 128], P('half', 'particle', 'slab'), may hold values from 0 to 255
- pose_bin: int32 [2, 256], P('half', 'particle'), may hold values from 0 to 31
- bin_gain: bfloat16 [2, 32], P('half'), may hold values from 0.25 to 4
- cutoffs: int32 [6], replicated, may hold values from 32 to 128, as said below
Outputs:
- refined: float32 [2, 256, 256, 256], P('half', None, ('particle', 'slab'))
Inputs may be any that keep to these rules, and one draw needn't show every extreme that they name: `cutoffs`: the last band's cutoff is 128.
All inputs are finite; a program needn't handle non-finite values.
Results may differ from a plain program's by a relative error of at most 0.0003.
Values sent between devices are 32-bit elements; how exact they have to be, the bound alone decides.
No kernel may reach another device: no remote copies, remote signals or barrier semaphores. Data moves between devices by JAX's collectives and lax.ppermute only.
A program may use at most 64 MiB of HBM per device.

v0:
```python
import math

import jax
import jax.numpy as jnp
import numpy as np
from jax import lax
from jax.experimental import pallas as pl
from jax.experimental.pallas import tpu as pltpu
from jax.sharding import PartitionSpec as P

BOX = 256
HALF = BOX // 2
TILE_ROWS = 8
BLOCKS = BOX // TILE_ROWS
BANDS = 6
GROUPS = 4
SLABS = 32
SENDERS = GROUPS * SLABS
PER = BANDS * 8
LANES = 128
error_floor = 1.0
bf16 = jnp.bfloat16
f32 = jnp.float32
VMEM = pl.BlockSpec(memory_space=pltpu.VMEM)
SMEM = pl.BlockSpec(memory_space=pltpu.SMEM)


def split(table):
    high = table.astype(np.float32).astype(jnp.bfloat16)
    low = (table - high.astype(np.float64)).astype(np.float32).astype(jnp.bfloat16)
    return high, low


def angles(left, right):
    return (np.outer(left, right) % BOX) * (2.0 * math.pi / BOX)


def tables():
    places = np.arange(BOX)
    y_order = (places % 64) * 4 + places // 64
    ky_order = (places % BLOCKS) * TILE_ROWS + places // BLOCKS
    turn = angles(y_order, ky_order)
    cosine, sine = np.cos(turn), np.sin(turn)
    along_y = np.block([[cosine, -sine], [sine, cosine]])
    turn = angles(places, places)
    cosine, sine = np.cos(turn), np.sin(turn)
    along_x_even = np.concatenate([cosine, -sine], axis=0)
    along_x_odd = np.concatenate([sine, cosine], axis=0)
    sender = np.arange(SENDERS)
    group, slab = sender // SLABS, sender % SLABS
    plane = slab * 8 + group * 2 + (slab >= SLABS // 2)
    turn = angles(places, plane)
    even, odd = np.cos(turn), -np.sin(turn)
    odd[:, 0] = np.cos(math.pi * places)
    along_z = np.concatenate([even, odd], axis=1) / BOX
    return split(along_y) + split(along_x_even) + split(along_x_odd) + split(along_z)


def two(value):
    high = value.astype(bf16)
    return high, (value - high.astype(f32)).astype(bf16)


def dot(a, b):
    return jnp.dot(a, b, preferred_element_type=f32)


def planes_kernel(
    cut_ref, kz_ref, keep_ref, come_ref, yh_ref, yl_ref, eh_ref, el_ref, oh_ref, ol_ref, out_ref, sh, sl, dh, dl, radius
):
    alone = kz_ref[0] == 0
    last = come_ref[0:1, 0:1]
    for i in range(16):
        kept = keep_ref[:, i * BOX : (i + 1) * BOX]
        come = jnp.where(alone, 0.0, come_ref[:, i * BOX : (i + 1) * BOX])
        rows = pl.ds(i * BLOCKS, BLOCKS)
        sh[rows, :], sl[rows, :] = two(kept + come)
        dh[rows, :], dl[rows, :] = two(kept - come)
    line = lax.broadcasted_iota(jnp.int32, (BOX, BOX), 0)
    col = lax.broadcasted_iota(jnp.int32, (BOX, BOX), 1)
    ky = (line & (BLOCKS - 1)) * TILE_ROWS + (line >> 5)
    ky = ((ky + HALF) & (BOX - 1)) - HALF
    kx = ((col + HALF) & (BOX - 1)) - HALF
    kz = ((kz_ref[0] + HALF) & (BOX - 1)) - HALF
    radius[...] = (ky * ky + kx * kx + kz * kz).astype(f32)

    @pl.loop(0, BANDS)
    def _(b):
        limit = (cut_ref[b] * cut_ref[b]).astype(f32)
        mask = jnp.where(radius[...] <= limit, 1.0, 0.0).astype(bf16)
        mask = jnp.concatenate([mask, mask], axis=0)

        def plane(high_ref, low_ref, th_ref, tl_ref):
            high, low = high_ref[...] * mask, low_ref[...] * mask
            mid = dot(yh_ref[...], high) + dot(yl_ref[...], high) + dot(yh_ref[...], low)
            mid = jnp.concatenate([mid[:BOX], mid[BOX:]], axis=1)
            high, low = two(mid)
            return dot(high, th_ref[...]) + dot(low, th_ref[...]) + dot(high, tl_ref[...])

        even = plane(sh, sl, eh_ref, el_ref)
        odd = plane(dh, dl, oh_ref, ol_ref)
        top = jnp.where(cut_ref[b] >= HALF, last, 0.0)
        odd = jnp.where(alone, jnp.broadcast_to(top, odd.shape), odd)
        for c, part in enumerate((even, odd)):
            for j in range(4):
                for side in range(2):
                    block = part[j * 64 : (j + 1) * 64, side * LANES : (side + 1) * LANES]
                    out_ref[pl.ds(side * PER + b * 8 + c * 4 + j, 64, stride=2 * PER), :] = block


def depth_kernel(core_ref, come_ref, zh_ref, zl_ref, own_ref, other_ref):
    b = pl.program_id(0)
    for out_ref, core in ((own_ref, core_ref[0]), (other_ref, 1 - core_ref[0])):
        start = b * 8 + core * 2
        sides = [
            jnp.concatenate(
                [come_ref[pl.ds(start + c * 4 + j, SENDERS, stride=PER), :] for j in range(2)], axis=1
            )
            for c in range(2)
        ]
        high, low = two(jnp.concatenate(sides, axis=0))
        full = dot(zh_ref[...], high) + dot(zl_ref[...], high) + dot(zh_ref[...], low)
        out_ref[0, 0] = full[:, :LANES]
        out_ref[0, 1] = full[:, LANES:]


def square_kernel(own_ref, other_ref, first_ref, second_ref, edge_ref):
    b = pl.program_id(0)
    lane = lax.broadcasted_iota(jnp.int32, (BOX, LANES), 1)

    @pl.when(b == 0)
    def _():
        edge_ref[...] = jnp.zeros_like(edge_ref)

    edge = edge_ref[...]
    for row, ref in enumerate((first_ref, second_ref)):
        gap = own_ref[0, row] - other_ref[0, row]
        square = gap * gap
        ref[0] = square
        spot = row * 32 + b
        edge = jnp.where(lane == spot, pltpu.roll(square, spot + 1, 1), edge)
        edge = jnp.where(lane == spot + 64, pltpu.roll(square, spot + 64, 1), edge)
    edge_ref[...] = edge


def blend_kernel(
    swap_ref,
    own_ref,
    other_ref,
    first_ref,
    second_ref,
    before_ref,
    after_ref,
    edge_ref,
    edge_before_ref,
    edge_after_ref,
    out_a_ref,
    out_b_ref,
    sums,
):
    b = pl.program_id(0)
    lane = lax.broadcasted_iota(jnp.int32, (BOX, LANES), 1)

    @pl.when(b == 0)
    def _():
        sums[...] = jnp.zeros_like(sums)

    middle = first_ref[0] + second_ref[0]
    edge = edge_ref[...]
    edge = edge + pltpu.roll(edge, LANES - 32, 1)
    for row in range(2):
        if row == 0:
            tall = middle + before_ref[0]
            border = edge + pltpu.roll(edge_before_ref[...], LANES - 32, 1)
        else:
            tall = middle + after_ref[0]
            border = edge + edge_after_ref[...]
        left = jnp.where(lane == 0, pltpu.roll(border, LANES - b, 1), pltpu.roll(tall, 1, 1))
        right = jnp.where(lane == LANES - 1, pltpu.roll(border, 63 - b, 1), pltpu.roll(tall, LANES - 1, 1))
        wide = tall + left + right
        full = wide + pltpu.roll(wide, 1, 0) + pltpu.roll(wide, BOX - 1, 0)
        weight = 1.0 / (full / 27.0 + error_floor)
        sums[row, 0] += weight * own_ref[0, row]
        sums[row, 1] += weight * other_ref[0, row]
        sums[row, 2] += weight

    @pl.when(b == BANDS - 1)
    def _():
        swap = swap_ref[0] == 1
        for row in range(2):
            mine = sums[row, 0] / sums[row, 2]
            theirs = sums[row, 1] / sums[row, 2]
            out_a_ref[row] = jnp.where(swap, theirs, mine)
            out_b_ref[row] = jnp.where(swap, mine, theirs)


def place(group, slab, half):
    return (group * SLABS + slab) * 2 + half


def mirror_pairs():
    pairs = []
    for group in range(GROUPS):
        for slab in range(SLABS):
            if slab < SLABS // 2:
                goal = (GROUPS - 1 - group, SLABS - 1 - slab)
            elif group:
                goal = (GROUPS - group, SLABS - 1 - slab)
            else:
                goal = (0, (SLABS - slab) % (SLABS // 2))
            pairs.append((group * SLABS + slab, goal[0] * SLABS + goal[1]))
    return pairs


def row_pairs(step, flip):
    pairs = []
    for n in range(SENDERS):
        goal = (n + step) % SENDERS
        for side in range(2):
            pairs.append((n // 2 * 4 + side * 2 + n % 2, goal // 2 * 4 + (side ^ flip) * 2 + goal % 2))
    return pairs


def home_pairs(flip):
    pairs = []
    for chips in range(SENDERS // 2):
        for side in range(2):
            for half in range(2):
                pairs.append((chips * 4 + side * 2 + half, chips * 4 + half * 2 + (side ^ flip)))
    return pairs


def on_device(tiles, tile_index, pose_bin, bin_gain, cutoffs):
    slab_pos = lax.axis_index("slab")
    group_pos = lax.axis_index("particle")
    half_pos = lax.axis_index("half")
    side_pos = slab_pos % 2
    everyone = ("particle", "slab", "half")
    slot_count = BOX // SLABS * BLOCKS
    tile_width = 2 * TILE_ROWS * BOX
    touched = tile_index.shape[2]
    flat_tiles = tiles[0].reshape(-1, tile_width)
    entry_slot = tile_index[0].reshape(-1)
    bin_ids = jnp.arange(bin_gain.shape[1], dtype=jnp.int32)
    particle_gain = jnp.sum(
        jnp.where(pose_bin[0][:, None] == bin_ids[None, :], bin_gain[0][None, :].astype(f32), 0.0),
        axis=1,
    )
    entry_gain = jnp.repeat(particle_gain, touched)
    slot_ids = jnp.arange(slot_count, dtype=jnp.int32)
    placing = jnp.where(slot_ids[:, None] == entry_slot[None, :], entry_gain[None, :], 0.0).astype(bf16)
    owned = lax.psum_scatter(
        jnp.dot(placing, flat_tiles, preferred_element_type=f32), "particle", scatter_dimension=0, tiled=True
    )
    late = (slab_pos >= SLABS // 2).astype(jnp.int32)
    kept = lax.dynamic_slice_in_dim(owned, late * BLOCKS, BLOCKS, 0)
    leaving = lax.dynamic_slice_in_dim(owned, (1 - late) * BLOCKS, BLOCKS, 0)
    come = lax.ppermute(leaving, ("particle", "slab"), mirror_pairs())
    plane = (slab_pos * 8 + group_pos * 2 + late).reshape(1)

    constants = [jnp.asarray(t) for t in tables()]
    square = (2 * BOX, BOX)
    sent = pl.pallas_call(
        planes_kernel,
        out_shape=jax.ShapeDtypeStruct((SENDERS * PER, LANES), f32),
        in_specs=[SMEM, SMEM] + [VMEM] * 8,
        out_specs=VMEM,
        scratch_shapes=[pltpu.VMEM(square, bf16)] * 4 + [pltpu.VMEM((BOX, BOX), f32)],
        name="planes",
    )(cutoffs, plane, kept, come, *constants[:6])
    gathered = lax.all_to_all(
        sent.reshape(SENDERS, PER, LANES), ("particle", "slab"), split_axis=0, concat_axis=0, tiled=True
    ).reshape(SENDERS * PER, LANES)

    rows_block = (1, 2, BOX, LANES)
    rows_spec = pl.BlockSpec(rows_block, lambda b: (b, 0, 0, 0))
    rows_shape = jax.ShapeDtypeStruct((BANDS, 2, BOX, LANES), f32)
    row_spec = pl.BlockSpec((1, BOX, LANES), lambda b: (b, 0, 0))
    row_shape = jax.ShapeDtypeStruct((BANDS, BOX, LANES), f32)
    edge_spec = pl.BlockSpec((BOX, LANES), lambda b: (0, 0))
    edge_shape = jax.ShapeDtypeStruct((BOX, LANES), f32)
    own, leaving = pl.pallas_call(
        depth_kernel,
        grid=(BANDS,),
        out_shape=(rows_shape, rows_shape),
        in_specs=[
            SMEM,
            pl.BlockSpec((SENDERS * PER, LANES), lambda b: (0, 0)),
            pl.BlockSpec((BOX, BOX), lambda b: (0, 0)),
            pl.BlockSpec((BOX, BOX), lambda b: (0, 0)),
        ],
        out_specs=(rows_spec, rows_spec),
        name="depth",
    )(half_pos.reshape(1), gathered, *constants[6:])
    other = lax.ppermute(leaving, "half", [(0, 1), (1, 0)])
    first, second, edge = pl.pallas_call(
        square_kernel,
        grid=(BANDS,),
        out_shape=(row_shape, row_shape, edge_shape),
        in_specs=[rows_spec, rows_spec],
        out_specs=(row_spec, row_spec, edge_spec),
        name="square",
    )(own, other)
    before = lax.ppermute(second, everyone, row_pairs(1, 0))
    after = lax.ppermute(first, everyone, row_pairs(-1, 0))
    edge_here = lax.ppermute(edge, everyone, row_pairs(0, 1))
    edge_before = lax.ppermute(edge, everyone, row_pairs(1, 1))
    edge_after = lax.ppermute(edge, everyone, row_pairs(-1, 1))
    swap = (side_pos != half_pos).astype(jnp.int32).reshape(1)
    block_spec = pl.BlockSpec((2, BOX, LANES), lambda b: (0, 0, 0))
    block_shape = jax.ShapeDtypeStruct((2, BOX, LANES), f32)
    near, far = pl.pallas_call(
        blend_kernel,
        grid=(BANDS,),
        out_shape=(block_shape, block_shape),
        in_specs=[SMEM, rows_spec, rows_spec] + [row_spec] * 4 + [edge_spec] * 3,
        out_specs=(block_spec, block_spec),
        scratch_shapes=[pltpu.VMEM((2, 3, BOX, LANES), f32)],
        name="blend",
    )(swap, own, other, first, second, before, after, edge_here, edge_before, edge_after)
    near = lax.ppermute(near, everyone, home_pairs(0))
    far = lax.ppermute(far, everyone, home_pairs(1))
    low = jnp.where(half_pos == 0, near, far)
    high = jnp.where(half_pos == 0, far, near)
    refined = jnp.concatenate([low, high], axis=2)
    return jnp.transpose(refined, (1, 0, 2))[None]


def solution(mesh):
    placed = (
        P("half", "particle", "slab", None),
        P("half", "particle", "slab"),
        P("half", "particle"),
        P("half", None),
        P(),
    )
    return jax.shard_map(
        on_device,
        mesh=mesh,
        in_specs=placed,
        out_specs=P("half", None, ("particle", "slab"), None),
        check_vma=False,
    )
```

profile of v0, /device:TPU:1, one launch (start us, length us, event | category | flops | bytes accessed | tf_op | source)
XLA Modules:
  0.0 321.8 jit_solution(14258538251412631192)
XLA Ops:
  6.5 0.0 reduce-scatter.2.cloned.1.call-start
  6.5 0.7 bitcast_convert_fusion
  7.2 0.7 select_reduce_fusion
  7.9 0.1 broadcast_in_dim.43
  8.0 0.1 broadcast_in_dim.44
  8.1 0.8 copy.17
  8.9 0.1 eq.38
  9.0 2.5 reshape_squeeze.3
  11.6 2.7 fusion
  14.2 0.0 reduce-scatter.2.cloned.1.call-update
  14.3 88.4 %reduce-scatter.2.cloned.1.call-done = f32[64,4096]{1,0:T(8,128)} async-done(((f32[256,4096]{1,0:T(8,128)}), f32[64,4096]{1,0:T(8,128)}) %reduce-scatter.2.cloned.1.call-update) | async-done | bytes 1048592 | tf_op jit(solution)/shard_map/reduce_scatter | solution.py:252
  102.6 2.1 constant_dynamic-slice_fusion
  104.7 3.4 %collective-permute-start = (f32[32,4096]{1,0:T(8,128)S(1)}, f32[32,4096]{1,0:T(8,128)S(1)}, u32[]{:S(2)}, u32[]{:S(2)}) collective-permute-start(f32[32,4096]{1,0:T(8,128)S(1)} %get-tuple-element.19), channel_id=1, source_target_pairs={{0,254},{2,252},{4,250},{6,248},{8,246},{10,244},{12,242},{14,240}... | collective-permute-start | bytes 1572872 | tf_op jit(solution)/shard_map/ppermute | solution.py:258
  108.1 20.5 %collective-permute-done.come_ref = f32[32,4096]{1,0:T(8,128)S(1)} collective-permute-done((f32[32,4096]{1,0:T(8,128)S(1)}, f32[32,4096]{1,0:T(8,128)S(1)}, u32[]{:S(2)}, u32[]{:S(2)}) %collective-permute-start) | collective-permute-done | bytes 524320 | tf_op jit(solution)/shard_map/ppermute | solution.py:258
  128.5 0.0 copy-start.4
  128.5 0.8 copy-done.4
  129.3 20.5 %planes.1 = f32[6144,128]{1,0:T(8,128)} custom-call(s32[6]{0:T(128)} %cut_ref.1, s32[1]{0:T(128)} %bitcast.2.kz_ref, f32[32,4096]{1,0:T(8,128)} %get-tuple-element.20.keep_ref, f32[32,4096]{1,0:T(8,128)} %copy-done.4, bf16[512,512]{1,0:T(8,128)(2,1)} %constant.57.clone.yh_ref, bf16[512,512]{1,0:T(8,128)(2,1)} %constant.58.clone.yl_ref, ...), custom_call_target="tpu_custom_call" | custom-call | tf_op jit(solution)/shard_map/planes/pallas_call | solution.py:263
  149.8 16.9 %all-to-all-start = ((f32[128,48,128]{2,1,0:T(8,128)}), f32[128,48,128]{2,1,0:T(8,128)S(1)}, u32[]{:S(2)}, u32[]{:S(2)}) async-start(f32[128,48,128]{2,1,0:T(8,128)} %bitcast.15), calls=%async_computation.1 | async-start | bytes 6291456 | tf_op jit(solution)/shard_map/all_to_all | solution.py:271
  166.7 75.2 %all-to-all-done = f32[128,48,128]{2,1,0:T(8,128)S(1)} async-done(((f32[128,48,128]{2,1,0:T(8,128)}), f32[128,48,128]{2,1,0:T(8,128)S(1)}, u32[]{:S(2)}, u32[]{:S(2)}) %all-to-all-start) | async-done | bytes 3145760 | tf_op jit(solution)/shard_map/all_to_all | solution.py:271
  241.9 0.0 copy-start
  241.9 1.6 copy-done
  243.6 6.4 %depth.1 = (f32[6,2,256,128]{3,2,1,0:T(8,128)}, f32[6,2,256,128]{3,2,1,0:T(8,128)}) custom-call(s32[1]{0:T(128)} %bitcast.1.core_ref, f32[6144,128]{1,0:T(8,128)} %bitcast.14, bf16[256,256]{1,0:T(8,128)(2,1)} %constant.63.clone.zh_ref, bf16[256,256]{1,0:T(8,128)(2,1)} %constant.64.clone.zl_ref), custom_call_target="tpu_custom_call" | custom-call | tf_op jit(solution)/shard_map/depth/pallas_call | solution.py:282
  250.0 2.5 collective-permute-start.1
  252.4 3.2 %collective-permute-done.1.other_ref = f32[6,2,256,128]{3,2,1,0:T(8,128)S(1)} collective-permute-done((f32[6,2,256,128]{3,2,1,0:T(8,128)}, f32[6,2,256,128]{3,2,1,0:T(8,128)S(1)}, u32[]{:S(2)}, u32[]{:S(2)}) %collective-permute-start.1) | collective-permute-done | bytes 1572896 | tf_op jit(solution)/shard_map/ppermute | solution.py:295
  255.7 0.0 copy-start.1
  255.7 1.2 copy-done.1
  256.8 5.1 %square.1 = (f32[6,256,128]{2,1,0:T(8,128)}, f32[6,256,128]{2,1,0:T(8,128)}, f32[256,128]{1,0:T(8,128)}) custom-call(f32[6,2,256,128]{3,2,1,0:T(8,128)} %get-tuple-element.12.own_ref, f32[6,2,256,128]{3,2,1,0:T(8,128)} %copy-done.1), custom_call_target="tpu_custom_call" | custom-call | tf_op jit(solution)/shard_map/square/pallas_call | solution.py:296
  261.9 0.5 collective-permute-start.3
  262.4 1.4 collective-permute-start.2
  263.7 0.0 collective-permute-start.6
  263.7 2.6 collective-permute-start.5
  266.4 0.5 collective-permute-start.4
  266.8 3.8 %collective-permute-done.6.edge_after_ref = f32[256,128]{1,0:T(8,128)S(1)} collective-permute-done((f32[256,128]{1,0:T(8,128)}, f32[256,128]{1,0:T(8,128)S(1)}, u32[]{:S(2)}, u32[]{:S(2)}) %collective-permute-start.6) | collective-permute-done | bytes 131104 | tf_op jit(solution)/shard_map/ppermute | solution.py:308
  270.6 0.0 copy-start.5
  270.6 17.7 %collective-permute-done.5.edge_before_ref = f32[256,128]{1,0:T(8,128)S(1)} collective-permute-done((f32[256,128]{1,0:T(8,128)}, f32[256,128]{1,0:T(8,128)S(1)}, u32[]{:S(2)}, u32[]{:S(2)}) %collective-permute-start.5) | collective-permute-done | bytes 131104 | tf_op jit(solution)/shard_map/ppermute | solution.py:307
  288.4 0.0 copy-start.6
  288.4 0.0 collective-permute-done.4.edge_ref
  288.4 0.0 copy-start.7
  288.4 0.0 collective-permute-done.3.after_ref
  288.4 0.0 copy-start.2
  288.4 0.0 collective-permute-done.2.before_ref
  288.4 0.0 copy-start.3
  288.4 0.0 copy-done.5
  288.4 0.6 copy-done.6
  289.0 0.1 copy-done.7
  289.1 0.3 copy-done.2
  289.4 0.2 copy-done.3
  289.6 7.0 %blend.1 = (f32[2,256,128]{2,1,0:T(8,128)}, f32[2,256,128]{2,1,0:T(8,128)}) custom-call(s32[1]{0:T(128)} %bitcast.swap_ref, f32[6,2,256,128]{3,2,1,0:T(8,128)} %get-tuple-element.12.own_ref, f32[6,2,256,128]{3,2,1,0:T(8,128)} %copy-done.1, f32[6,256,128]{2,1,0:T(8,128)} %get-tuple-element.14.first_ref, f32[6,256,128]{2,1,0:T(8,128)} %get-tuple-element.15.second_ref, ...), custom_call_target="tpu_custom_call" | custom-call | tf_op jit(solution)/shard_map/blend/pallas_call | solution.py:312
  296.6 10.7 %collective-permute-start.7 = (f32[2,256,128]{2,1,0:T(8,128)}, f32[2,256,128]{2,1,0:T(8,128)S(1)}, u32[]{:S(2)}, u32[]{:S(2)}) collective-permute-start(f32[2,256,128]{2,1,0:T(8,128)} %get-tuple-element.17), channel_id=1, source_target_pairs={{0,0},{1,2},{2,1},{3,3},{4,4},{5,6},{6,5},{7,7},{8,8},{9,10},{10,9... | collective-permute-start | bytes 786440 | tf_op jit(solution)/shard_map/ppermute | solution.py:321
  307.2 0.1 collective-permute-start.8
  307.3 4.1 %collective-permute-done.7 = f32[2,256,128]{2,1,0:T(8,128)S(1)} collective-permute-done((f32[2,256,128]{2,1,0:T(8,128)}, f32[2,256,128]{2,1,0:T(8,128)S(1)}, u32[]{:S(2)}, u32[]{:S(2)}) %collective-permute-start.7) | collective-permute-done | bytes 262176 | tf_op jit(solution)/shard_map/ppermute | solution.py:321
  311.5 2.2 collective-permute-done.8
  313.7 1.2 copy.18
  (2 shorter events, 0.1 us)
Async XLA Ops:
  6.5 96.1 %reduce-scatter.2.cloned.1.call-start = ((), (), s32[]{:S(2)}) async-start(), calls=%async_computation.2 | async-start | bytes 5242880 | tf_op jit(solution)/shard_map/reduce_scatter | solution.py:252
  104.7 23.8 %collective-permute-start = (f32[32,4096]{1,0:T(8,128)S(1)}, f32[32,4096]{1,0:T(8,128)S(1)}, u32[]{:S(2)}, u32[]{:S(2)}) collective-permute-start(f32[32,4096]{1,0:T(8,128)S(1)} %get-tuple-element.19), channel_id=1, source_target_pairs={{0,254},{2,252},{4,250},{6,248},{8,246},{10,244},{12,242},{14,240}... | collective-permute-start | bytes 1572872 | tf_op jit(solution)/shard_map/ppermute | solution.py:258
  128.5 0.8 copy-start.4
  149.8 92.1 %all-to-all-start = ((f32[128,48,128]{2,1,0:T(8,128)}), f32[128,48,128]{2,1,0:T(8,128)S(1)}, u32[]{:S(2)}, u32[]{:S(2)}) async-start(f32[128,48,128]{2,1,0:T(8,128)} %bitcast.15), calls=%async_computation.1 | async-start | bytes 6291456 | tf_op jit(solution)/shard_map/all_to_all | solution.py:271
  241.9 1.6 copy-start
  250.0 5.7 %collective-permute-start.1 = (f32[6,2,256,128]{3,2,1,0:T(8,128)}, f32[6,2,256,128]{3,2,1,0:T(8,128)S(1)}, u32[]{:S(2)}, u32[]{:S(2)}) collective-permute-start(f32[6,2,256,128]{3,2,1,0:T(8,128)} %get-tuple-element.13), channel_id=1, source_target_pairs={{0,1},{1,0},{2,3},{3,2},{4,5},{5,4},{6,7},{7,6},{8,9},{9,8},{10,11... | collective-permute-start | bytes 4718600 | tf_op jit(solution)/shard_map/ppermute | solution.py:295
  255.7 1.2 copy-start.1
  261.9 26.5 %collective-permute-start.3 = (f32[6,256,128]{2,1,0:T(8,128)}, f32[6,256,128]{2,1,0:T(8,128)S(1)}, u32[]{:S(2)}, u32[]{:S(2)}) collective-permute-start(f32[6,256,128]{2,1,0:T(8,128)} %get-tuple-element.14.first_ref), channel_id=1, source_target_pairs={{0,253},{2,255},{1,0},{3,2},{4,1},{6,3},{5,4},{7,6},{8,5},{10,7},{... | collective-permute-start | bytes 2359304 | tf_op jit(solution)/shard_map/ppermute | solution.py:305
  262.4 26.0 %collective-permute-start.2 = (f32[6,256,128]{2,1,0:T(8,128)}, f32[6,256,128]{2,1,0:T(8,128)S(1)}, u32[]{:S(2)}, u32[]{:S(2)}) collective-permute-start(f32[6,256,128]{2,1,0:T(8,128)} %get-tuple-element.15.second_ref), channel_id=1, source_target_pairs={{0,1},{2,3},{1,4},{3,6},{4,5},{6,7},{5,8},{7,10},{8,9},{10,11},{9,... | collective-permute-start | bytes 2359304 | tf_op jit(solution)/shard_map/ppermute | solution.py:304
  263.7 6.9 %collective-permute-start.6 = (f32[256,128]{1,0:T(8,128)}, f32[256,128]{1,0:T(8,128)S(1)}, u32[]{:S(2)}, u32[]{:S(2)}) collective-permute-start(f32[256,128]{1,0:T(8,128)} %get-tuple-element.16), channel_id=1, source_target_pairs={{0,255},{2,253},{1,2},{3,0},{4,3},{6,1},{5,6},{7,4},{8,7},{10,5},{... | collective-permute-start | bytes 393224 | tf_op jit(solution)/shard_map/ppermute | solution.py:308
  263.7 24.6 %collective-permute-start.5 = (f32[256,128]{1,0:T(8,128)}, f32[256,128]{1,0:T(8,128)S(1)}, u32[]{:S(2)}, u32[]{:S(2)}) collective-permute-start(f32[256,128]{1,0:T(8,128)} %get-tuple-element.16), channel_id=1, source_target_pairs={{0,3},{2,1},{1,6},{3,4},{4,7},{6,5},{5,10},{7,8},{8,11},{10,9},{9,... | collective-permute-start | bytes 393224 | tf_op jit(solution)/shard_map/ppermute | solution.py:307
  266.4 22.0 %collective-permute-start.4 = (f32[256,128]{1,0:T(8,128)}, f32[256,128]{1,0:T(8,128)S(1)}, u32[]{:S(2)}, u32[]{:S(2)}) collective-permute-start(f32[256,128]{1,0:T(8,128)} %get-tuple-element.16), channel_id=1, source_target_pairs={{0,2},{2,0},{1,3},{3,1},{4,6},{6,4},{5,7},{7,5},{8,10},{10,8},{9,1... | collective-permute-start | bytes 393224 | tf_op jit(solution)/shard_map/ppermute | solution.py:306
  270.6 17.8 %copy-start.5 = (f32[256,128]{1,0:T(8,128)}, f32[256,128]{1,0:T(8,128)S(1)}, u32[]{:S(2)}) copy-start(f32[256,128]{1,0:T(8,128)S(1)} %collective-permute-done.6.edge_after_ref) | copy-start | bytes 393220
  288.4 0.6 copy-start.6
  288.4 0.7 copy-start.7
  288.4 1.0 copy-start.2
  288.4 1.2 copy-start.3
  296.6 14.9 %collective-permute-start.7 = (f32[2,256,128]{2,1,0:T(8,128)}, f32[2,256,128]{2,1,0:T(8,128)S(1)}, u32[]{:S(2)}, u32[]{:S(2)}) collective-permute-start(f32[2,256,128]{2,1,0:T(8,128)} %get-tuple-element.17), channel_id=1, source_target_pairs={{0,0},{1,2},{2,1},{3,3},{4,4},{5,6},{6,5},{7,7},{8,8},{9,10},{10,9... | collective-permute-start | bytes 786440 | tf_op jit(solution)/shard_map/ppermute | solution.py:321
  307.2 6.4 %collective-permute-start.8 = (f32[2,256,128]{2,1,0:T(8,128)}, f32[2,256,128]{2,1,0:T(8,128)S(1)}, u32[]{:S(2)}, u32[]{:S(2)}) collective-permute-start(f32[2,256,128]{2,1,0:T(8,128)} %get-tuple-element.18), channel_id=1, source_target_pairs={{0,1},{1,3},{2,0},{3,2},{4,5},{5,7},{6,4},{7,6},{8,9},{9,11},{10,8... | collective-permute-start | bytes 786440 | tf_op jit(solution)/shard_map/ppermute | solution.py:322
Sparse Core Ops, SparseCore 0:
  14.4 88.2 reduce-scatter.1
where the time goes:
time: 322 us
  waiting for transfers between devices  215 us (67%)
  Pallas kernels  38.9 us (12%)
  starting transfers between devices  38.3 us (12%)
  between operations  13.5 us (4%)
  local copies, waits for them, and re-layouts  11.7 us (4%)
    reduce_scatter x1, waiting for transfers between devices, on_device(): lax.psum_scatter(jnp.dot(placing, flat_tiles, preferred_element_type=f32)...  88.4 us
    all_to_all x1, waiting for transfers between devices, on_device(): lax.all_to_all(sent.reshape(SENDERS, PER, LANES), ('particle', 'slab'), s...  75.2 us
    pallas_call x1, Pallas kernels, on_device(): pl.pallas_call(planes_kernel, out_shape=jax.ShapeDtypeStruct((SENDERS * P...  20.5 us
    ppermute x1, waiting for transfers between devices, on_device(): come = lax.ppermute(leaving, ('particle', 'slab'), mirror_pairs())  20.5 us
    ppermute x1, waiting for transfers between devices, on_device(): edge_before = lax.ppermute(edge, everyone, row_pairs(1, 1))  17.7 us
    all_to_all x1, starting transfers between devices, on_device(): lax.all_to_all(sent.reshape(SENDERS, PER, LANES), ('particle', 'slab'), s...  16.9 us
    ppermute x1, starting transfers between devices, on_device(): near = lax.ppermute(near, everyone, home_pairs(0))  10.7 us
    pallas_call x1, Pallas kernels, on_device(): pl.pallas_call(blend_kernel, grid=(BANDS,), out_shape=(block_shape, block...  6.96 us
  transfers between devices with their start and end apart: 11, of which 8 were waited for; matrix products, arithmetic and copies ran while one was open for 0% of the time, Pallas kernels for 0%

commit v1 on v0

--- a/solution.py
+++ b/solution.py
@@ -44,8 +44,7 @@
     along_y = np.block([[cosine, -sine], [sine, cosine]])
     turn = angles(places, places)
     cosine, sine = np.cos(turn), np.sin(turn)
-    along_x_even = np.concatenate([cosine, -sine], axis=0)
-    along_x_odd = np.concatenate([sine, cosine], axis=0)
+    along_x = np.block([[cosine, sine], [-sine, cosine]])
     sender = np.arange(SENDERS)
     group, slab = sender // SLABS, sender % SLABS
     plane = slab * 8 + group * 2 + (slab >= SLABS // 2)
@@ -53,7 +52,7 @@
     even, odd = np.cos(turn), -np.sin(turn)
     odd[:, 0] = np.cos(math.pi * places)
     along_z = np.concatenate([even, odd], axis=1) / BOX
-    return split(along_y) + split(along_x_even) + split(along_x_odd) + split(along_z)
+    return split(along_y) + split(along_x) + split(along_z)
 
 
 def two(value):
@@ -65,17 +64,65 @@
     return jnp.dot(a, b, preferred_element_type=f32)
 
 
-def planes_kernel(
-    cut_ref, kz_ref, keep_ref, come_ref, yh_ref, yl_ref, eh_ref, el_ref, oh_ref, ol_ref, out_ref, sh, sl, dh, dl, radius
+def mark(rows, slots, gains):
+    return jnp.where(rows == slots, gains, 0.0).astype(bf16)
+
+
+def place_kernel(
+    plane_ref, flag_ref, slot_ref, gain_ref, tile_ref, flip_ref, *refs
 ):
+    outs, (kept_mark, sent_mark, sent_mark_first, turn, saved) = refs[:9], refs[9:]
+    step = pl.program_id(0)
+    row = lax.broadcasted_iota(jnp.int32, (BLOCKS, BOX), 0)
+    col = lax.broadcasted_iota(jnp.int32, (BLOCKS, BOX), 1)
+
+    @pl.when(step == 0)
+    def _():
+        slots = jnp.broadcast_to(slot_ref[...], (BLOCKS, BOX))
+        gains = jnp.broadcast_to(gain_ref[...], (BLOCKS, BOX))
+        for i in range(4):
+            rows = pl.ds(i * BLOCKS, BLOCKS)
+            kept_mark[rows, :] = mark(plane_ref[i] * BLOCKS + row, slots, gains)
+            start = plane_ref[4 + i] * BLOCKS
+            sent_mark[rows, :] = mark(start + BLOCKS - 1 - row, slots, gains)
+            sent_mark_first[rows, :] = mark(start + ((BLOCKS - row) & (BLOCKS - 1)), slots, gains)
+        line = lax.broadcasted_iota(jnp.int32, (BOX, BOX), 0)
+        wide = lax.broadcasted_iota(jnp.int32, (BOX, BOX), 1)
+        turn[...] = jnp.where(((line + wide) & (BOX - 1)) == 0, 1.0, 0.0).astype(bf16)
+
+    kept = dot(kept_mark[...], tile_ref[...])
+    flipped = dot(flip_ref[...], turn[...])
+    flipped = jnp.where(step >= TILE_ROWS, -flipped, flipped).astype(bf16)
+    marks = jnp.where((step & (TILE_ROWS - 1)) == 0, sent_mark_first[...], sent_mark[...])
+    sent = dot(marks, flipped)
+
+    @pl.when(step == 0)
+    def _():
+        saved[...] = sent
+
+    corner = (row == 0) & (col == 0) & (step == TILE_ROWS)
+    parts = []
+    for i in range(4):
+        part = kept[i * BLOCKS : (i + 1) * BLOCKS]
+        parts.append(jnp.where(corner & (flag_ref[i] == 1), 0.0, part))
+    for i in range(4):
+        part = sent[i * BLOCKS : (i + 1) * BLOCKS]
+        alone = jnp.where(corner, saved[i * BLOCKS : (i + 1) * BLOCKS, :], 0.0)
+        parts.append(jnp.where(flag_ref[4 + i] == 1, alone, part))
+    parts[2:3] = [parts[2][: BLOCKS // 2], parts[2][BLOCKS // 2 :]]
+    for out_ref, part in zip(outs, parts):
+        out_ref[...] = part
+
+
+def planes_kernel(cut_ref, kz_ref, own_ref, up_ref, down_ref, yh_ref, yl_ref, xh_ref, xl_ref, out_ref, sh, sl, radius):
     alone = kz_ref[0] == 0
-    last = come_ref[0:1, 0:1]
     for i in range(16):
-        kept = keep_ref[:, i * BOX : (i + 1) * BOX]
-        come = jnp.where(alone, 0.0, come_ref[:, i * BOX : (i + 1) * BOX])
+        cols = pl.ds(i * BOX, BOX)
         rows = pl.ds(i * BLOCKS, BLOCKS)
-        sh[rows, :], sl[rows, :] = two(kept + come)
-        dh[rows, :], dl[rows, :] = two(kept - come)
+        whole = own_ref[:, cols] + up_ref[:, cols] + down_ref[:, cols]
+        if i == TILE_ROWS:
+            last = whole[0:1, 0:1]
+        sh[rows, :], sl[rows, :] = two(whole)
     line = lax.broadcasted_iota(jnp.int32, (BOX, BOX), 0)
     col = lax.broadcasted_iota(jnp.int32, (BOX, BOX), 1)
     ky = (line & (BLOCKS - 1)) * TILE_ROWS + (line >> 5)
@@ -89,16 +136,12 @@
         limit = (cut_ref[b] * cut_ref[b]).astype(f32)
         mask = jnp.where(radius[...] <= limit, 1.0, 0.0).astype(bf16)
         mask = jnp.concatenate([mask, mask], axis=0)
-
-        def plane(high_ref, low_ref, th_ref, tl_ref):
-            high, low = high_ref[...] * mask, low_ref[...] * mask
-            mid = dot(yh_ref[...], high) + dot(yl_ref[...], high) + dot(yh_ref[...], low)
-            mid = jnp.concatenate([mid[:BOX], mid[BOX:]], axis=1)
-            high, low = two(mid)
-            return dot(high, th_ref[...]) + dot(low, th_ref[...]) + dot(high, tl_ref[...])
-
-        even = plane(sh, sl, eh_ref, el_ref)
-        odd = plane(dh, dl, oh_ref, ol_ref)
+        high, low = sh[...] * mask, sl[...] * mask
+        mid = dot(yh_ref[...], high) + dot(yl_ref[...], high) + dot(yh_ref[...], low)
+        mid = jnp.concatenate([mid[:BOX], mid[BOX:]], axis=1)
+        high, low = two(mid)
+        both = dot(high, xh_ref[...]) + dot(low, xh_ref[...]) + dot(high, xl_ref[...])
+        even, odd = both[:, :BOX], both[:, BOX:]
         top = jnp.where(cut_ref[b] >= HALF, last, 0.0)
         odd = jnp.where(alone, jnp.broadcast_to(top, odd.shape), odd)
         for c, part in enumerate((even, odd)):
@@ -194,22 +237,23 @@
             out_b_ref[row] = jnp.where(swap, mine, theirs)
 
 
-def place(group, slab, half):
-    return (group * SLABS + slab) * 2 + half
-
-
-def mirror_pairs():
+def chip(depth, spot):
+    return depth // 2 * SLABS + spot * 2 + depth % 2
+
+
+def mirror_pairs(ahead):
     pairs = []
-    for group in range(GROUPS):
-        for slab in range(SLABS):
-            if slab < SLABS // 2:
-                goal = (GROUPS - 1 - group, SLABS - 1 - slab)
-            elif group:
-                goal = (GROUPS - group, SLABS - 1 - slab)
-            else:
-                goal = (0, (SLABS - slab) % (SLABS // 2))
-            pairs.append((group * SLABS + slab, goal[0] * SLABS + goal[1]))
+    for depth in range(8):
+        for spot in range(16):
+            goal = (depth, 15 - spot)
+            if spot >= 8 and (depth + ahead) % 8 // 2 == 0:
+                goal = ((depth + 1) % 8, 15 - spot) if depth % 2 else ((depth - 1) % 8, (16 - spot) % 8)
+            pairs.append((chip(depth, spot), chip(*goal)))
     return pairs
+
+
+def ring_pairs(step):
+    return [(chip(d, s), chip((d + step) % 8, s)) for d in range(8) for s in range(16)]
 
 
 def row_pairs(step, flip):
@@ -236,26 +280,53 @@
     half_pos = lax.axis_index("half")
     side_pos = slab_pos % 2
     everyone = ("particle", "slab", "half")
-    slot_count = BOX // SLABS * BLOCKS
     tile_width = 2 * TILE_ROWS * BOX
     touched = tile_index.shape[2]
     flat_tiles = tiles[0].reshape(-1, tile_width)
-    entry_slot = tile_index[0].reshape(-1)
+    entry_slot = tile_index[0].reshape(1, -1)
     bin_ids = jnp.arange(bin_gain.shape[1], dtype=jnp.int32)
     particle_gain = jnp.sum(
         jnp.where(pose_bin[0][:, None] == bin_ids[None, :], bin_gain[0][None, :].astype(f32), 0.0),
         axis=1,
     )
-    entry_gain = jnp.repeat(particle_gain, touched)
-    slot_ids = jnp.arange(slot_count, dtype=jnp.int32)
-    placing = jnp.where(slot_ids[:, None] == entry_slot[None, :], entry_gain[None, :], 0.0).astype(bf16)
-    owned = lax.psum_scatter(
-        jnp.dot(placing, flat_tiles, preferred_element_type=f32), "particle", scatter_dimension=0, tiled=True
-    )
+    entry_gain = jnp.repeat(particle_gain, touched).reshape(1, -1)
     late = (slab_pos >= SLABS // 2).astype(jnp.int32)
-    kept = lax.dynamic_slice_in_dim(owned, late * BLOCKS, BLOCKS, 0)
-    leaving = lax.dynamic_slice_in_dim(owned, (1 - late) * BLOCKS, BLOCKS, 0)
-    come = lax.ppermute(leaving, ("particle", "slab"), mirror_pairs())
+    depth_pos = group_pos * 2 + side_pos
+    own_line = (depth_pos + jnp.array([0, 2, 4, -2], jnp.int32)) % 8 // 2
+    sent_line = (depth_pos + jnp.array([3, -3, 1, -1], jnp.int32)) % 8 // 2
+    sent_plane = jnp.where(late == 1, (8 - 2 * sent_line) % 8, 7 - 2 * sent_line)
+    plane_list = jnp.concatenate([2 * own_line + late, sent_plane]).astype(jnp.int32)
+    flags = jnp.concatenate([(slab_pos == 0) & (own_line == 0), (slab_pos == 16) & (sent_line == 0)])
+    entries = len(flat_tiles)
+    heights = [BLOCKS, BLOCKS, BLOCKS // 2, BLOCKS // 2] + [BLOCKS] * 5
+    row_in = pl.BlockSpec((1, entries), lambda i: (0, 0))
+    own, ahead, far_a, far_b, behind, *sent = pl.pallas_call(
+        place_kernel,
+        grid=(2 * TILE_ROWS,),
+        out_shape=tuple(jax.ShapeDtypeStruct((h, tile_width), f32) for h in heights),
+        in_specs=[
+            SMEM,
+            SMEM,
+            row_in,
+            row_in,
+            pl.BlockSpec((entries, BOX), lambda i: (0, i)),
+            pl.BlockSpec((entries, BOX), lambda i: (0, i // 8 * 8 + (8 - i % 8) % 8)),
+        ],
+        out_specs=tuple(pl.BlockSpec((h, BOX), lambda i: (0, i)) for h in heights),
+        scratch_shapes=[pltpu.VMEM((4 * BLOCKS, entries), bf16)] * 3
+        + [pltpu.VMEM((BOX, BOX), bf16), pltpu.VMEM((4 * BLOCKS, BOX), f32)],
+        name="place",
+    )(plane_list, flags.astype(jnp.int32), entry_slot, entry_gain, flat_tiles, flat_tiles)
+    here = ("particle", "slab")
+    up, down = ring_pairs(1), ring_pairs(-1)
+    rise, sink = lax.ppermute(far_a, here, up), lax.ppermute(far_b, here, down)
+    come = [lax.ppermute(part, here, mirror_pairs(e)) for part, e in zip(sent, (3, -3, 1, -1))]
+    cut = BLOCKS // 2
+    rise = jnp.concatenate([come[0][:cut] + rise, come[0][cut:]], axis=0)
+    sink = jnp.concatenate([come[1][:cut], come[1][cut:] + sink], axis=0)
+    rise, sink = lax.ppermute(rise, here, up), lax.ppermute(sink, here, down)
+    rise, sink = lax.ppermute(ahead + rise, here, up), lax.ppermute(behind + sink, here, down)
+    rise, sink = lax.ppermute(come[2] + rise, here, up), lax.ppermute(come[3] + sink, here, down)
     plane = (slab_pos * 8 + group_pos * 2 + late).reshape(1)
 
     constants = [jnp.asarray(t) for t in tables()]
@@ -263,11 +334,11 @@
     sent = pl.pallas_call(
         planes_kernel,
         out_shape=jax.ShapeDtypeStruct((SENDERS * PER, LANES), f32),
-        in_specs=[SMEM, SMEM] + [VMEM] * 8,
+        in_specs=[SMEM, SMEM] + [VMEM] * 7,
         out_specs=VMEM,
-        scratch_shapes=[pltpu.VMEM(square, bf16)] * 4 + [pltpu.VMEM((BOX, BOX), f32)],
+        scratch_shapes=[pltpu.VMEM(square, bf16)] * 2 + [pltpu.VMEM((BOX, BOX), f32)],
         name="planes",
-    )(cutoffs, plane, kept, come, *constants[:6])
+    )(cutoffs, plane, own, rise, sink, *constants[:4])
     gathered = lax.all_to_all(
         sent.reshape(SENDERS, PER, LANES), ("particle", "slab"), split_axis=0, concat_axis=0, tiled=True
     ).reshape(SENDERS * PER, LANES)
@@ -291,7 +362,7 @@
         ],
         out_specs=(rows_spec, rows_spec),
         name="depth",
-    )(half_pos.reshape(1), gathered, *constants[6:])
+    )(half_pos.reshape(1), gathered, *constants[4:])
     other = lax.ppermute(leaving, "half", [(0, 1), (1, 0)])
     first, second, edge = pl.pallas_call(
         square_kernel,

time: 322 us -> 281 us (0.87)
  waiting for transfers between devices: 215 us -> 151 us
  starting transfers between devices: 38.3 us -> 65.5 us
  between operations: 13.5 us -> 0.2 us
  Pallas kernels: 38.9 us -> 47.3 us
    reduce_scatter x1 -> x0, waiting for transfers between devices: 88.4 us -> none  [on_device(): lax.psum_scatter(jnp.dot(placing, flat_tiles, preferred_element_type=f32)...]
    ppermute x1 -> x12, starting transfers between devices: 3.37 us -> 30.6 us  [the longest x4 12.6 us: on_device(): lax.ppermute(part, here, mirror_pairs(e))]
    ppermute x1 -> x12, waiting for transfers between devices: 20.5 us -> 47.1 us  [the longest x4 23.7 us: on_device(): lax.ppermute(part, here, mirror_pairs(e))]
    pallas_call x0 -> x1, Pallas kernels: none -> 13.4 us  [on_device(): pl.pallas_call(place_kernel, grid=(2 * TILE_ROWS,), out_shape=tuple((jax....]
    pallas_call x1, Pallas kernels: 20.5 us -> 15.5 us  [on_device(): pl.pallas_call(planes_kernel, out_shape=jax.ShapeDtypeStruct((SENDERS * P...]
  transfers between devices with their start and end apart: 11 -> 21, of which waited for: 8 -> 14; matrix products, arithmetic and copies ran while one was open for 0% -> 0% of each run, Pallas kernels for 0% -> 0%
where the time goes in v1:
time: 281 us; the launch traced here: 280 us
  waiting for transfers between devices  151 us (54%)
  starting transfers between devices  65.5 us (23%)
  Pallas kernels  47.3 us (17%)
  local copies, waits for them, and re-layouts  12.3 us (4%)
  other arithmetic  3.81 us (1%)
    all_to_all x1, waiting for transfers between devices, on_device(): lax.all_to_all(sent.reshape(SENDERS, PER, LANES), ('particle', 'slab'), s...  72.5 us
    ppermute x4, waiting for transfers between devices, on_device(): lax.ppermute(part, here, mirror_pairs(e))  23.7 us
    ppermute x1, waiting for transfers between devices, on_device(): edge_before = lax.ppermute(edge, everyone, row_pairs(1, 1))  18 us
    pallas_call x1, Pallas kernels, on_device(): pl.pallas_call(planes_kernel, out_shape=jax.ShapeDtypeStruct((SENDERS * P...  15.5 us
    all_to_all x1, starting transfers between devices, on_device(): lax.all_to_all(sent.reshape(SENDERS, PER, LANES), ('particle', 'slab'), s...  14.6 us
    pallas_call x1, Pallas kernels, on_device(): pl.pallas_call(place_kernel, grid=(2 * TILE_ROWS,), out_shape=tuple((jax....  13.4 us
    ppermute x4, starting transfers between devices, on_device(): lax.ppermute(part, here, mirror_pairs(e))  12.6 us
    ppermute x1, starting transfers between devices, on_device(): near = lax.ppermute(near, everyone, home_pairs(0))  10.1 us
  transfers between devices with their start and end apart: 21, of which 14 were waited for; matrix products, arithmetic and copies ran while one was open for 0% of the time, Pallas kernels for 0%

profile of v1, /device:TPU:1, one launch (start us, length us, event | category | flops | bytes accessed | tf_op | source)
XLA Modules:
  0.0 280.0 jit_solution(2694576489047714814)
XLA Ops:
  0.0 0.7 bitcast_convert_fusion
  0.7 0.7 compare_and_fusion
  1.4 0.7 select_reduce_fusion
  2.1 0.1 broadcast_in_dim.28
  2.2 0.6 reshape_reshape.3.gain_ref
  2.8 0.8 copy.18
  3.6 0.7 reshape_squeeze.6.slot_ref
  4.3 4.0 %reshape_squeeze.7.tile_ref.flip_ref = bf16[256,4096]{1,0:T(8,128)(2,1)} reshape(bf16[1,64,4,4096]{3,2,1,0:T(4,128)(2,1)} %param.13) | data formatting | bytes 4194304 | tf_op jit(solution)/shard_map/reshape;squeeze | solution.py:285
  8.3 0.7 add_convert_fusion.flag_ref
  8.9 0.6 pad_add_fusion.plane_ref
  9.5 13.4 %place.1 = (f32[32,4096]{1,0:T(8,128)}, f32[32,4096]{1,0:T(8,128)}, f32[16,4096]{1,0:T(8,128)}, f32[16,4096]{1,0:T(8,128)}, f32[32,4096]{1,0:T(8,128)}, /*index=...) custom-call(s32[8]{0:T(128)} %pad_add_fusion.plane_ref, ...), custom_call_target="tpu_custom_call" | custom-call | tf_op jit(solution)/shard_map/place/pallas_call | solution.py:303
  22.9 5.8 %collective-permute-start.1 = (f32[32,4096]{1,0:T(8,128)}, f32[32,4096]{1,0:T(8,128)S(1)}, u32[]{:S(2)}, u32[]{:S(2)}) collective-permute-start(f32[32,4096]{1,0:T(8,128)} %get-tuple-element.24), channel_id=1, source_target_pairs={{0,60},{4,56},{8,52},{12,48},{16,44},{20,40},{24,36},{28,32},{32,2... | collective-permute-start | bytes 1572872 | tf_op jit(solution)/shard_map/ppermute | solution.py:323
  28.8 1.6 collective-permute-start.2
  30.4 3.9 %collective-permute-start.8 = (f32[16,4096]{1,0:T(8,128)}, f32[16,4096]{1,0:T(8,128)S(1)}, u32[]{:S(2)}, u32[]{:S(2)}) collective-permute-start(f32[16,4096]{1,0:T(8,128)} %get-tuple-element.29), channel_id=1, source_target_pairs={{0,194},{4,198},{8,202},{12,206},{16,210},{20,214},{24,218},{28,22... | collective-permute-start | bytes 786440 | tf_op jit(solution)/shard_map/ppermute | solution.py:322
  34.3 0.2 collective-permute-start.7
  34.5 5.8 %collective-permute-done.2 = f32[16,4096]{1,0:T(8,128)S(1)} collective-permute-done((f32[16,4096]{1,0:T(8,128)}, f32[16,4096]{1,0:T(8,128)S(1)}, u32[]{:S(2)}, u32[]{:S(2)}) %collective-permute-start.2) | collective-permute-done | bytes 262176 | tf_op jit(solution)/shard_map/ppermute | solution.py:322
  40.3 0.0 collective-permute-done.1
  40.4 1.9 collective-permute-start.3
  42.3 9.5 %collective-permute-done.7 = f32[32,4096]{1,0:T(8,128)S(1)} collective-permute-done((f32[32,4096]{1,0:T(8,128)}, f32[32,4096]{1,0:T(8,128)S(1)}, u32[]{:S(2)}, u32[]{:S(2)}) %collective-permute-start.7) | collective-permute-done | bytes 524320 | tf_op jit(solution)/shard_map/ppermute | solution.py:323
  51.9 5.5 %collective-permute-start.9 = (f32[32,4096]{1,0:T(8,128)S(1)}, f32[32,4096]{1,0:T(8,128)S(1)}, u32[]{:S(2)}, u32[]{:S(2)}) collective-permute-start(f32[32,4096]{1,0:T(8,128)S(1)} %pad_maximum_fusion.1), channel_id=1, source_target_pairs={{0,194},{4,198},{8,202},{12,206},{16,210},{20,214},{24,218},{28,22... | collective-permute-start | bytes 1572872 | tf_op jit(solution)/shard_map/ppermute | solution.py:327
  57.4 4.6 %collective-permute-start = (f32[32,4096]{1,0:T(8,128)S(1)}, f32[32,4096]{1,0:T(8,128)S(1)}, u32[]{:S(2)}, u32[]{:S(2)}) collective-permute-start(f32[32,4096]{1,0:T(8,128)S(1)} %copy-done.12), channel_id=1, source_target_pairs={{0,60},{4,56},{8,52},{12,48},{16,44},{20,40},{24,36},{28,32},{32,1... | collective-permute-start | bytes 1572872 | tf_op jit(solution)/shard_map/ppermute | solution.py:323
  62.1 1.9 collective-permute-start.6
  64.0 0.0 collective-permute-done.3
  64.0 0.1 add.76
  64.1 0.1 collective-permute-start.4
  64.2 3.2 %collective-permute-done.9 = f32[32,4096]{1,0:T(8,128)S(1)} collective-permute-done((f32[32,4096]{1,0:T(8,128)S(1)}, f32[32,4096]{1,0:T(8,128)S(1)}, u32[]{:S(2)}, u32[]{:S(2)}) %collective-permute-start.9) | collective-permute-done | bytes 524320 | tf_op jit(solution)/shard_map/ppermute | solution.py:327
  67.3 0.1 add.79
  67.4 3.5 %collective-permute-start.10 = (f32[32,4096]{1,0:T(8,128)S(1)}, f32[32,4096]{1,0:T(8,128)S(1)}, u32[]{:S(2)}, u32[]{:S(2)}) collective-permute-start(f32[32,4096]{1,0:T(8,128)S(1)} %add.79), channel_id=1, source_target_pairs={{0,194},{4,198},{8,202},{12,206},{16,210},{20,214},{24,218},{28,22... | collective-permute-start | bytes 1572872 | tf_op jit(solution)/shard_map/ppermute | solution.py:328
  70.9 3.8 %collective-permute-done = f32[32,4096]{1,0:T(8,128)S(1)} collective-permute-done((f32[32,4096]{1,0:T(8,128)S(1)}, f32[32,4096]{1,0:T(8,128)S(1)}, u32[]{:S(2)}, u32[]{:S(2)}) %collective-permute-start) | collective-permute-done | bytes 524320 | tf_op jit(solution)/shard_map/ppermute | solution.py:323
  74.7 2.8 %collective-permute-done.4 = f32[32,4096]{1,0:T(8,128)S(1)} collective-permute-done((f32[32,4096]{1,0:T(8,128)S(1)}, f32[32,4096]{1,0:T(8,128)S(1)}, u32[]{:S(2)}, u32[]{:S(2)}) %collective-permute-start.4) | collective-permute-done | bytes 524320 | tf_op jit(solution)/shard_map/ppermute | solution.py:328
  77.5 0.1 add.77
  77.6 0.1 collective-permute-start.5
  77.7 10.3 %collective-permute-done.6 = f32[32,4096]{1,0:T(8,128)S(1)} collective-permute-done((f32[32,4096]{1,0:T(8,128)S(1)}, f32[32,4096]{1,0:T(8,128)S(1)}, u32[]{:S(2)}, u32[]{:S(2)}) %collective-permute-start.6) | collective-permute-done | bytes 524320 | tf_op jit(solution)/shard_map/ppermute | solution.py:323
  88.0 0.1 add.80
  88.0 1.3 collective-permute-start.11
  89.3 8.2 %collective-permute-done.5.up_ref = f32[32,4096]{1,0:T(8,128)S(1)} collective-permute-done((f32[32,4096]{1,0:T(8,128)S(1)}, f32[32,4096]{1,0:T(8,128)S(1)}, u32[]{:S(2)}, u32[]{:S(2)}) %collective-permute-start.5) | collective-permute-done | bytes 524320 | tf_op jit(solution)/shard_map/ppermute | solution.py:329
  97.6 3.5 %collective-permute-done.11.down_ref = f32[32,4096]{1,0:T(8,128)S(1)} collective-permute-done((f32[32,4096]{1,0:T(8,128)S(1)}, f32[32,4096]{1,0:T(8,128)S(1)}, u32[]{:S(2)}, u32[]{:S(2)}) %collective-permute-start.11) | collective-permute-done | bytes 524320 | tf_op jit(solution)/shard_map/ppermute | solution.py:329
  101.1 0.8 copy-done.7
  101.9 15.5 %planes.1 = f32[6144,128]{1,0:T(8,128)} custom-call(s32[6]{0:T(128)} %cut_ref.1, s32[1]{0:T(128)} %bitcast.2.kz_ref, f32[32,4096]{1,0:T(8,128)} %get-tuple-element.21.own_ref, f32[32,4096]{1,0:T(8,128)} %copy-done.6, f32[32,4096]{1,0:T(8,128)} %copy-done.7, bf16[512,512]{1,0:T(8,128)(2,1)} %constant.97.clone.yh_ref, bf16[512,512]{1,0:T(8,128)(2,1)} %constant.98.clone.yl_ref, ...), custom_call_target="tpu_custom_call" | custom-call | tf_op jit(solution)/shard_map/planes/pallas_call | solution.py:334
  117.4 14.6 %all-to-all-start = ((f32[128,48,128]{2,1,0:T(8,128)}), f32[128,48,128]{2,1,0:T(8,128)S(1)}, u32[]{:S(2)}, u32[]{:S(2)}) async-start(f32[128,48,128]{2,1,0:T(8,128)} %bitcast.14), calls=%async_computation | async-start | bytes 6291456 | tf_op jit(solution)/shard_map/all_to_all | solution.py:342
  132.0 72.5 %all-to-all-done = f32[128,48,128]{2,1,0:T(8,128)S(1)} async-done(((f32[128,48,128]{2,1,0:T(8,128)}), f32[128,48,128]{2,1,0:T(8,128)S(1)}, u32[]{:S(2)}, u32[]{:S(2)}) %all-to-all-start) | async-done | bytes 3145760 | tf_op jit(solution)/shard_map/all_to_all | solution.py:342
  204.4 1.6 copy-done
  206.1 6.4 %depth.1 = (f32[6,2,256,128]{3,2,1,0:T(8,128)}, f32[6,2,256,128]{3,2,1,0:T(8,128)}) custom-call(s32[1]{0:T(128)} %bitcast.1.core_ref, f32[6144,128]{1,0:T(8,128)} %bitcast.13, bf16[256,256]{1,0:T(8,128)(2,1)} %constant.101.clone.zh_ref, bf16[256,256]{1,0:T(8,128)(2,1)} %constant.102.clone.zl_ref), custom_call_target="tpu_custom_call" | custom-call | tf_op jit(solution)/shard_map/depth/pallas_call | solution.py:353
  212.5 5.2 %collective-permute-start.12 = (f32[6,2,256,128]{3,2,1,0:T(8,128)}, f32[6,2,256,128]{3,2,1,0:T(8,128)S(1)}, u32[]{:S(2)}, u32[]{:S(2)}) collective-permute-start(f32[6,2,256,128]{3,2,1,0:T(8,128)} %get-tuple-element.31), channel_id=1, source_target_pairs={{0,1},{1,0},{2,3},{3,2},{4,5},{5,4},{6,7},{7,6},{8,9},{9,8},{10,11... | collective-permute-start | bytes 4718600 | tf_op jit(solution)/shard_map/ppermute | solution.py:366
  217.7 3.2 %collective-permute-done.12.other_ref = f32[6,2,256,128]{3,2,1,0:T(8,128)S(1)} collective-permute-done((f32[6,2,256,128]{3,2,1,0:T(8,128)}, f32[6,2,256,128]{3,2,1,0:T(8,128)S(1)}, u32[]{:S(2)}, u32[]{:S(2)}) %collective-permute-start.12) | collective-permute-done | bytes 1572896 | tf_op jit(solution)/shard_map/ppermute | solution.py:366
  221.0 1.2 copy-done.1
  222.2 5.1 %square.1 = (f32[6,256,128]{2,1,0:T(8,128)}, f32[6,256,128]{2,1,0:T(8,128)}, f32[256,128]{1,0:T(8,128)}) custom-call(f32[6,2,256,128]{3,2,1,0:T(8,128)} %get-tuple-element.30.own_ref, f32[6,2,256,128]{3,2,1,0:T(8,128)} %copy-done.1), custom_call_target="tpu_custom_call" | custom-call | tf_op jit(solution)/shard_map/square/pallas_call | solution.py:367
  227.3 0.5 collective-permute-start.14
  227.7 1.4 collective-permute-start.13
  229.1 0.0 collective-permute-start.17
  229.1 2.6 collective-permute-start.16
  231.7 0.5 collective-permute-start.15
  232.2 3.8 %collective-permute-done.17.edge_after_ref = f32[256,128]{1,0:T(8,128)S(1)} collective-permute-done((f32[256,128]{1,0:T(8,128)}, f32[256,128]{1,0:T(8,128)S(1)}, u32[]{:S(2)}, u32[]{:S(2)}) %collective-permute-start.17) | collective-permute-done | bytes 131104 | tf_op jit(solution)/shard_map/ppermute | solution.py:379
  236.0 18.0 %collective-permute-done.16.edge_before_ref = f32[256,128]{1,0:T(8,128)S(1)} collective-permute-done((f32[256,128]{1,0:T(8,128)}, f32[256,128]{1,0:T(8,128)S(1)}, u32[]{:S(2)}, u32[]{:S(2)}) %collective-permute-start.16) | collective-permute-done | bytes 131104 | tf_op jit(solution)/shard_map/ppermute | solution.py:378
  254.0 0.6 copy-done.9
  254.6 0.1 copy-done.10
  254.7 0.3 copy-done.2
  254.9 0.3 copy-done.3
  255.2 7.0 %blend.1 = (f32[2,256,128]{2,1,0:T(8,128)}, f32[2,256,128]{2,1,0:T(8,128)}) custom-call(s32[1]{0:T(128)} %bitcast.swap_ref, f32[6,2,256,128]{3,2,1,0:T(8,128)} %get-tuple-element.30.own_ref, f32[6,2,256,128]{3,2,1,0:T(8,128)} %copy-done.1, f32[6,256,128]{2,1,0:T(8,128)} %get-tuple-element.32.first_ref, f32[6,256,128]{2,1,0:T(8,128)} %get-tuple-element.33.second_ref, ...), custom_call_target="tpu_custom_call" | custom-call | tf_op jit(solution)/shard_map/blend/pallas_call | solution.py:383
  262.2 10.1 %collective-permute-start.18 = (f32[2,256,128]{2,1,0:T(8,128)}, f32[2,256,128]{2,1,0:T(8,128)S(1)}, u32[]{:S(2)}, u32[]{:S(2)}) collective-permute-start(f32[2,256,128]{2,1,0:T(8,128)} %get-tuple-element.35), channel_id=1, source_target_pairs={{0,0},{1,2},{2,1},{3,3},{4,4},{5,6},{6,5},{7,7},{8,8},{9,10},{10,9... | collective-permute-start | bytes 786440 | tf_op jit(solution)/shard_map/ppermute | solution.py:392
  272.3 0.1 collective-permute-start.19
  272.4 4.1 %collective-permute-done.18 = f32[2,256,128]{2,1,0:T(8,128)S(1)} collective-permute-done((f32[2,256,128]{2,1,0:T(8,128)}, f32[2,256,128]{2,1,0:T(8,128)S(1)}, u32[]{:S(2)}, u32[]{:S(2)}) %collective-permute-start.18) | collective-permute-done | bytes 262176 | tf_op jit(solution)/shard_map/ppermute | solution.py:392
  276.6 2.2 collective-permute-done.19
  278.8 1.2 copy.19
  (32 shorter events, 0.3 us)
Async XLA Ops:
  22.9 17.4 %collective-permute-start.1 = (f32[32,4096]{1,0:T(8,128)}, f32[32,4096]{1,0:T(8,128)S(1)}, u32[]{:S(2)}, u32[]{:S(2)}) collective-permute-start(f32[32,4096]{1,0:T(8,128)} %get-tuple-element.24), channel_id=1, source_target_pairs={{0,60},{4,56},{8,52},{12,48},{16,44},{20,40},{24,36},{28,32},{32,2... | collective-permute-start | bytes 1572872 | tf_op jit(solution)/shard_map/ppermute | solution.py:323
  28.8 11.5 %collective-permute-start.2 = (f32[16,4096]{1,0:T(8,128)}, f32[16,4096]{1,0:T(8,128)S(1)}, u32[]{:S(2)}, u32[]{:S(2)}) collective-permute-start(f32[16,4096]{1,0:T(8,128)} %get-tuple-element.25), channel_id=1, source_target_pairs={{0,2},{4,6},{8,10},{12,14},{16,18},{20,22},{24,26},{28,30},{32,34}... | collective-permute-start | bytes 786440 | tf_op jit(solution)/shard_map/ppermute | solution.py:322
  30.4 11.9 %collective-permute-start.8 = (f32[16,4096]{1,0:T(8,128)}, f32[16,4096]{1,0:T(8,128)S(1)}, u32[]{:S(2)}, u32[]{:S(2)}) collective-permute-start(f32[16,4096]{1,0:T(8,128)} %get-tuple-element.29), channel_id=1, source_target_pairs={{0,194},{4,198},{8,202},{12,206},{16,210},{20,214},{24,218},{28,22... | collective-permute-start | bytes 786440 | tf_op jit(solution)/shard_map/ppermute | solution.py:322
  34.3 23.1 %copy-start.12 = (f32[32,4096]{1,0:T(8,128)S(1)}, f32[32,4096]{1,0:T(8,128)}, u32[]{:S(2)}) copy-start(f32[32,4096]{1,0:T(8,128)} %get-tuple-element.22) | copy-start | bytes 1572868
  34.3 27.7 %copy-start.11 = (f32[32,4096]{1,0:T(8,128)S(1)}, f32[32,4096]{1,0:T(8,128)}, u32[]{:S(2)}) copy-start(f32[32,4096]{1,0:T(8,128)} %get-tuple-element.26) | copy-start | bytes 1572868
  34.3 29.7 %copy-start.5 = (f32[32,4096]{1,0:T(8,128)S(1)}, f32[32,4096]{1,0:T(8,128)}, u32[]{:S(2)}) copy-start(f32[32,4096]{1,0:T(8,128)} %get-tuple-element.23) | copy-start | bytes 1572868
  34.3 17.5 %collective-permute-start.7 = (f32[32,4096]{1,0:T(8,128)}, f32[32,4096]{1,0:T(8,128)S(1)}, u32[]{:S(2)}, u32[]{:S(2)}) collective-permute-start(f32[32,4096]{1,0:T(8,128)} %get-tuple-element.28), channel_id=1, source_target_pairs={{0,60},{4,56},{8,52},{12,48},{16,44},{20,40},{24,36},{28,32},{32,2... | collective-permute-start | bytes 1572872 | tf_op jit(solution)/shard_map/ppermute | solution.py:323
  40.4 27.0 %copy-start.4 = (f32[32,4096]{1,0:T(8,128)S(1)}, f32[32,4096]{1,0:T(8,128)}, u32[]{:S(2)}) copy-start(f32[32,4096]{1,0:T(8,128)} %get-tuple-element.27) | copy-start | bytes 1572868
  40.4 23.7 %collective-permute-start.3 = (f32[32,4096]{1,0:T(8,128)S(1)}, f32[32,4096]{1,0:T(8,128)S(1)}, u32[]{:S(2)}, u32[]{:S(2)}) collective-permute-start(f32[32,4096]{1,0:T(8,128)S(1)} %pad_maximum_fusion), channel_id=1, source_target_pairs={{0,2},{4,6},{8,10},{12,14},{16,18},{20,22},{24,26},{28,30},{32,34}... | collective-permute-start | bytes 1572872 | tf_op jit(solution)/shard_map/ppermute | solution.py:327
  51.9 15.4 %collective-permute-start.9 = (f32[32,4096]{1,0:T(8,128)S(1)}, f32[32,4096]{1,0:T(8,128)S(1)}, u32[]{:S(2)}, u32[]{:S(2)}) collective-permute-start(f32[32,4096]{1,0:T(8,128)S(1)} %pad_maximum_fusion.1), channel_id=1, source_target_pairs={{0,194},{4,198},{8,202},{12,206},{16,210},{20,214},{24,218},{28,22... | collective-permute-start | bytes 1572872 | tf_op jit(solution)/shard_map/ppermute | solution.py:327
  57.4 17.3 %collective-permute-start = (f32[32,4096]{1,0:T(8,128)S(1)}, f32[32,4096]{1,0:T(8,128)S(1)}, u32[]{:S(2)}, u32[]{:S(2)}) collective-permute-start(f32[32,4096]{1,0:T(8,128)S(1)} %copy-done.12), channel_id=1, source_target_pairs={{0,60},{4,56},{8,52},{12,48},{16,44},{20,40},{24,36},{28,32},{32,1... | collective-permute-start | bytes 1572872 | tf_op jit(solution)/shard_map/ppermute | solution.py:323
  62.1 25.9 %collective-permute-start.6 = (f32[32,4096]{1,0:T(8,128)S(1)}, f32[32,4096]{1,0:T(8,128)S(1)}, u32[]{:S(2)}, u32[]{:S(2)}) collective-permute-start(f32[32,4096]{1,0:T(8,128)S(1)} %copy-done.11), channel_id=1, source_target_pairs={{0,60},{4,56},{8,52},{12,48},{16,44},{20,40},{24,36},{28,32},{32,2... | collective-permute-start | bytes 1572872 | tf_op jit(solution)/shard_map/ppermute | solution.py:323
  64.1 13.4 %collective-permute-start.4 = (f32[32,4096]{1,0:T(8,128)S(1)}, f32[32,4096]{1,0:T(8,128)S(1)}, u32[]{:S(2)}, u32[]{:S(2)}) collective-permute-start(f32[32,4096]{1,0:T(8,128)S(1)} %add.76), channel_id=1, source_target_pairs={{0,2},{4,6},{8,10},{12,14},{16,18},{20,22},{24,26},{28,30},{32,34}... | collective-permute-start | bytes 1572872 | tf_op jit(solution)/shard_map/ppermute | solution.py:328
  67.4 20.6 %collective-permute-start.10 = (f32[32,4096]{1,0:T(8,128)S(1)}, f32[32,4096]{1,0:T(8,128)S(1)}, u32[]{:S(2)}, u32[]{:S(2)}) collective-permute-start(f32[32,4096]{1,0:T(8,128)S(1)} %add.79), channel_id=1, source_target_pairs={{0,194},{4,198},{8,202},{12,206},{16,210},{20,214},{24,218},{28,22... | collective-permute-start | bytes 1572872 | tf_op jit(solution)/shard_map/ppermute | solution.py:328
  77.6 20.0 %collective-permute-start.5 = (f32[32,4096]{1,0:T(8,128)S(1)}, f32[32,4096]{1,0:T(8,128)S(1)}, u32[]{:S(2)}, u32[]{:S(2)}) collective-permute-start(f32[32,4096]{1,0:T(8,128)S(1)} %add.77), channel_id=1, source_target_pairs={{0,2},{4,6},{8,10},{12,14},{16,18},{20,22},{24,26},{28,30},{32,34}... | collective-permute-start | bytes 1572872 | tf_op jit(solution)/shard_map/ppermute | solution.py:329
  88.0 13.1 %collective-permute-start.11 = (f32[32,4096]{1,0:T(8,128)S(1)}, f32[32,4096]{1,0:T(8,128)S(1)}, u32[]{:S(2)}, u32[]{:S(2)}) collective-permute-start(f32[32,4096]{1,0:T(8,128)S(1)} %add.80), channel_id=1, source_target_pairs={{0,194},{4,198},{8,202},{12,206},{16,210},{20,214},{24,218},{28,22... | collective-permute-start | bytes 1572872 | tf_op jit(solution)/shard_map/ppermute | solution.py:329
  97.6 3.5 %copy-start.6 = (f32[32,4096]{1,0:T(8,128)}, f32[32,4096]{1,0:T(8,128)S(1)}, u32[]{:S(2)}) copy-start(f32[32,4096]{1,0:T(8,128)S(1)} %collective-permute-done.5.up_ref) | copy-start | bytes 1572868
  101.1 0.8 copy-start.7
  117.4 87.1 %all-to-all-start = ((f32[128,48,128]{2,1,0:T(8,128)}), f32[128,48,128]{2,1,0:T(8,128)S(1)}, u32[]{:S(2)}, u32[]{:S(2)}) async-start(f32[128,48,128]{2,1,0:T(8,128)} %bitcast.14), calls=%async_computation | async-start | bytes 6291456 | tf_op jit(solution)/shard_map/all_to_all | solution.py:342
  204.4 1.6 copy-start
  212.5 8.5 %collective-permute-start.12 = (f32[6,2,256,128]{3,2,1,0:T(8,128)}, f32[6,2,256,128]{3,2,1,0:T(8,128)S(1)}, u32[]{:S(2)}, u32[]{:S(2)}) collective-permute-start(f32[6,2,256,128]{3,2,1,0:T(8,128)} %get-tuple-element.31), channel_id=1, source_target_pairs={{0,1},{1,0},{2,3},{3,2},{4,5},{5,4},{6,7},{7,6},{8,9},{9,8},{10,11... | collective-permute-start | bytes 4718600 | tf_op jit(solution)/shard_map/ppermute | solution.py:366
  221.0 1.2 copy-start.1
  227.3 26.7 %collective-permute-start.14 = (f32[6,256,128]{2,1,0:T(8,128)}, f32[6,256,128]{2,1,0:T(8,128)S(1)}, u32[]{:S(2)}, u32[]{:S(2)}) collective-permute-start(f32[6,256,128]{2,1,0:T(8,128)} %get-tuple-element.32.first_ref), channel_id=1, source_target_pairs={{0,253},{2,255},{1,0},{3,2},{4,1},{6,3},{5,4},{7,6},{8,5},{10,7},{... | collective-permute-start | bytes 2359304 | tf_op jit(solution)/shard_map/ppermute | solution.py:376
  227.7 26.3 %collective-permute-start.13 = (f32[6,256,128]{2,1,0:T(8,128)}, f32[6,256,128]{2,1,0:T(8,128)S(1)}, u32[]{:S(2)}, u32[]{:S(2)}) collective-permute-start(f32[6,256,128]{2,1,0:T(8,128)} %get-tuple-element.33.second_ref), channel_id=1, source_target_pairs={{0,1},{2,3},{1,4},{3,6},{4,5},{6,7},{5,8},{7,10},{8,9},{10,11},{9,... | collective-permute-start | bytes 2359304 | tf_op jit(solution)/shard_map/ppermute | solution.py:375
  229.1 6.9 %collective-permute-start.17 = (f32[256,128]{1,0:T(8,128)}, f32[256,128]{1,0:T(8,128)S(1)}, u32[]{:S(2)}, u32[]{:S(2)}) collective-permute-start(f32[256,128]{1,0:T(8,128)} %get-tuple-element.34), channel_id=1, source_target_pairs={{0,255},{2,253},{1,2},{3,0},{4,3},{6,1},{5,6},{7,4},{8,7},{10,5},{... | collective-permute-start | bytes 393224 | tf_op jit(solution)/shard_map/ppermute | solution.py:379
  229.1 24.9 %collective-permute-start.16 = (f32[256,128]{1,0:T(8,128)}, f32[256,128]{1,0:T(8,128)S(1)}, u32[]{:S(2)}, u32[]{:S(2)}) collective-permute-start(f32[256,128]{1,0:T(8,128)} %get-tuple-element.34), channel_id=1, source_target_pairs={{0,3},{2,1},{1,6},{3,4},{4,7},{6,5},{5,10},{7,8},{8,11},{10,9},{9,... | collective-permute-start | bytes 393224 | tf_op jit(solution)/shard_map/ppermute | solution.py:378
  231.7 22.2 %collective-permute-start.15 = (f32[256,128]{1,0:T(8,128)}, f32[256,128]{1,0:T(8,128)S(1)}, u32[]{:S(2)}, u32[]{:S(2)}) collective-permute-start(f32[256,128]{1,0:T(8,128)} %get-tuple-element.34), channel_id=1, source_target_pairs={{0,2},{2,0},{1,3},{3,1},{4,6},{6,4},{5,7},{7,5},{8,10},{10,8},{9,1... | collective-permute-start | bytes 393224 | tf_op jit(solution)/shard_map/ppermute | solution.py:377
  236.0 18.0 %copy-start.8 = (f32[256,128]{1,0:T(8,128)}, f32[256,128]{1,0:T(8,128)S(1)}, u32[]{:S(2)}) copy-start(f32[256,128]{1,0:T(8,128)S(1)} %collective-permute-done.17.edge_after_ref) | copy-start | bytes 393220
  254.0 0.7 copy-start.9
  254.0 0.7 copy-start.10
  254.0 1.0 copy-start.2
  254.0 1.3 copy-start.3
  262.2 14.4 %collective-permute-start.18 = (f32[2,256,128]{2,1,0:T(8,128)}, f32[2,256,128]{2,1,0:T(8,128)S(1)}, u32[]{:S(2)}, u32[]{:S(2)}) collective-permute-start(f32[2,256,128]{2,1,0:T(8,128)} %get-tuple-element.35), channel_id=1, source_target_pairs={{0,0},{1,2},{2,1},{3,3},{4,4},{5,6},{6,5},{7,7},{8,8},{9,10},{10,9... | collective-permute-start | bytes 786440 | tf_op jit(solution)/shard_map/ppermute | solution.py:392
  272.3 6.4 %collective-permute-start.19 = (f32[2,256,128]{2,1,0:T(8,128)}, f32[2,256,128]{2,1,0:T(8,128)S(1)}, u32[]{:S(2)}, u32[]{:S(2)}) collective-permute-start(f32[2,256,128]{2,1,0:T(8,128)} %get-tuple-element.36), channel_id=1, source_target_pairs={{0,1},{1,3},{2,0},{3,2},{4,5},{5,7},{6,4},{7,6},{8,9},{9,11},{10,8... | collective-permute-start | bytes 786440 | tf_op jit(solution)/shard_map/ppermute | solution.py:393

commit v2 on v1

v2 whole, which is shorter than its diff:
```python
import math

import jax
import jax.numpy as jnp
import numpy as np
from jax import lax
from jax.experimental import pallas as pl
from jax.experimental.pallas import tpu as pltpu
from jax.sharding import PartitionSpec as P

BOX = 256
HALF = BOX // 2
TILE_ROWS = 8
BLOCKS = BOX // TILE_ROWS
BANDS = 6
PACE = 2
GROUPS = 4
SLABS = 32
SENDERS = GROUPS * SLABS
PER = BANDS * 8
LANES = 128
error_floor = 1.0
bf16 = jnp.bfloat16
f32 = jnp.float32
VMEM = pl.BlockSpec(memory_space=pltpu.VMEM)
SMEM = pl.BlockSpec(memory_space=pltpu.SMEM)


def split(table):
    high = table.astype(np.float32).astype(jnp.bfloat16)
    low = (table - high.astype(np.float64)).astype(np.float32).astype(jnp.bfloat16)
    return high, low


def angles(left, right):
    return (np.outer(left, right) % BOX) * (2.0 * math.pi / BOX)


def tables():
    places = np.arange(BOX)
    block = places % 64
    y_order = (block % 32 * 2 + block // 32) * 4 + places // 64
    ky_order = (places % BLOCKS) * TILE_ROWS + places // BLOCKS
    turn = angles(y_order, ky_order)
    cosine, sine = np.cos(turn), np.sin(turn)
    along_y = np.stack(split(cosine) + split(sine))
    turn = angles(places, places)
    along_x = np.stack(split(np.cos(turn)) + split(np.sin(turn)))
    sender = np.arange(SENDERS)
    group, slab = sender // SLABS, sender % SLABS
    plane = slab * 8 + group * 2 + (slab >= SLABS // 2)
    turn = angles(places, plane)
    even, odd = np.cos(turn), -np.sin(turn)
    odd[:, 0] = np.cos(math.pi * places)
    along_z = np.stack(split(np.concatenate([even, odd], axis=1) / BOX))
    return along_y, along_x, along_z


def two(value):
    high = value.astype(bf16)
    return high, (value - high.astype(f32)).astype(bf16)


def dot(a, b):
    return jnp.dot(a, b, preferred_element_type=f32)


def mark(rows, slots, gains):
    return jnp.where(rows == slots, gains, 0.0).astype(bf16)


def place_kernel(slab_ref, group_ref, index_ref, bin_ref, gain_ref, tile_ref, *refs):
    outs, (kept_mark, sent_mark, sent_mark_first, turn, saved) = refs[:9], refs[9:]
    step = pl.program_id(0)
    slab, group = slab_ref[0], group_ref[0]
    depth, late = group * 2 + slab % 2, slab // (SLABS // 2)
    row = lax.broadcasted_iota(jnp.int32, (BLOCKS, BOX), 0)
    col = lax.broadcasted_iota(jnp.int32, (BLOCKS, BOX), 1)
    own_line = [((depth + d) & 7) // 2 for d in (0, 2, 4, 6)]
    sent_line = [((depth + d) & 7) // 2 for d in (3, 5, 1, 7)]

    @pl.when(step == 0)
    def _():
        touched, particles = index_ref.shape
        entries = touched * particles
        bins = gain_ref.shape[1]
        line = lax.broadcasted_iota(jnp.int32, (particles, entries), 0)
        wide = lax.broadcasted_iota(jnp.int32, (particles, entries), 1)
        spread = jnp.where(wide // touched == line, 1.0, 0.0).astype(bf16)
        slots = dot(index_ref[...].astype(f32).astype(bf16), spread)
        line = lax.broadcasted_iota(jnp.int32, slots.shape, 0)
        wide = lax.broadcasted_iota(jnp.int32, slots.shape, 1)
        slots = jnp.sum(jnp.where(wide % touched == line, slots, 0.0), axis=0, keepdims=True)
        slots = jnp.broadcast_to(slots, (BLOCKS, entries)).astype(jnp.int32)
        line = lax.broadcasted_iota(jnp.int32, (bins, bins), 0)
        wide = lax.broadcasted_iota(jnp.int32, (bins, bins), 1)
        table = jnp.broadcast_to(gain_ref[...].astype(f32), (bins, bins))
        table = jnp.sum(jnp.where(line == wide, table, 0.0), axis=1, keepdims=True)
        line = lax.broadcasted_iota(jnp.int32, (bins, particles), 0)
        gains = jnp.where(line == bin_ref[...], table, 0.0).astype(bf16)
        gains = jnp.sum(dot(gains, spread), axis=0, keepdims=True)
        gains = jnp.broadcast_to(gains, (BLOCKS, entries))
        for i in range(4):
            rows = pl.ds(i * BLOCKS, BLOCKS)
            kept_mark[rows, :] = mark((2 * own_line[i] + late) * BLOCKS + row, slots, gains)
            start = jnp.where(late == 1, (8 - 2 * sent_line[i]) & 7, 7 - 2 * sent_line[i]) * BLOCKS
            sent_mark[rows, :] = mark(start + BLOCKS - 1 - row, slots, gains)
            sent_mark_first[rows, :] = mark(start + ((BLOCKS - row) & (BLOCKS - 1)), slots, gains)
        line = lax.broadcasted_iota(jnp.int32, (BOX, BOX), 0)
        wide = lax.broadcasted_iota(jnp.int32, (BOX, BOX), 1)
        turn[...] = jnp.where(((line + wide) & (BOX - 1)) == 0, 1.0, 0.0).astype(bf16)

    sign = jnp.where(step == 1, -1.0, 1.0)
    tile = tile_ref[...].reshape(-1, TILE_ROWS * BOX)
    for r in range(TILE_ROWS):
        cols = pl.ds(r * BOX, BOX)
        back = (TILE_ROWS - r) % TILE_ROWS * BOX
        kept = dot(kept_mark[...], tile[:, r * BOX : (r + 1) * BOX])
        flipped = (dot(tile[:, back : back + BOX], turn[...]) * sign).astype(bf16)
        sent = dot((sent_mark if r else sent_mark_first)[...], flipped)
        if r == 0:
            first = (row == 0) & (col == 0)
            last_sent = saved[...]
            saved[...] = sent
        parts = []
        for i in range(4):
            part = kept[i * BLOCKS : (i + 1) * BLOCKS]
            if r == 0:
                part = jnp.where(first & (step == 1) & (slab == 0) & (own_line[i] == 0), 0.0, part)
            parts.append(part)
        for i in range(4):
            part = sent[i * BLOCKS : (i + 1) * BLOCKS]
            alone = 0.0
            if r == 0:
                alone = jnp.where(first & (step == 1), last_sent[i * BLOCKS : (i + 1) * BLOCKS], 0.0)
            parts.append(jnp.where((slab == SLABS // 2) & (sent_line[i] == 0), alone, part))
        parts[2:3] = [parts[2][: BLOCKS // 2], parts[2][BLOCKS // 2 :]]
        for out_ref, part in zip(outs, parts):
            out_ref[:, cols] = part


def fill(four_ref, out_ref, down):
    for third, low in enumerate((0, 0, 1) if down else (0, 1, 0)):
        cosine, sine = four_ref[low], four_ref[2 + low]
        start = third * 2 * BOX
        for i in range(2):
            for j in range(2):
                block = cosine if i == j else (sine if (i == 1) != down else -sine)
                if down:
                    out_ref[start + i * BOX : start + (i + 1) * BOX, j * BOX : (j + 1) * BOX] = block
                else:
                    out_ref[i * BOX : (i + 1) * BOX, start + j * BOX : start + (j + 1) * BOX] = block


def planes_kernel(cut_ref, kz_ref, own_ref, up_ref, down_ref, cy_ref, cx_ref, out_ref, sh, sl, radius, y_ref, x_ref):
    fill(cy_ref, y_ref, False)
    fill(cx_ref, x_ref, True)
    alone = kz_ref[0] == 0
    for i in range(16):
        cols = pl.ds(i * BOX, BOX)
        rows = pl.ds(i * BLOCKS, BLOCKS)
        whole = own_ref[:, cols] + up_ref[:, cols] + down_ref[:, cols]
        if i == TILE_ROWS:
            last = whole[0:1, 0:1]
        sh[rows, :], sl[rows, :] = two(whole)
    line = lax.broadcasted_iota(jnp.int32, (BOX, BOX), 0)
    col = lax.broadcasted_iota(jnp.int32, (BOX, BOX), 1)
    ky = (line & (BLOCKS - 1)) * TILE_ROWS + (line >> 5)
    ky = ((ky + HALF) & (BOX - 1)) - HALF
    kx = ((col + HALF) & (BOX - 1)) - HALF
    kz = ((kz_ref[0] + HALF) & (BOX - 1)) - HALF
    radius[...] = (ky * ky + kx * kx + kz * kz).astype(f32)

    @pl.loop(0, BANDS)
    def _(b):
        limit = (cut_ref[b] * cut_ref[b]).astype(f32)
        mask = jnp.where(radius[...] <= limit, 1.0, 0.0).astype(bf16)
        mask = jnp.concatenate([mask, mask], axis=0)
        high, low = sh[...] * mask, sl[...] * mask
        mid = dot(y_ref[...], jnp.concatenate([high, high, low], axis=0))
        high, low = two(jnp.concatenate([mid[:BOX], mid[BOX:]], axis=1))
        both = dot(jnp.concatenate([high, low, high], axis=1), x_ref[...])
        even, odd = both[:, :BOX], both[:, BOX:]
        top = jnp.where(cut_ref[b] >= HALF, last, 0.0)
        odd = jnp.where(alone, jnp.broadcast_to(top, odd.shape), odd)
        for c, part in enumerate((even, odd)):
            for j in range(4):
                for side in range(2):
                    for odd_block in range(2):
                        start = j * 64 + odd_block * 32
                        block = part[start : start + 32, side * LANES : (side + 1) * LANES]
                        goal = 2 * (odd_block ^ side) + side
                        out_ref[pl.ds(goal * PER + b * 8 + c * 4 + j, 32, stride=4 * PER), :] = block


def depth_kernel(core_ref, come_ref, z_ref, own_ref, other_ref, own_edge_ref, other_edge_ref, own_edge, other_edge):
    step = pl.program_id(0)
    lane = lax.broadcasted_iota(jnp.int32, (BOX, LANES), 1)
    turn = jnp.concatenate([z_ref[0], z_ref[1], z_ref[0]], axis=1)
    for out_ref, edge, core in (
        (own_ref, own_edge, core_ref[0]),
        (other_ref, other_edge, 1 - core_ref[0]),
    ):
        found = jnp.where(step == 0, 0.0, edge[...])
        for i in range(PACE):
            start = (step * PACE + i) * 8 + core * 2
            sides = [
                jnp.concatenate(
                    [come_ref[pl.ds(start + c * 4 + j, SENDERS, stride=PER), :] for j in range(2)], axis=1
                )
                for c in range(2)
            ]
            high, low = two(jnp.concatenate(sides, axis=0))
            full = dot(turn, jnp.concatenate([high, high, low], axis=0))
            for row in range(2):
                part = full[:, row * LANES : (row + 1) * LANES]
                out_ref[i, row] = part
                spot = (step * PACE + i) * 4 + row * 2
                found = jnp.where((lane >> 1) == (spot >> 1), pltpu.roll(part, spot + 1, 1), found)
        edge[...] = found

    @pl.when(step == BANDS // PACE - 1)
    def _():
        narrow = lax.broadcasted_iota(jnp.int32, (64, LANES), 1)
        for out_ref, edge in ((own_edge_ref, own_edge), (other_edge_ref, other_edge)):
            packed = edge[0:64, :]
            for q in range(1, 4):
                packed = jnp.where((narrow >> 5) == q, pltpu.roll(edge[q * 64 : (q + 1) * 64, :], q * 32, 1), packed)
            out_ref[...] = packed


def square_kernel(own_ref, other_ref, own_edge_ref, other_edge_ref, first_ref, second_ref, border):
    step = pl.program_id(0)
    lane = lax.broadcasted_iota(jnp.int32, (BOX, LANES), 1)

    @pl.when(step == 0)
    def _():
        gap = own_edge_ref[...] - other_edge_ref[...]
        gap = gap * gap
        for q in range(4):
            border[q * 64 : (q + 1) * 64, :] = pltpu.roll(gap, (LANES - q * 32) % LANES, 1)

    for i in range(PACE):
        for row, ref in enumerate((first_ref, second_ref)):
            gap = own_ref[i, row] - other_ref[i, row]
            square = gap * gap
            spot = (step * PACE + i) * 4 + row * 2
            beyond = pltpu.roll(border[...], LANES - 1 - spot, 1)
            left = pltpu.roll(jnp.where(lane == LANES - 1, beyond, square), 1, 1)
            right = pltpu.roll(jnp.where(lane == 0, beyond, square), LANES - 1, 1)
            ref[i] = square + left + right


def blend_kernel(
    swap_ref, own_ref, other_ref, first_ref, second_ref, before_ref, after_ref, out_a_ref, out_b_ref, sums
):
    step = pl.program_id(0)

    @pl.when(step == 0)
    def _():
        sums[...] = jnp.zeros_like(sums)

    for row in range(2):
        mine, theirs, total = sums[row, 0], sums[row, 1], sums[row, 2]
        for i in range(PACE):
            wide = first_ref[i] + second_ref[i] + (before_ref if row == 0 else after_ref)[i]
            full = wide + pltpu.roll(wide, 1, 0) + pltpu.roll(wide, BOX - 1, 0)
            weight = 1.0 / (full / 27.0 + error_floor)
            mine = mine + weight * own_ref[i, row]
            theirs = theirs + weight * other_ref[i, row]
            total = total + weight
        sums[row, 0], sums[row, 1], sums[row, 2] = mine, theirs, total

    @pl.when(step == BANDS // PACE - 1)
    def _():
        swap = swap_ref[0] == 1
        for row in range(2):
            mine = sums[row, 0] / sums[row, 2]
            theirs = sums[row, 1] / sums[row, 2]
            out_a_ref[row] = jnp.where(swap, theirs, mine)
            out_b_ref[row] = jnp.where(swap, mine, theirs)


def chip(depth, spot):
    return depth // 2 * SLABS + spot * 2 + depth % 2


def mirror_pairs(ahead):
    pairs = []
    for depth in range(8):
        for spot in range(16):
            goal = (depth, 15 - spot)
            if spot >= 8 and (depth + ahead) % 8 // 2 == 0:
                goal = ((depth + 1) % 8, 15 - spot) if depth % 2 else ((depth - 1) % 8, (16 - spot) % 8)
            pairs.append((chip(depth, spot), chip(*goal)))
    return pairs


def ring_pairs(step):
    return [(chip(d, s), chip((d + step) % 8, s)) for d in range(8) for s in range(16)]


def holder(block, side, core):
    return (2 * (block ^ side) + side) * 2 + core


def row_pairs(step):
    pairs = []
    for n in range(SENDERS):
        goal = (n + step) % SENDERS
        pairs += [(holder(n // 2, side, n % 2), holder(goal // 2, side, goal % 2)) for side in range(2)]
    return pairs


def edge_pairs(flip):
    return [
        (holder(block, side, core), holder(block, 1 - side, core ^ flip))
        for block in range(64)
        for side in range(2)
        for core in range(2)
    ]


def home_pairs(flip):
    return [
        (holder(block, side, core), (2 * block + core) * 2 + (side ^ flip))
        for block in range(64)
        for side in range(2)
        for core in range(2)
    ]


def on_device(tiles, tile_index, pose_bin, bin_gain, cutoffs):
    slab_pos = lax.axis_index("slab")
    group_pos = lax.axis_index("particle")
    half_pos = lax.axis_index("half")
    side_pos = slab_pos % 2
    everyone = ("particle", "slab", "half")
    tile_width = 2 * TILE_ROWS * BOX
    _, particles, touched, _ = tiles.shape
    entries = particles * touched
    late = (slab_pos >= SLABS // 2).astype(jnp.int32)
    heights = [BLOCKS, BLOCKS, BLOCKS // 2, BLOCKS // 2] + [BLOCKS] * 5
    own, ahead, far_a, far_b, behind, *sent = pl.pallas_call(
        place_kernel,
        grid=(2,),
        out_shape=tuple(jax.ShapeDtypeStruct((h, tile_width), f32) for h in heights),
        in_specs=[
            SMEM,
            SMEM,
            pl.BlockSpec((touched, particles), lambda i: (0, 0)),
            pl.BlockSpec((1, particles), lambda i: (0, 0)),
            pl.BlockSpec((1, bin_gain.shape[1]), lambda i: (0, 0)),
            pl.BlockSpec((particles, touched, tile_width // 2), lambda i: (0, 0, i)),
        ],
        out_specs=tuple(pl.BlockSpec((h, tile_width // 2), lambda i: (0, i)) for h in heights),
        scratch_shapes=[pltpu.VMEM((4 * BLOCKS, entries), bf16)] * 3
        + [pltpu.VMEM((BOX, BOX), bf16), pltpu.VMEM((4 * BLOCKS, BOX), f32)],
        name="place",
    )(slab_pos.reshape(1), group_pos.reshape(1), tile_index[0].T, pose_bin, bin_gain, tiles[0])
    here = ("particle", "slab")
    up, down = ring_pairs(1), ring_pairs(-1)
    rise, sink = lax.ppermute(far_a, here, up), lax.ppermute(far_b, here, down)
    come = [lax.ppermute(part, here, mirror_pairs(e)) for part, e in zip(sent, (3, -3, 1, -1))]
    cut = BLOCKS // 2
    rise = jnp.concatenate([come[0][:cut] + rise, come[0][cut:]], axis=0)
    sink = jnp.concatenate([come[1][:cut], come[1][cut:] + sink], axis=0)
    rise, sink = lax.ppermute(rise, here, up), lax.ppermute(sink, here, down)
    rise, sink = lax.ppermute(ahead + rise, here, up), lax.ppermute(behind + sink, here, down)
    rise, sink = lax.ppermute(come[2] + rise, here, up), lax.ppermute(come[3] + sink, here, down)
    plane = (slab_pos * 8 + group_pos * 2 + late).reshape(1)

    constants = [jnp.asarray(t) for t in tables()]
    square = (2 * BOX, BOX)
    sent = pl.pallas_call(
        planes_kernel,
        out_shape=jax.ShapeDtypeStruct((SENDERS * PER, LANES), f32),
        in_specs=[SMEM, SMEM] + [VMEM] * 5,
        out_specs=VMEM,
        scratch_shapes=[
            pltpu.VMEM(square, bf16),
            pltpu.VMEM(square, bf16),
            pltpu.VMEM((BOX, BOX), f32),
            pltpu.VMEM((2 * BOX, 6 * BOX), bf16),
            pltpu.VMEM((6 * BOX, 2 * BOX), bf16),
        ],
        name="planes",
    )(cutoffs, plane, own, rise, sink, *constants[:2])
    gathered = lax.all_to_all(
        sent.reshape(SENDERS, PER, LANES), ("particle", "slab"), split_axis=0, concat_axis=0, tiled=True
    ).reshape(SENDERS * PER, LANES)

    steps = BANDS // PACE
    rows_spec = pl.BlockSpec((PACE, 2, BOX, LANES), lambda b: (b, 0, 0, 0))
    rows_shape = jax.ShapeDtypeStruct((BANDS, 2, BOX, LANES), f32)
    row_spec = pl.BlockSpec((PACE, BOX, LANES), lambda b: (b, 0, 0))
    row_shape = jax.ShapeDtypeStruct((BANDS, BOX, LANES), f32)
    edge_spec = pl.BlockSpec((64, LANES), lambda b: (0, 0))
    edge_shape = jax.ShapeDtypeStruct((64, LANES), f32)
    edge_room = pltpu.VMEM((BOX, LANES), f32)
    own, leaving, own_edge, other_edge = pl.pallas_call(
        depth_kernel,
        grid=(steps,),
        out_shape=(rows_shape, rows_shape, edge_shape, edge_shape),
        in_specs=[
            SMEM,
            pl.BlockSpec((SENDERS * PER, LANES), lambda b: (0, 0)),
            pl.BlockSpec((2, BOX, BOX), lambda b: (0, 0, 0)),
        ],
        out_specs=(rows_spec, rows_spec, edge_spec, edge_spec),
        scratch_shapes=[edge_room, edge_room],
        name="depth",
    )(half_pos.reshape(1), gathered, constants[2])
    own_edge = lax.ppermute(own_edge, everyone, edge_pairs(0))
    other_edge = lax.ppermute(other_edge, everyone, edge_pairs(1))
    other = lax.ppermute(leaving, "half", [(0, 1), (1, 0)])
    first, second = pl.pallas_call(
        square_kernel,
        grid=(steps,),
        out_shape=(row_shape, row_shape),
        in_specs=[rows_spec, rows_spec, edge_spec, edge_spec],
        out_specs=(row_spec, row_spec),
        scratch_shapes=[edge_room],
        name="square",
    )(own, other, own_edge, other_edge)
    before = lax.ppermute(second, everyone, row_pairs(1))
    after = lax.ppermute(first, everyone, row_pairs(-1))
    swap = (side_pos != half_pos).astype(jnp.int32).reshape(1)
    block_spec = pl.BlockSpec((2, BOX, LANES), lambda b: (0, 0, 0))
    block_shape = jax.ShapeDtypeStruct((2, BOX, LANES), f32)
    near, far = pl.pallas_call(
        blend_kernel,
        grid=(steps,),
        out_shape=(block_shape, block_shape),
        in_specs=[SMEM, rows_spec, rows_spec] + [row_spec] * 4,
        out_specs=(block_spec, block_spec),
        scratch_shapes=[pltpu.VMEM((2, 3, BOX, LANES), f32)],
        name="blend",
    )(swap, own, other, first, second, before, after)
    near = lax.ppermute(near, everyone, home_pairs(0))
    far = lax.ppermute(far, everyone, home_pairs(1))
    low = jnp.where(half_pos == 0, near, far)
    high = jnp.where(half_pos == 0, far, near)
    refined = jnp.concatenate([low, high], axis=2)
    return jnp.transpose(refined, (1, 0, 2))[None]


def solution(mesh):
    placed = (
        P("half", "particle", "slab", None),
        P("half", "particle", "slab"),
        P("half", "particle"),
        P("half", None),
        P(),
    )
    return jax.shard_map(
        on_device,
        mesh=mesh,
        in_specs=placed,
        out_specs=P("half", None, ("particle", "slab"), None),
        check_vma=False,
    )
```

time: 281 us -> 243 us (0.86)
  Pallas kernels: 47.3 us -> 35.1 us
  waiting for transfers between devices: 151 us -> 141 us
  starting transfers between devices: 65.5 us -> 59.2 us
  local copies, waits for them, and re-layouts: 12.3 us -> 6.04 us
  other arithmetic: 3.81 us -> 0.45 us
    pallas_call x4, Pallas kernels: 31.9 us -> 19.5 us  [the longest x1 5.88 us: on_device(): pl.pallas_call(depth_kernel, grid=(steps,), out_shape=(rows_shape, rows_s...]
    ppermute x5 -> x4, waiting for transfers between devices: 21.8 us -> 12.5 us  [the longest x1 10.2 us: on_device(): after = lax.ppermute(first, everyone, row_pairs(-1))]
    ppermute x1, starting transfers between devices: 10.1 us -> 3.8 us  [on_device(): near = lax.ppermute(near, everyone, home_pairs(0))]
    another operation x3 -> x0, local copies, waits for them, and re-layouts: 5.32 us -> none  [the longest x1 3.97 us: on_device(): flat_tiles = tiles[0].reshape(-1, tile_width)]
    ppermute x1, waiting for transfers between devices: 4.15 us -> 8.74 us  [on_device(): near = lax.ppermute(near, everyone, home_pairs(0))]
    ppermute x1, waiting for transfers between devices: 3.25 us -> 0.01 us  [on_device(): other = lax.ppermute(leaving, 'half', [(0, 1), (1, 0)])]
    unnamed x27 -> x24, local copies, waits for them, and re-layouts: 5.66 us -> 4.84 us
  transfers between devices with their start and end apart: 21 -> 20, of which waited for: 14 -> 13; matrix products, arithmetic and copies ran while one was open for 0% -> 0% of each run, Pallas kernels for 0% -> 0%
where the time goes in v2:
time: 243 us; the launch traced here: 242 us
  waiting for transfers between devices  141 us (58%)
  starting transfers between devices  59.2 us (24%)
  Pallas kernels  35.1 us (14%)
  local copies, waits for them, and re-layouts  6.04 us (2%)
    all_to_all x1, waiting for transfers between devices, on_device(): lax.all_to_all(sent.reshape(SENDERS, PER, LANES), ('particle', 'slab'), s...  72.5 us
    ppermute x4, waiting for transfers between devices, on_device(): lax.ppermute(part, here, mirror_pairs(e))  23.7 us
    pallas_call x1, Pallas kernels, on_device(): pl.pallas_call(planes_kernel, out_shape=jax.ShapeDtypeStruct((SENDERS * P...  15.6 us
    all_to_all x1, starting transfers between devices, on_device(): lax.all_to_all(sent.reshape(SENDERS, PER, LANES), ('particle', 'slab'), s...  14.8 us
    ppermute x4, starting transfers between devices, on_device(): lax.ppermute(part, here, mirror_pairs(e))  12.5 us
    ppermute x1, waiting for transfers between devices, on_device(): after = lax.ppermute(first, everyone, row_pairs(-1))  10.2 us
    ppermute x1, waiting for transfers between devices, on_device(): near = lax.ppermute(near, everyone, home_pairs(0))  8.74 us
    ppermute x1, waiting for transfers between devices, on_device(): lax.ppermute(come[2] + rise, here, up)  8.22 us
  transfers between devices with their start and end apart: 20, of which 13 were waited for; matrix products, arithmetic and copies ran while one was open for 0% of the time, Pallas kernels for 0%

profile of v2, /device:TPU:1, one launch (start us, length us, event | category | flops | bytes accessed | tf_op | source)
XLA Modules:
  0.0 241.7 jit_solution(12520372718977631030)
XLA Ops:
  0.0 4.5 %place.1 = (f32[32,4096]{1,0:T(8,128)}, f32[32,4096]{1,0:T(8,128)}, f32[16,4096]{1,0:T(8,128)}, f32[16,4096]{1,0:T(8,128)}, f32[32,4096]{1,0:T(8,128)}, /*index=...) custom-call(s32[1]{0:T(128)} %bitcast.3.slab_ref, s32[1]{0:T(128)} %bitcast.4.group_ref, ...), custom_call_target="tpu_custom_call" | custom-call | tf_op jit(solution)/shard_map/place/pallas_call | solution.py:344
  4.5 5.8 %collective-permute-start.1 = (f32[32,4096]{1,0:T(8,128)}, f32[32,4096]{1,0:T(8,128)S(1)}, u32[]{:S(2)}, u32[]{:S(2)}) collective-permute-start(f32[32,4096]{1,0:T(8,128)} %get-tuple-element.25), channel_id=1, source_target_pairs={{0,60},{4,56},{8,52},{12,48},{16,44},{20,40},{24,36},{28,32},{32,2... | collective-permute-start | bytes 1572872 | tf_op jit(solution)/shard_map/ppermute | solution.py:364
  10.3 1.6 collective-permute-start.2
  11.9 3.9 %collective-permute-start.8 = (f32[16,4096]{1,0:T(8,128)}, f32[16,4096]{1,0:T(8,128)S(1)}, u32[]{:S(2)}, u32[]{:S(2)}) collective-permute-start(f32[16,4096]{1,0:T(8,128)} %get-tuple-element.30), channel_id=1, source_target_pairs={{0,194},{4,198},{8,202},{12,206},{16,210},{20,214},{24,218},{28,22... | collective-permute-start | bytes 786440 | tf_op jit(solution)/shard_map/ppermute | solution.py:363
  15.9 0.0 copy-start.11
  15.9 0.2 collective-permute-start.7
  16.0 5.8 %collective-permute-done.2 = f32[16,4096]{1,0:T(8,128)S(1)} collective-permute-done((f32[16,4096]{1,0:T(8,128)}, f32[16,4096]{1,0:T(8,128)S(1)}, u32[]{:S(2)}, u32[]{:S(2)}) %collective-permute-start.2) | collective-permute-done | bytes 262176 | tf_op jit(solution)/shard_map/ppermute | solution.py:363
  21.8 0.0 collective-permute-done.1
  21.9 0.0 copy-start.4
  21.9 1.9 collective-permute-start.3
  23.8 0.0 collective-permute-done.8
  23.8 9.5 %collective-permute-done.7 = f32[32,4096]{1,0:T(8,128)S(1)} collective-permute-done((f32[32,4096]{1,0:T(8,128)}, f32[32,4096]{1,0:T(8,128)S(1)}, u32[]{:S(2)}, u32[]{:S(2)}) %collective-permute-start.7) | collective-permute-done | bytes 524320 | tf_op jit(solution)/shard_map/ppermute | solution.py:364
  33.4 5.5 %collective-permute-start.9 = (f32[32,4096]{1,0:T(8,128)S(1)}, f32[32,4096]{1,0:T(8,128)S(1)}, u32[]{:S(2)}, u32[]{:S(2)}) collective-permute-start(f32[32,4096]{1,0:T(8,128)S(1)} %pad_maximum_fusion.1), channel_id=1, source_target_pairs={{0,194},{4,198},{8,202},{12,206},{16,210},{20,214},{24,218},{28,22... | collective-permute-start | bytes 1572872 | tf_op jit(solution)/shard_map/ppermute | solution.py:368
  39.0 0.0 copy-done.11
  39.0 4.6 %collective-permute-start = (f32[32,4096]{1,0:T(8,128)S(1)}, f32[32,4096]{1,0:T(8,128)S(1)}, u32[]{:S(2)}, u32[]{:S(2)}) collective-permute-start(f32[32,4096]{1,0:T(8,128)S(1)} %copy-done.11), channel_id=1, source_target_pairs={{0,60},{4,56},{8,52},{12,48},{16,44},{20,40},{24,36},{28,32},{32,1... | collective-permute-start | bytes 1572872 | tf_op jit(solution)/shard_map/ppermute | solution.py:364
  43.6 0.0 copy-done.10
  43.6 1.9 collective-permute-start.6
  45.6 0.0 collective-permute-done.3
  45.6 0.0 copy-done.5
  45.6 0.1 add.32
  45.6 0.1 collective-permute-start.4
  45.7 3.2 %collective-permute-done.9 = f32[32,4096]{1,0:T(8,128)S(1)} collective-permute-done((f32[32,4096]{1,0:T(8,128)S(1)}, f32[32,4096]{1,0:T(8,128)S(1)}, u32[]{:S(2)}, u32[]{:S(2)}) %collective-permute-start.9) | collective-permute-done | bytes 524320 | tf_op jit(solution)/shard_map/ppermute | solution.py:368
  48.9 0.0 copy-done.4
  48.9 0.1 add.35
  48.9 3.5 %collective-permute-start.10 = (f32[32,4096]{1,0:T(8,128)S(1)}, f32[32,4096]{1,0:T(8,128)S(1)}, u32[]{:S(2)}, u32[]{:S(2)}) collective-permute-start(f32[32,4096]{1,0:T(8,128)S(1)} %add.35), channel_id=1, source_target_pairs={{0,194},{4,198},{8,202},{12,206},{16,210},{20,214},{24,218},{28,22... | collective-permute-start | bytes 1572872 | tf_op jit(solution)/shard_map/ppermute | solution.py:369
  52.4 3.8 %collective-permute-done = f32[32,4096]{1,0:T(8,128)S(1)} collective-permute-done((f32[32,4096]{1,0:T(8,128)S(1)}, f32[32,4096]{1,0:T(8,128)S(1)}, u32[]{:S(2)}, u32[]{:S(2)}) %collective-permute-start) | collective-permute-done | bytes 524320 | tf_op jit(solution)/shard_map/ppermute | solution.py:364
  56.3 2.8 %collective-permute-done.4 = f32[32,4096]{1,0:T(8,128)S(1)} collective-permute-done((f32[32,4096]{1,0:T(8,128)S(1)}, f32[32,4096]{1,0:T(8,128)S(1)}, u32[]{:S(2)}, u32[]{:S(2)}) %collective-permute-start.4) | collective-permute-done | bytes 524320 | tf_op jit(solution)/shard_map/ppermute | solution.py:369
  59.1 0.1 add.33
  59.1 0.1 collective-permute-start.5
  59.2 10.3 %collective-permute-done.6 = f32[32,4096]{1,0:T(8,128)S(1)} collective-permute-done((f32[32,4096]{1,0:T(8,128)S(1)}, f32[32,4096]{1,0:T(8,128)S(1)}, u32[]{:S(2)}, u32[]{:S(2)}) %collective-permute-start.6) | collective-permute-done | bytes 524320 | tf_op jit(solution)/shard_map/ppermute | solution.py:364
  69.5 0.0 collective-permute-done.10
  69.5 0.1 add.36
  69.5 1.3 collective-permute-start.11
  70.9 8.2 %collective-permute-done.5.up_ref = f32[32,4096]{1,0:T(8,128)S(1)} collective-permute-done((f32[32,4096]{1,0:T(8,128)S(1)}, f32[32,4096]{1,0:T(8,128)S(1)}, u32[]{:S(2)}, u32[]{:S(2)}) %collective-permute-start.5) | collective-permute-done | bytes 524320 | tf_op jit(solution)/shard_map/ppermute | solution.py:370
  79.1 3.5 %collective-permute-done.11.down_ref = f32[32,4096]{1,0:T(8,128)S(1)} collective-permute-done((f32[32,4096]{1,0:T(8,128)S(1)}, f32[32,4096]{1,0:T(8,128)S(1)}, u32[]{:S(2)}, u32[]{:S(2)}) %collective-permute-start.11) | collective-permute-done | bytes 524320 | tf_op jit(solution)/shard_map/ppermute | solution.py:370
  82.6 0.0 copy-done.6
  82.6 0.8 copy-done.7
  83.4 15.6 %planes.1 = f32[6144,128]{1,0:T(8,128)} custom-call(s32[6]{0:T(128)} %cut_ref.1, s32[1]{0:T(128)} %bitcast.2.kz_ref, f32[32,4096]{1,0:T(8,128)} %get-tuple-element.22.own_ref, f32[32,4096]{1,0:T(8,128)} %copy-done.6, f32[32,4096]{1,0:T(8,128)} %copy-done.7, bf16[4,256,256]{2,1,0:T(8,128)(2,1)} %constant.38.clone.cy_ref, ...), custom_call_target="tpu_custom_call" | custom-call | tf_op jit(solution)/shard_map/planes/pallas_call | solution.py:375
  99.0 14.8 %all-to-all-start = ((f32[128,48,128]{2,1,0:T(8,128)}), f32[128,48,128]{2,1,0:T(8,128)S(1)}, u32[]{:S(2)}, u32[]{:S(2)}) async-start(f32[128,48,128]{2,1,0:T(8,128)} %bitcast.16), calls=%async_computation | async-start | bytes 6291456 | tf_op jit(solution)/shard_map/all_to_all | solution.py:389
  113.8 72.5 %all-to-all-done = f32[128,48,128]{2,1,0:T(8,128)S(1)} async-done(((f32[128,48,128]{2,1,0:T(8,128)}), f32[128,48,128]{2,1,0:T(8,128)S(1)}, u32[]{:S(2)}, u32[]{:S(2)}) %all-to-all-start) | async-done | bytes 3145760 | tf_op jit(solution)/shard_map/all_to_all | solution.py:389
  186.3 1.6 copy-done
  188.0 5.9 %depth.1 = (f32[6,2,256,128]{3,2,1,0:T(8,128)}, f32[6,2,256,128]{3,2,1,0:T(8,128)}, f32[64,128]{1,0:T(8,128)}, f32[64,128]{1,0:T(8,128)}) custom-call(s32[1]{0:T(128)} %bitcast.1.core_ref, f32[6144,128]{1,0:T(8,128)} %bitcast.15, bf16[2,256,256]{2,1,0:T(8,128)(2,1)} %constant.40.clone.z_ref), custom_call_target="tpu_custom_call" | custom-call | tf_op jit(solution)/shard_map/depth/pallas_call | solution.py:401
  193.8 5.3 %collective-permute-start.12 = (f32[6,2,256,128]{3,2,1,0:T(8,128)}, f32[6,2,256,128]{3,2,1,0:T(8,128)S(1)}, u32[]{:S(2)}, u32[]{:S(2)}) collective-permute-start(f32[6,2,256,128]{3,2,1,0:T(8,128)} %get-tuple-element.32), channel_id=1, source_target_pairs={{0,1},{1,0},{2,3},{3,2},{4,5},{5,4},{6,7},{7,6},{8,9},{9,8},{10,11... | collective-permute-start | bytes 4718600 | tf_op jit(solution)/shard_map/ppermute | solution.py:416
  199.1 0.0 collective-permute-start.13
  199.1 2.6 %collective-permute-start.14 = (f32[64,128]{1,0:T(8,128)}, f32[64,128]{1,0:T(8,128)S(1)}, u32[]{:S(2)}, u32[]{:S(2)}) collective-permute-start(f32[64,128]{1,0:T(8,128)} %get-tuple-element.34), channel_id=1, source_target_pairs={{0,7},{1,6},{6,1},{7,0},{4,3},{5,2},{2,5},{3,4},{8,15},{9,14},{14,... | collective-permute-start | bytes 98312 | tf_op jit(solution)/shard_map/ppermute | solution.py:415
  201.7 1.2 collective-permute-done.13.own_edge_ref
  203.0 1.1 collective-permute-done.14.other_edge_ref
  204.0 0.0 collective-permute-done.12.other_ref
  204.0 0.0 copy-done.8
  204.0 0.6 copy-done.9
  204.6 0.6 copy-done.1
  205.2 4.5 %square.1 = (f32[6,256,128]{2,1,0:T(8,128)}, f32[6,256,128]{2,1,0:T(8,128)}) custom-call(f32[6,2,256,128]{3,2,1,0:T(8,128)} %get-tuple-element.31.own_ref, f32[6,2,256,128]{3,2,1,0:T(8,128)} %copy-done.1, f32[64,128]{1,0:T(8,128)} %copy-done.8, f32[64,128]{1,0:T(8,128)} %copy-done.9), custom_call_target="tpu_custom_call" | custom-call | tf_op jit(solution)/shard_map/square/pallas_call | solution.py:417
  209.8 0.3 collective-permute-start.16
  210.1 1.4 collective-permute-start.15
  211.5 10.2 %collective-permute-done.16.after_ref = f32[6,256,128]{2,1,0:T(8,128)S(1)} collective-permute-done((f32[6,256,128]{2,1,0:T(8,128)}, f32[6,256,128]{2,1,0:T(8,128)S(1)}, u32[]{:S(2)}, u32[]{:S(2)}) %collective-permute-start.16) | collective-permute-done | bytes 786464 | tf_op jit(solution)/shard_map/ppermute | solution.py:427
  221.7 0.0 collective-permute-done.15.before_ref
  221.7 0.9 copy-done.2
  222.6 0.3 copy-done.3
  222.9 4.6 %blend.1 = (f32[2,256,128]{2,1,0:T(8,128)}, f32[2,256,128]{2,1,0:T(8,128)}) custom-call(s32[1]{0:T(128)} %bitcast.swap_ref, f32[6,2,256,128]{3,2,1,0:T(8,128)} %get-tuple-element.31.own_ref, f32[6,2,256,128]{3,2,1,0:T(8,128)} %copy-done.1, f32[6,256,128]{2,1,0:T(8,128)} %get-tuple-element.35.first_ref, f32[6,256,128]{2,1,0:T(8,128)} %get-tuple-element.36.second_ref, ...), custom_call_target="tpu_custom_call" | custom-call | tf_op jit(solution)/shard_map/blend/pallas_call | solution.py:431
  227.5 3.8 %collective-permute-start.17 = (f32[2,256,128]{2,1,0:T(8,128)}, f32[2,256,128]{2,1,0:T(8,128)S(1)}, u32[]{:S(2)}, u32[]{:S(2)}) collective-permute-start(f32[2,256,128]{2,1,0:T(8,128)} %get-tuple-element.37), channel_id=1, source_target_pairs={{0,0},{1,2},{6,1},{7,3},{4,4},{5,6},{2,5},{3,7},{8,8},{9,10},{14,9... | collective-permute-start | bytes 786440 | tf_op jit(solution)/shard_map/ppermute | solution.py:440
  231.3 0.4 collective-permute-start.18
  231.7 8.7 %collective-permute-done.17 = f32[2,256,128]{2,1,0:T(8,128)S(1)} collective-permute-done((f32[2,256,128]{2,1,0:T(8,128)}, f32[2,256,128]{2,1,0:T(8,128)S(1)}, u32[]{:S(2)}, u32[]{:S(2)}) %collective-permute-start.17) | collective-permute-done | bytes 262176 | tf_op jit(solution)/shard_map/ppermute | solution.py:440
  240.4 0.0 collective-permute-done.18
  240.5 1.2 copy.9
  (16 shorter events, 0.3 us)
Async XLA Ops:
  4.5 17.3 %collective-permute-start.1 = (f32[32,4096]{1,0:T(8,128)}, f32[32,4096]{1,0:T(8,128)S(1)}, u32[]{:S(2)}, u32[]{:S(2)}) collective-permute-start(f32[32,4096]{1,0:T(8,128)} %get-tuple-element.25), channel_id=1, source_target_pairs={{0,60},{4,56},{8,52},{12,48},{16,44},{20,40},{24,36},{28,32},{32,2... | collective-permute-start | bytes 1572872 | tf_op jit(solution)/shard_map/ppermute | solution.py:364
  10.3 11.5 %collective-permute-start.2 = (f32[16,4096]{1,0:T(8,128)}, f32[16,4096]{1,0:T(8,128)S(1)}, u32[]{:S(2)}, u32[]{:S(2)}) collective-permute-start(f32[16,4096]{1,0:T(8,128)} %get-tuple-element.26), channel_id=1, source_target_pairs={{0,2},{4,6},{8,10},{12,14},{16,18},{20,22},{24,26},{28,30},{32,34}... | collective-permute-start | bytes 786440 | tf_op jit(solution)/shard_map/ppermute | solution.py:363
  11.9 11.9 %collective-permute-start.8 = (f32[16,4096]{1,0:T(8,128)}, f32[16,4096]{1,0:T(8,128)S(1)}, u32[]{:S(2)}, u32[]{:S(2)}) collective-permute-start(f32[16,4096]{1,0:T(8,128)} %get-tuple-element.30), channel_id=1, source_target_pairs={{0,194},{4,198},{8,202},{12,206},{16,210},{20,214},{24,218},{28,22... | collective-permute-start | bytes 786440 | tf_op jit(solution)/shard_map/ppermute | solution.py:363
  15.9 23.1 %copy-start.11 = (f32[32,4096]{1,0:T(8,128)S(1)}, f32[32,4096]{1,0:T(8,128)}, u32[]{:S(2)}) copy-start(f32[32,4096]{1,0:T(8,128)} %get-tuple-element.23) | copy-start | bytes 1572868
  15.9 27.7 %copy-start.10 = (f32[32,4096]{1,0:T(8,128)S(1)}, f32[32,4096]{1,0:T(8,128)}, u32[]{:S(2)}) copy-start(f32[32,4096]{1,0:T(8,128)} %get-tuple-element.27) | copy-start | bytes 1572868
  15.9 29.7 %copy-start.5 = (f32[32,4096]{1,0:T(8,128)S(1)}, f32[32,4096]{1,0:T(8,128)}, u32[]{:S(2)}) copy-start(f32[32,4096]{1,0:T(8,128)} %get-tuple-element.24) | copy-start | bytes 1572868
  15.9 17.5 %collective-permute-start.7 = (f32[32,4096]{1,0:T(8,128)}, f32[32,4096]{1,0:T(8,128)S(1)}, u32[]{:S(2)}, u32[]{:S(2)}) collective-permute-start(f32[32,4096]{1,0:T(8,128)} %get-tuple-element.29), channel_id=1, source_target_pairs={{0,60},{4,56},{8,52},{12,48},{16,44},{20,40},{24,36},{28,32},{32,2... | collective-permute-start | bytes 1572872 | tf_op jit(solution)/shard_map/ppermute | solution.py:364
  21.9 27.0 %copy-start.4 = (f32[32,4096]{1,0:T(8,128)S(1)}, f32[32,4096]{1,0:T(8,128)}, u32[]{:S(2)}) copy-start(f32[32,4096]{1,0:T(8,128)} %get-tuple-element.28) | copy-start | bytes 1572868
  21.9 23.7 %collective-permute-start.3 = (f32[32,4096]{1,0:T(8,128)S(1)}, f32[32,4096]{1,0:T(8,128)S(1)}, u32[]{:S(2)}, u32[]{:S(2)}) collective-permute-start(f32[32,4096]{1,0:T(8,128)S(1)} %pad_maximum_fusion), channel_id=1, source_target_pairs={{0,2},{4,6},{8,10},{12,14},{16,18},{20,22},{24,26},{28,30},{32,34}... | collective-permute-start | bytes 1572872 | tf_op jit(solution)/shard_map/ppermute | solution.py:368
  33.4 15.4 %collective-permute-start.9 = (f32[32,4096]{1,0:T(8,128)S(1)}, f32[32,4096]{1,0:T(8,128)S(1)}, u32[]{:S(2)}, u32[]{:S(2)}) collective-permute-start(f32[32,4096]{1,0:T(8,128)S(1)} %pad_maximum_fusion.1), channel_id=1, source_target_pairs={{0,194},{4,198},{8,202},{12,206},{16,210},{20,214},{24,218},{28,22... | collective-permute-start | bytes 1572872 | tf_op jit(solution)/shard_map/ppermute | solution.py:368
  39.0 17.3 %collective-permute-start = (f32[32,4096]{1,0:T(8,128)S(1)}, f32[32,4096]{1,0:T(8,128)S(1)}, u32[]{:S(2)}, u32[]{:S(2)}) collective-permute-start(f32[32,4096]{1,0:T(8,128)S(1)} %copy-done.11), channel_id=1, source_target_pairs={{0,60},{4,56},{8,52},{12,48},{16,44},{20,40},{24,36},{28,32},{32,1... | collective-permute-start | bytes 1572872 | tf_op jit(solution)/shard_map/ppermute | solution.py:364
  43.6 25.9 %collective-permute-start.6 = (f32[32,4096]{1,0:T(8,128)S(1)}, f32[32,4096]{1,0:T(8,128)S(1)}, u32[]{:S(2)}, u32[]{:S(2)}) collective-permute-start(f32[32,4096]{1,0:T(8,128)S(1)} %copy-done.10), channel_id=1, source_target_pairs={{0,60},{4,56},{8,52},{12,48},{16,44},{20,40},{24,36},{28,32},{32,2... | collective-permute-start | bytes 1572872 | tf_op jit(solution)/shard_map/ppermute | solution.py:364
  45.6 13.4 %collective-permute-start.4 = (f32[32,4096]{1,0:T(8,128)S(1)}, f32[32,4096]{1,0:T(8,128)S(1)}, u32[]{:S(2)}, u32[]{:S(2)}) collective-permute-start(f32[32,4096]{1,0:T(8,128)S(1)} %add.32), channel_id=1, source_target_pairs={{0,2},{4,6},{8,10},{12,14},{16,18},{20,22},{24,26},{28,30},{32,34}... | collective-permute-start | bytes 1572872 | tf_op jit(solution)/shard_map/ppermute | solution.py:369
  48.9 20.6 %collective-permute-start.10 = (f32[32,4096]{1,0:T(8,128)S(1)}, f32[32,4096]{1,0:T(8,128)S(1)}, u32[]{:S(2)}, u32[]{:S(2)}) collective-permute-start(f32[32,4096]{1,0:T(8,128)S(1)} %add.35), channel_id=1, source_target_pairs={{0,194},{4,198},{8,202},{12,206},{16,210},{20,214},{24,218},{28,22... | collective-permute-start | bytes 1572872 | tf_op jit(solution)/shard_map/ppermute | solution.py:369
  59.1 20.0 %collective-permute-start.5 = (f32[32,4096]{1,0:T(8,128)S(1)}, f32[32,4096]{1,0:T(8,128)S(1)}, u32[]{:S(2)}, u32[]{:S(2)}) collective-permute-start(f32[32,4096]{1,0:T(8,128)S(1)} %add.33), channel_id=1, source_target_pairs={{0,2},{4,6},{8,10},{12,14},{16,18},{20,22},{24,26},{28,30},{32,34}... | collective-permute-start | bytes 1572872 | tf_op jit(solution)/shard_map/ppermute | solution.py:370
  69.5 13.1 %collective-permute-start.11 = (f32[32,4096]{1,0:T(8,128)S(1)}, f32[32,4096]{1,0:T(8,128)S(1)}, u32[]{:S(2)}, u32[]{:S(2)}) collective-permute-start(f32[32,4096]{1,0:T(8,128)S(1)} %add.36), channel_id=1, source_target_pairs={{0,194},{4,198},{8,202},{12,206},{16,210},{20,214},{24,218},{28,22... | collective-permute-start | bytes 1572872 | tf_op jit(solution)/shard_map/ppermute | solution.py:370
  79.1 3.6 %copy-start.6 = (f32[32,4096]{1,0:T(8,128)}, f32[32,4096]{1,0:T(8,128)S(1)}, u32[]{:S(2)}) copy-start(f32[32,4096]{1,0:T(8,128)S(1)} %collective-permute-done.5.up_ref) | copy-start | bytes 1572868
  82.6 0.8 copy-start.7
  99.0 87.3 %all-to-all-start = ((f32[128,48,128]{2,1,0:T(8,128)}), f32[128,48,128]{2,1,0:T(8,128)S(1)}, u32[]{:S(2)}, u32[]{:S(2)}) async-start(f32[128,48,128]{2,1,0:T(8,128)} %bitcast.16), calls=%async_computation | async-start | bytes 6291456 | tf_op jit(solution)/shard_map/all_to_all | solution.py:389
  186.3 1.6 copy-start
  193.8 10.2 %collective-permute-start.12 = (f32[6,2,256,128]{3,2,1,0:T(8,128)}, f32[6,2,256,128]{3,2,1,0:T(8,128)S(1)}, u32[]{:S(2)}, u32[]{:S(2)}) collective-permute-start(f32[6,2,256,128]{3,2,1,0:T(8,128)} %get-tuple-element.32), channel_id=1, source_target_pairs={{0,1},{1,0},{2,3},{3,2},{4,5},{5,4},{6,7},{7,6},{8,9},{9,8},{10,11... | collective-permute-start | bytes 4718600 | tf_op jit(solution)/shard_map/ppermute | solution.py:416
  199.1 3.9 %collective-permute-start.13 = (f32[64,128]{1,0:T(8,128)}, f32[64,128]{1,0:T(8,128)S(1)}, u32[]{:S(2)}, u32[]{:S(2)}) collective-permute-start(f32[64,128]{1,0:T(8,128)} %get-tuple-element.33), channel_id=1, source_target_pairs={{0,6},{1,7},{6,0},{7,1},{4,2},{5,3},{2,4},{3,5},{8,14},{9,15},{14,... | collective-permute-start | bytes 98312 | tf_op jit(solution)/shard_map/ppermute | solution.py:414
  199.1 4.9 %collective-permute-start.14 = (f32[64,128]{1,0:T(8,128)}, f32[64,128]{1,0:T(8,128)S(1)}, u32[]{:S(2)}, u32[]{:S(2)}) collective-permute-start(f32[64,128]{1,0:T(8,128)} %get-tuple-element.34), channel_id=1, source_target_pairs={{0,7},{1,6},{6,1},{7,0},{4,3},{5,2},{2,5},{3,4},{8,15},{9,14},{14,... | collective-permute-start | bytes 98312 | tf_op jit(solution)/shard_map/ppermute | solution.py:415
  203.0 1.1 copy-start.8
  204.0 0.6 copy-start.9
  204.0 1.2 copy-start.1
  209.8 11.9 %collective-permute-start.16 = (f32[6,256,128]{2,1,0:T(8,128)}, f32[6,256,128]{2,1,0:T(8,128)S(1)}, u32[]{:S(2)}, u32[]{:S(2)}) collective-permute-start(f32[6,256,128]{2,1,0:T(8,128)} %get-tuple-element.35.first_ref), channel_id=1, source_target_pairs={{0,253},{6,251},{1,0},{7,6},{4,1},{2,7},{5,4},{3,2},{8,5},{14,3},{... | collective-permute-start | bytes 2359304 | tf_op jit(solution)/shard_map/ppermute | solution.py:427
  210.1 11.6 %collective-permute-start.15 = (f32[6,256,128]{2,1,0:T(8,128)}, f32[6,256,128]{2,1,0:T(8,128)S(1)}, u32[]{:S(2)}, u32[]{:S(2)}) collective-permute-start(f32[6,256,128]{2,1,0:T(8,128)} %get-tuple-element.36.second_ref), channel_id=1, source_target_pairs={{0,1},{6,7},{1,4},{7,2},{4,5},{2,3},{5,8},{3,14},{8,9},{14,15},{9,... | collective-permute-start | bytes 2359304 | tf_op jit(solution)/shard_map/ppermute | solution.py:426
  221.7 0.9 copy-start.2
  221.7 1.2 copy-start.3
  227.5 12.9 %collective-permute-start.17 = (f32[2,256,128]{2,1,0:T(8,128)}, f32[2,256,128]{2,1,0:T(8,128)S(1)}, u32[]{:S(2)}, u32[]{:S(2)}) collective-permute-start(f32[2,256,128]{2,1,0:T(8,128)} %get-tuple-element.37), channel_id=1, source_target_pairs={{0,0},{1,2},{6,1},{7,3},{4,4},{5,6},{2,5},{3,7},{8,8},{9,10},{14,9... | collective-permute-start | bytes 786440 | tf_op jit(solution)/shard_map/ppermute | solution.py:440
  231.3 9.1 %collective-permute-start.18 = (f32[2,256,128]{2,1,0:T(8,128)}, f32[2,256,128]{2,1,0:T(8,128)S(1)}, u32[]{:S(2)}, u32[]{:S(2)}) collective-permute-start(f32[2,256,128]{2,1,0:T(8,128)} %get-tuple-element.38), channel_id=1, source_target_pairs={{0,1},{1,3},{6,0},{7,2},{4,5},{5,7},{2,4},{3,6},{8,9},{9,11},{14,8... | collective-permute-start | bytes 786440 | tf_op jit(solution)/shard_map/ppermute | solution.py:441

commit v3 on v2

--- a/solution.py
+++ b/solution.py
@@ -38,14 +38,16 @@
 
 def tables():
     places = np.arange(BOX)
-    block = places % 64
-    y_order = (block % 32 * 2 + block // 32) * 4 + places // 64
-    ky_order = (places % BLOCKS) * TILE_ROWS + places // BLOCKS
-    turn = angles(y_order, ky_order)
-    cosine, sine = np.cos(turn), np.sin(turn)
-    along_y = np.stack(split(cosine) + split(sine))
-    turn = angles(places, places)
-    along_x = np.stack(split(np.cos(turn)) + split(np.sin(turn)))
+    near = np.arange(HALF)
+    along_y, along_x = [], []
+    for odd in range(2):
+        turn = angles(near, near % BLOCKS * TILE_ROWS + near // BLOCKS * 2 + odd)
+        cosine, sine = np.cos(turn), np.sin(turn)
+        along_y.append(np.stack(split(np.block([[cosine, -sine], [sine, cosine]]))))
+        turn = angles(2 * near + odd, near)
+        cosine, sine = np.cos(turn), np.sin(turn)
+        along_x.append(np.stack(split(np.block([[cosine, sine], [-sine, cosine]]))))
+    along_y, along_x = np.stack(along_y), np.stack(along_x)
     sender = np.arange(SENDERS)
     group, slab = sender // SLABS, sender % SLABS
     plane = slab * 8 + group * 2 + (slab >= SLABS // 2)
@@ -70,7 +72,7 @@
 
 
 def place_kernel(slab_ref, group_ref, index_ref, bin_ref, gain_ref, tile_ref, *refs):
-    outs, (kept_mark, sent_mark, sent_mark_first, turn, saved) = refs[:9], refs[9:]
+    outs, (kept_mark, sent_mark, sent_mark_first, turn, moved, saved) = refs[:9], refs[9:]
     step = pl.program_id(0)
     slab, group = slab_ref[0], group_ref[0]
     depth, late = group * 2 + slab % 2, slab // (SLABS // 2)
@@ -108,16 +110,20 @@
             sent_mark_first[rows, :] = mark(start + ((BLOCKS - row) & (BLOCKS - 1)), slots, gains)
         line = lax.broadcasted_iota(jnp.int32, (BOX, BOX), 0)
         wide = lax.broadcasted_iota(jnp.int32, (BOX, BOX), 1)
-        turn[...] = jnp.where(((line + wide) & (BOX - 1)) == 0, 1.0, 0.0).astype(bf16)
+        wide = (wide & (HALF - 1)) * 2 + (wide >> 7)
+        turn[:, :BOX] = jnp.where(line == wide, 1.0, 0.0).astype(bf16)
+        turn[:, BOX:] = jnp.where(((line + wide) & (BOX - 1)) == 0, 1.0, 0.0).astype(bf16)
 
     sign = jnp.where(step == 1, -1.0, 1.0)
     tile = tile_ref[...].reshape(-1, TILE_ROWS * BOX)
     for r in range(TILE_ROWS):
+        both = dot(tile[:, r * BOX : (r + 1) * BOX], turn[...])
+        moved[r, 0] = both[:, :BOX].astype(bf16)
+        moved[r, 1] = (both[:, BOX:] * sign).astype(bf16)
+    for r in range(TILE_ROWS):
         cols = pl.ds(r * BOX, BOX)
-        back = (TILE_ROWS - r) % TILE_ROWS * BOX
-        kept = dot(kept_mark[...], tile[:, r * BOX : (r + 1) * BOX])
-        flipped = (dot(tile[:, back : back + BOX], turn[...]) * sign).astype(bf16)
-        sent = dot((sent_mark if r else sent_mark_first)[...], flipped)
+        kept = dot(kept_mark[...], moved[r, 0])
+        sent = dot((sent_mark if r else sent_mark_first)[...], moved[(TILE_ROWS - r) % TILE_ROWS, 1])
         if r == 0:
             first = (row == 0) & (col == 0)
             last_sent = saved[...]
@@ -139,58 +145,70 @@
             out_ref[:, cols] = part
 
 
-def fill(four_ref, out_ref, down):
-    for third, low in enumerate((0, 0, 1) if down else (0, 1, 0)):
-        cosine, sine = four_ref[low], four_ref[2 + low]
-        start = third * 2 * BOX
-        for i in range(2):
-            for j in range(2):
-                block = cosine if i == j else (sine if (i == 1) != down else -sine)
-                if down:
-                    out_ref[start + i * BOX : start + (i + 1) * BOX, j * BOX : (j + 1) * BOX] = block
-                else:
-                    out_ref[i * BOX : (i + 1) * BOX, start + j * BOX : start + (j + 1) * BOX] = block
-
-
-def planes_kernel(cut_ref, kz_ref, own_ref, up_ref, down_ref, cy_ref, cx_ref, out_ref, sh, sl, radius, y_ref, x_ref):
-    fill(cy_ref, y_ref, False)
-    fill(cx_ref, x_ref, True)
+def beside(*parts):
+    return jnp.concatenate(parts, axis=1)
+
+
+def above(*parts):
+    return jnp.concatenate(parts, axis=0)
+
+
+def planes_kernel(cut_ref, kz_ref, own_ref, up_ref, down_ref, y_ref, x_ref, out_ref, sh, sl, radius):
     alone = kz_ref[0] == 0
     for i in range(16):
+        c, r = divmod(i, TILE_ROWS)
         cols = pl.ds(i * BOX, BOX)
-        rows = pl.ds(i * BLOCKS, BLOCKS)
+        rows = pl.ds(r % 2 * BOX + c * HALF + r // 2 * BLOCKS, BLOCKS)
         whole = own_ref[:, cols] + up_ref[:, cols] + down_ref[:, cols]
         if i == TILE_ROWS:
             last = whole[0:1, 0:1]
         sh[rows, :], sl[rows, :] = two(whole)
     line = lax.broadcasted_iota(jnp.int32, (BOX, BOX), 0)
     col = lax.broadcasted_iota(jnp.int32, (BOX, BOX), 1)
-    ky = (line & (BLOCKS - 1)) * TILE_ROWS + (line >> 5)
+    ky = (line & (BLOCKS - 1)) * TILE_ROWS + ((line >> 5) & 3) * 2 + (line >> 7)
+    kx = (col & (HALF - 1)) * 2 + (col >> 7)
     ky = ((ky + HALF) & (BOX - 1)) - HALF
-    kx = ((col + HALF) & (BOX - 1)) - HALF
+    kx = ((kx + HALF) & (BOX - 1)) - HALF
     kz = ((kz_ref[0] + HALF) & (BOX - 1)) - HALF
     radius[...] = (ky * ky + kx * kx + kz * kz).astype(f32)
-
-    @pl.loop(0, BANDS)
-    def _(b):
-        limit = (cut_ref[b] * cut_ref[b]).astype(f32)
-        mask = jnp.where(radius[...] <= limit, 1.0, 0.0).astype(bf16)
-        mask = jnp.concatenate([mask, mask], axis=0)
-        high, low = sh[...] * mask, sl[...] * mask
-        mid = dot(y_ref[...], jnp.concatenate([high, high, low], axis=0))
-        high, low = two(jnp.concatenate([mid[:BOX], mid[BOX:]], axis=1))
-        both = dot(jnp.concatenate([high, low, high], axis=1), x_ref[...])
-        even, odd = both[:, :BOX], both[:, BOX:]
-        top = jnp.where(cut_ref[b] >= HALF, last, 0.0)
-        odd = jnp.where(alone, jnp.broadcast_to(top, odd.shape), odd)
-        for c, part in enumerate((even, odd)):
-            for j in range(4):
-                for side in range(2):
-                    for odd_block in range(2):
-                        start = j * 64 + odd_block * 32
-                        block = part[start : start + 32, side * LANES : (side + 1) * LANES]
-                        goal = 2 * (odd_block ^ side) + side
-                        out_ref[pl.ds(goal * PER + b * 8 + c * 4 + j, 32, stride=4 * PER), :] = block
+    upper = lax.broadcasted_iota(jnp.int32, (BLOCKS, 8, LANES), 1) < 4
+
+    @pl.loop(0, BANDS // 2)
+    def _(pair):
+        parts = []
+        for odd in range(2):
+            sides = []
+            for i in range(2):
+                cut = cut_ref[pair * 2 + i]
+                near = radius[odd * HALF : (odd + 1) * HALF, :] <= (cut * cut).astype(f32)
+                mask = jnp.where(near, 1.0, 0.0).astype(bf16)
+                mask = above(mask, mask)
+                rows = pl.ds(odd * BOX, BOX)
+                high, low = sh[rows, :] * mask, sl[rows, :] * mask
+                sides.append(above(high, high, low))
+            parts.append(dot(beside(y_ref[odd, 0], y_ref[odd, 1], y_ref[odd, 0]), beside(*sides)))
+        plus, minus = parts[0] + parts[1], parts[0] - parts[1]
+        mids = ([], [])
+        for i in range(2):
+            cols = slice(i * BOX, (i + 1) * BOX)
+            real = two(above(plus[:HALF, cols], minus[:HALF, cols]))
+            imag = two(above(plus[HALF:, cols], minus[HALF:, cols]))
+            for odd in range(2):
+                few = slice(odd * HALF, (odd + 1) * HALF)
+                high = beside(real[0][:, few], imag[0][:, few])
+                low = beside(real[1][:, few], imag[1][:, few])
+                mids[odd].append(beside(high, low, high))
+        parts = [dot(above(*mids[odd]), above(x_ref[odd, 0], x_ref[odd, 0], x_ref[odd, 1])) for odd in range(2)]
+        for i in range(2):
+            b = pair * 2 + i
+            value = jnp.where(cut_ref[b] >= HALF, last, 0.0)
+            first, second = parts[0][i * BOX : (i + 1) * BOX], parts[1][i * BOX : (i + 1) * BOX]
+            for side, full in enumerate((first + second, first - second)):
+                even, odd = full[:, :LANES], full[:, LANES:]
+                odd = jnp.where(alone, jnp.broadcast_to(value, odd.shape), odd)
+                even, odd = even.reshape(BLOCKS, 8, LANES), odd.reshape(BLOCKS, 8, LANES)
+                out_ref[:, 3 * side, b] = jnp.where(upper, even, pltpu.roll(odd, 4, 1))
+                out_ref[:, 2 - side, b] = jnp.where(upper, pltpu.roll(even, 4, 1), odd)
 
 
 def depth_kernel(core_ref, come_ref, z_ref, own_ref, other_ref, own_edge_ref, other_edge_ref, own_edge, other_edge):
@@ -355,35 +373,33 @@
         ],
         out_specs=tuple(pl.BlockSpec((h, tile_width // 2), lambda i: (0, i)) for h in heights),
         scratch_shapes=[pltpu.VMEM((4 * BLOCKS, entries), bf16)] * 3
-        + [pltpu.VMEM((BOX, BOX), bf16), pltpu.VMEM((4 * BLOCKS, BOX), f32)],
+        + [pltpu.VMEM((BOX, 2 * BOX), bf16), pltpu.VMEM((TILE_ROWS, 2, entries, BOX), bf16)]
+        + [pltpu.VMEM((4 * BLOCKS, BOX), f32)],
         name="place",
     )(slab_pos.reshape(1), group_pos.reshape(1), tile_index[0].T, pose_bin, bin_gain, tiles[0])
     here = ("particle", "slab")
     up, down = ring_pairs(1), ring_pairs(-1)
-    rise, sink = lax.ppermute(far_a, here, up), lax.ppermute(far_b, here, down)
-    come = [lax.ppermute(part, here, mirror_pairs(e)) for part, e in zip(sent, (3, -3, 1, -1))]
     cut = BLOCKS // 2
+
+    def send(part, pairs):
+        return lax.ppermute(part, here, pairs)
+
+    come = [send(sent[i], mirror_pairs(e)) for i, e in enumerate((3, -3, 1, -1))]
+    rise, sink = send(far_a, up), send(far_b, down)
     rise = jnp.concatenate([come[0][:cut] + rise, come[0][cut:]], axis=0)
     sink = jnp.concatenate([come[1][:cut], come[1][cut:] + sink], axis=0)
-    rise, sink = lax.ppermute(rise, here, up), lax.ppermute(sink, here, down)
-    rise, sink = lax.ppermute(ahead + rise, here, up), lax.ppermute(behind + sink, here, down)
-    rise, sink = lax.ppermute(come[2] + rise, here, up), lax.ppermute(come[3] + sink, here, down)
+    rise, sink = send(rise, up), send(sink, down)
+    rise, sink = send(ahead + rise, up), send(behind + sink, down)
+    rise, sink = send(come[2] + rise, up), send(come[3] + sink, down)
     plane = (slab_pos * 8 + group_pos * 2 + late).reshape(1)
 
     constants = [jnp.asarray(t) for t in tables()]
-    square = (2 * BOX, BOX)
     sent = pl.pallas_call(
         planes_kernel,
-        out_shape=jax.ShapeDtypeStruct((SENDERS * PER, LANES), f32),
+        out_shape=jax.ShapeDtypeStruct((SENDERS // 4, 4, BANDS, 8, LANES), f32),
         in_specs=[SMEM, SMEM] + [VMEM] * 5,
         out_specs=VMEM,
-        scratch_shapes=[
-            pltpu.VMEM(square, bf16),
-            pltpu.VMEM(square, bf16),
-            pltpu.VMEM((BOX, BOX), f32),
-            pltpu.VMEM((2 * BOX, 6 * BOX), bf16),
-            pltpu.VMEM((6 * BOX, 2 * BOX), bf16),
-        ],
+        scratch_shapes=[pltpu.VMEM((2 * BOX, BOX), bf16)] * 2 + [pltpu.VMEM((BOX, BOX), f32)],
         name="planes",
     )(cutoffs, plane, own, rise, sink, *constants[:2])
     gathered = lax.all_to_all(
@@ -453,6 +469,7 @@
         P("half", None),
         P(),
     )
+
     return jax.shard_map(
         on_device,
         mesh=mesh,

time: 243 us -> 234 us (0.963)
  Pallas kernels: 35.1 us -> 26.8 us
    pallas_call x1, Pallas kernels: 15.6 us -> 6.93 us  [on_device(): pl.pallas_call(planes_kernel, out_shape=jax.ShapeDtypeStruct((SENDERS //...]
where the time goes in v3:
time: 234 us; the launch traced here: 233 us
  waiting for transfers between devices  141 us (60%)
  starting transfers between devices  59.2 us (25%)
  Pallas kernels  26.8 us (11%)
  local copies, waits for them, and re-layouts  6.04 us (3%)
    all_to_all x1, waiting for transfers between devices, on_device(): lax.all_to_all(sent.reshape(SENDERS, PER, LANES), ('particle', 'slab'), s...  72.5 us
    ppermute x12, waiting for transfers between devices, send(): return lax.ppermute(part, here, pairs)  47.1 us
    ppermute x12, starting transfers between devices, send(): return lax.ppermute(part, here, pairs)  30.5 us
    all_to_all x1, starting transfers between devices, on_device(): lax.all_to_all(sent.reshape(SENDERS, PER, LANES), ('particle', 'slab'), s...  14.8 us
    ppermute x1, waiting for transfers between devices, on_device(): after = lax.ppermute(first, everyone, row_pairs(-1))  10.2 us
    ppermute x1, waiting for transfers between devices, on_device(): near = lax.ppermute(near, everyone, home_pairs(0))  8.74 us
    pallas_call x1, Pallas kernels, on_device(): pl.pallas_call(planes_kernel, out_shape=jax.ShapeDtypeStruct((SENDERS //...  6.93 us
    pallas_call x1, Pallas kernels, on_device(): pl.pallas_call(depth_kernel, grid=(steps,), out_shape=(rows_shape, rows_s...  5.87 us
  transfers between devices with their start and end apart: 20, of which 13 were waited for; matrix products, arithmetic and copies ran while one was open for 0% of the time, Pallas kernels for 0%

profile of v3, /device:TPU:1, one launch (start us, length us, event | category | flops | bytes accessed | tf_op | source)
XLA Modules:
  0.0 233.5 jit_solution(23536837539308672)
XLA Ops:
  0.0 4.9 %place.1 = (f32[32,4096]{1,0:T(8,128)}, f32[32,4096]{1,0:T(8,128)}, f32[16,4096]{1,0:T(8,128)}, f32[16,4096]{1,0:T(8,128)}, f32[32,4096]{1,0:T(8,128)}, /*index=...) custom-call(s32[1]{0:T(128)} %bitcast.3.slab_ref, s32[1]{0:T(128)} %bitcast.4.group_ref, ...), custom_call_target="tpu_custom_call" | custom-call | tf_op jit(solution)/shard_map/place/pallas_call | solution.py:362
  4.9 5.8 %collective-permute-start.1 = (f32[32,4096]{1,0:T(8,128)}, f32[32,4096]{1,0:T(8,128)S(1)}, u32[]{:S(2)}, u32[]{:S(2)}) collective-permute-start(f32[32,4096]{1,0:T(8,128)} %get-tuple-element.25), channel_id=1, source_target_pairs={{0,60},{4,56},{8,52},{12,48},{16,44},{20,40},{24,36},{28,32},{32,2... | collective-permute-start | bytes 1572872 | tf_op jit(solution)/shard_map/ppermute | solution.py:385
  10.7 1.6 collective-permute-start.2
  12.4 3.9 %collective-permute-start.8 = (f32[16,4096]{1,0:T(8,128)}, f32[16,4096]{1,0:T(8,128)S(1)}, u32[]{:S(2)}, u32[]{:S(2)}) collective-permute-start(f32[16,4096]{1,0:T(8,128)} %get-tuple-element.30), channel_id=1, source_target_pairs={{0,194},{4,198},{8,202},{12,206},{16,210},{20,214},{24,218},{28,22... | collective-permute-start | bytes 786440 | tf_op jit(solution)/shard_map/ppermute | solution.py:385
  16.3 0.0 copy-start.11
  16.3 0.2 collective-permute-start.7
  16.5 5.7 %collective-permute-done.2 = f32[16,4096]{1,0:T(8,128)S(1)} collective-permute-done((f32[16,4096]{1,0:T(8,128)}, f32[16,4096]{1,0:T(8,128)S(1)}, u32[]{:S(2)}, u32[]{:S(2)}) %collective-permute-start.2) | collective-permute-done | bytes 262176 | tf_op jit(solution)/shard_map/ppermute | solution.py:385
  22.2 0.0 collective-permute-done.1
  22.3 0.0 copy-start.4
  22.3 1.9 collective-permute-start.3
  24.3 0.0 collective-permute-done.8
  24.3 9.5 %collective-permute-done.7 = f32[32,4096]{1,0:T(8,128)S(1)} collective-permute-done((f32[32,4096]{1,0:T(8,128)}, f32[32,4096]{1,0:T(8,128)S(1)}, u32[]{:S(2)}, u32[]{:S(2)}) %collective-permute-start.7) | collective-permute-done | bytes 524320 | tf_op jit(solution)/shard_map/ppermute | solution.py:385
  33.9 5.5 %collective-permute-start.9 = (f32[32,4096]{1,0:T(8,128)S(1)}, f32[32,4096]{1,0:T(8,128)S(1)}, u32[]{:S(2)}, u32[]{:S(2)}) collective-permute-start(f32[32,4096]{1,0:T(8,128)S(1)} %pad_maximum_fusion.1), channel_id=1, source_target_pairs={{0,194},{4,198},{8,202},{12,206},{16,210},{20,214},{24,218},{28,22... | collective-permute-start | bytes 1572872 | tf_op jit(solution)/shard_map/ppermute | solution.py:385
  39.4 0.0 copy-done.11
  39.4 4.6 %collective-permute-start = (f32[32,4096]{1,0:T(8,128)S(1)}, f32[32,4096]{1,0:T(8,128)S(1)}, u32[]{:S(2)}, u32[]{:S(2)}) collective-permute-start(f32[32,4096]{1,0:T(8,128)S(1)} %copy-done.11), channel_id=1, source_target_pairs={{0,60},{4,56},{8,52},{12,48},{16,44},{20,40},{24,36},{28,32},{32,1... | collective-permute-start | bytes 1572872 | tf_op jit(solution)/shard_map/ppermute | solution.py:385
  44.0 0.0 copy-done.10
  44.0 1.9 collective-permute-start.6
  46.0 0.0 collective-permute-done.3
  46.0 0.0 copy-done.5
  46.0 0.1 add.32
  46.1 0.1 collective-permute-start.4
  46.2 3.1 %collective-permute-done.9 = f32[32,4096]{1,0:T(8,128)S(1)} collective-permute-done((f32[32,4096]{1,0:T(8,128)S(1)}, f32[32,4096]{1,0:T(8,128)S(1)}, u32[]{:S(2)}, u32[]{:S(2)}) %collective-permute-start.9) | collective-permute-done | bytes 524320 | tf_op jit(solution)/shard_map/ppermute | solution.py:385
  49.3 0.0 copy-done.4
  49.3 0.1 add.35
  49.4 3.5 %collective-permute-start.10 = (f32[32,4096]{1,0:T(8,128)S(1)}, f32[32,4096]{1,0:T(8,128)S(1)}, u32[]{:S(2)}, u32[]{:S(2)}) collective-permute-start(f32[32,4096]{1,0:T(8,128)S(1)} %add.35), channel_id=1, source_target_pairs={{0,194},{4,198},{8,202},{12,206},{16,210},{20,214},{24,218},{28,22... | collective-permute-start | bytes 1572872 | tf_op jit(solution)/shard_map/ppermute | solution.py:385
  52.9 3.8 %collective-permute-done = f32[32,4096]{1,0:T(8,128)S(1)} collective-permute-done((f32[32,4096]{1,0:T(8,128)S(1)}, f32[32,4096]{1,0:T(8,128)S(1)}, u32[]{:S(2)}, u32[]{:S(2)}) %collective-permute-start) | collective-permute-done | bytes 524320 | tf_op jit(solution)/shard_map/ppermute | solution.py:385
  56.7 2.8 %collective-permute-done.4 = f32[32,4096]{1,0:T(8,128)S(1)} collective-permute-done((f32[32,4096]{1,0:T(8,128)S(1)}, f32[32,4096]{1,0:T(8,128)S(1)}, u32[]{:S(2)}, u32[]{:S(2)}) %collective-permute-start.4) | collective-permute-done | bytes 524320 | tf_op jit(solution)/shard_map/ppermute | solution.py:385
  59.5 0.1 add.33
  59.6 0.1 collective-permute-start.5
  59.7 10.3 %collective-permute-done.6 = f32[32,4096]{1,0:T(8,128)S(1)} collective-permute-done((f32[32,4096]{1,0:T(8,128)S(1)}, f32[32,4096]{1,0:T(8,128)S(1)}, u32[]{:S(2)}, u32[]{:S(2)}) %collective-permute-start.6) | collective-permute-done | bytes 524320 | tf_op jit(solution)/shard_map/ppermute | solution.py:385
  69.9 0.0 collective-permute-done.10
  69.9 0.1 add.36
  70.0 1.3 collective-permute-start.11
  71.3 8.2 %collective-permute-done.5.up_ref = f32[32,4096]{1,0:T(8,128)S(1)} collective-permute-done((f32[32,4096]{1,0:T(8,128)S(1)}, f32[32,4096]{1,0:T(8,128)S(1)}, u32[]{:S(2)}, u32[]{:S(2)}) %collective-permute-start.5) | collective-permute-done | bytes 524320 | tf_op jit(solution)/shard_map/ppermute | solution.py:385
  79.5 3.5 %collective-permute-done.11.down_ref = f32[32,4096]{1,0:T(8,128)S(1)} collective-permute-done((f32[32,4096]{1,0:T(8,128)S(1)}, f32[32,4096]{1,0:T(8,128)S(1)}, u32[]{:S(2)}, u32[]{:S(2)}) %collective-permute-start.11) | collective-permute-done | bytes 524320 | tf_op jit(solution)/shard_map/ppermute | solution.py:385
  83.1 0.0 copy-done.6
  83.1 0.8 copy-done.7
  83.9 6.9 %planes.1 = f32[32,4,6,8,128]{4,3,2,1,0:T(8,128)} custom-call(s32[6]{0:T(128)} %cut_ref.1, s32[1]{0:T(128)} %bitcast.2.kz_ref, f32[32,4096]{1,0:T(8,128)} %get-tuple-element.22.own_ref, f32[32,4096]{1,0:T(8,128)} %copy-done.6, f32[32,4096]{1,0:T(8,128)} %copy-done.7, bf16[2,2,256,256]{3,2,1,0:T(8,128)(2,1)} %constant.38.clone.y_ref, ...), custom_call_target="tpu_custom_call" | custom-call | tf_op jit(solution)/shard_map/planes/pallas_call | solution.py:397
  90.8 14.8 %all-to-all-start = ((f32[128,48,128]{2,1,0:T(8,128)}), f32[128,48,128]{2,1,0:T(8,128)S(1)}, u32[]{:S(2)}, u32[]{:S(2)}) async-start(f32[128,48,128]{2,1,0:T(8,128)} %bitcast.16), calls=%async_computation | async-start | bytes 6291456 | tf_op jit(solution)/shard_map/all_to_all | solution.py:405
  105.6 72.5 %all-to-all-done = f32[128,48,128]{2,1,0:T(8,128)S(1)} async-done(((f32[128,48,128]{2,1,0:T(8,128)}), f32[128,48,128]{2,1,0:T(8,128)S(1)}, u32[]{:S(2)}, u32[]{:S(2)}) %all-to-all-start) | async-done | bytes 3145760 | tf_op jit(solution)/shard_map/all_to_all | solution.py:405
  178.1 1.6 copy-done
  179.7 5.9 %depth.1 = (f32[6,2,256,128]{3,2,1,0:T(8,128)}, f32[6,2,256,128]{3,2,1,0:T(8,128)}, f32[64,128]{1,0:T(8,128)}, f32[64,128]{1,0:T(8,128)}) custom-call(s32[1]{0:T(128)} %bitcast.1.core_ref, f32[6144,128]{1,0:T(8,128)} %bitcast.15, bf16[2,256,256]{2,1,0:T(8,128)(2,1)} %constant.40.clone.z_ref), custom_call_target="tpu_custom_call" | custom-call | tf_op jit(solution)/shard_map/depth/pallas_call | solution.py:417
  185.6 5.3 %collective-permute-start.12 = (f32[6,2,256,128]{3,2,1,0:T(8,128)}, f32[6,2,256,128]{3,2,1,0:T(8,128)S(1)}, u32[]{:S(2)}, u32[]{:S(2)}) collective-permute-start(f32[6,2,256,128]{3,2,1,0:T(8,128)} %get-tuple-element.32), channel_id=1, source_target_pairs={{0,1},{1,0},{2,3},{3,2},{4,5},{5,4},{6,7},{7,6},{8,9},{9,8},{10,11... | collective-permute-start | bytes 4718600 | tf_op jit(solution)/shard_map/ppermute | solution.py:432
  190.9 0.0 collective-permute-start.13
  190.9 2.6 %collective-permute-start.14 = (f32[64,128]{1,0:T(8,128)}, f32[64,128]{1,0:T(8,128)S(1)}, u32[]{:S(2)}, u32[]{:S(2)}) collective-permute-start(f32[64,128]{1,0:T(8,128)} %get-tuple-element.34), channel_id=1, source_target_pairs={{0,7},{1,6},{6,1},{7,0},{4,3},{5,2},{2,5},{3,4},{8,15},{9,14},{14,... | collective-permute-start | bytes 98312 | tf_op jit(solution)/shard_map/ppermute | solution.py:431
  193.5 1.2 collective-permute-done.13.own_edge_ref
  194.8 1.1 collective-permute-done.14.other_edge_ref
  195.8 0.0 collective-permute-done.12.other_ref
  195.8 0.0 copy-done.8
  195.8 0.6 copy-done.9
  196.4 0.6 copy-done.1
  197.0 4.5 %square.1 = (f32[6,256,128]{2,1,0:T(8,128)}, f32[6,256,128]{2,1,0:T(8,128)}) custom-call(f32[6,2,256,128]{3,2,1,0:T(8,128)} %get-tuple-element.31.own_ref, f32[6,2,256,128]{3,2,1,0:T(8,128)} %copy-done.1, f32[64,128]{1,0:T(8,128)} %copy-done.8, f32[64,128]{1,0:T(8,128)} %copy-done.9), custom_call_target="tpu_custom_call" | custom-call | tf_op jit(solution)/shard_map/square/pallas_call | solution.py:433
  201.5 0.3 collective-permute-start.16
  201.9 1.4 collective-permute-start.15
  203.3 10.2 %collective-permute-done.16.after_ref = f32[6,256,128]{2,1,0:T(8,128)S(1)} collective-permute-done((f32[6,256,128]{2,1,0:T(8,128)}, f32[6,256,128]{2,1,0:T(8,128)S(1)}, u32[]{:S(2)}, u32[]{:S(2)}) %collective-permute-start.16) | collective-permute-done | bytes 786464 | tf_op jit(solution)/shard_map/ppermute | solution.py:443
  213.5 0.0 collective-permute-done.15.before_ref
  213.5 0.9 copy-done.2
  214.4 0.3 copy-done.3
  214.7 4.6 %blend.1 = (f32[2,256,128]{2,1,0:T(8,128)}, f32[2,256,128]{2,1,0:T(8,128)}) custom-call(s32[1]{0:T(128)} %bitcast.swap_ref, f32[6,2,256,128]{3,2,1,0:T(8,128)} %get-tuple-element.31.own_ref, f32[6,2,256,128]{3,2,1,0:T(8,128)} %copy-done.1, f32[6,256,128]{2,1,0:T(8,128)} %get-tuple-element.35.first_ref, f32[6,256,128]{2,1,0:T(8,128)} %get-tuple-element.36.second_ref, ...), custom_call_target="tpu_custom_call" | custom-call | tf_op jit(solution)/shard_map/blend/pallas_call | solution.py:447
  219.2 3.8 %collective-permute-start.17 = (f32[2,256,128]{2,1,0:T(8,128)}, f32[2,256,128]{2,1,0:T(8,128)S(1)}, u32[]{:S(2)}, u32[]{:S(2)}) collective-permute-start(f32[2,256,128]{2,1,0:T(8,128)} %get-tuple-element.37), channel_id=1, source_target_pairs={{0,0},{1,2},{6,1},{7,3},{4,4},{5,6},{2,5},{3,7},{8,8},{9,10},{14,9... | collective-permute-start | bytes 786440 | tf_op jit(solution)/shard_map/ppermute | solution.py:456
  223.0 0.4 collective-permute-start.18
  223.4 8.7 %collective-permute-done.17 = f32[2,256,128]{2,1,0:T(8,128)S(1)} collective-permute-done((f32[2,256,128]{2,1,0:T(8,128)}, f32[2,256,128]{2,1,0:T(8,128)S(1)}, u32[]{:S(2)}, u32[]{:S(2)}) %collective-permute-start.17) | collective-permute-done | bytes 262176 | tf_op jit(solution)/shard_map/ppermute | solution.py:456
  232.2 0.0 collective-permute-done.18
  232.3 1.2 copy.9
  (16 shorter events, 0.3 us)
Async XLA Ops:
  4.9 17.3 %collective-permute-start.1 = (f32[32,4096]{1,0:T(8,128)}, f32[32,4096]{1,0:T(8,128)S(1)}, u32[]{:S(2)}, u32[]{:S(2)}) collective-permute-start(f32[32,4096]{1,0:T(8,128)} %get-tuple-element.25), channel_id=1, source_target_pairs={{0,60},{4,56},{8,52},{12,48},{16,44},{20,40},{24,36},{28,32},{32,2... | collective-permute-start | bytes 1572872 | tf_op jit(solution)/shard_map/ppermute | solution.py:385
  10.7 11.5 %collective-permute-start.2 = (f32[16,4096]{1,0:T(8,128)}, f32[16,4096]{1,0:T(8,128)S(1)}, u32[]{:S(2)}, u32[]{:S(2)}) collective-permute-start(f32[16,4096]{1,0:T(8,128)} %get-tuple-element.26), channel_id=1, source_target_pairs={{0,2},{4,6},{8,10},{12,14},{16,18},{20,22},{24,26},{28,30},{32,34}... | collective-permute-start | bytes 786440 | tf_op jit(solution)/shard_map/ppermute | solution.py:385
  12.4 11.9 %collective-permute-start.8 = (f32[16,4096]{1,0:T(8,128)}, f32[16,4096]{1,0:T(8,128)S(1)}, u32[]{:S(2)}, u32[]{:S(2)}) collective-permute-start(f32[16,4096]{1,0:T(8,128)} %get-tuple-element.30), channel_id=1, source_target_pairs={{0,194},{4,198},{8,202},{12,206},{16,210},{20,214},{24,218},{28,22... | collective-permute-start | bytes 786440 | tf_op jit(solution)/shard_map/ppermute | solution.py:385
  16.3 23.1 %copy-start.11 = (f32[32,4096]{1,0:T(8,128)S(1)}, f32[32,4096]{1,0:T(8,128)}, u32[]{:S(2)}) copy-start(f32[32,4096]{1,0:T(8,128)} %get-tuple-element.23) | copy-start | bytes 1572868
  16.3 27.7 %copy-start.10 = (f32[32,4096]{1,0:T(8,128)S(1)}, f32[32,4096]{1,0:T(8,128)}, u32[]{:S(2)}) copy-start(f32[32,4096]{1,0:T(8,128)} %get-tuple-element.27) | copy-start | bytes 1572868
  16.3 29.7 %copy-start.5 = (f32[32,4096]{1,0:T(8,128)S(1)}, f32[32,4096]{1,0:T(8,128)}, u32[]{:S(2)}) copy-start(f32[32,4096]{1,0:T(8,128)} %get-tuple-element.24) | copy-start | bytes 1572868
  16.3 17.5 %collective-permute-start.7 = (f32[32,4096]{1,0:T(8,128)}, f32[32,4096]{1,0:T(8,128)S(1)}, u32[]{:S(2)}, u32[]{:S(2)}) collective-permute-start(f32[32,4096]{1,0:T(8,128)} %get-tuple-element.29), channel_id=1, source_target_pairs={{0,60},{4,56},{8,52},{12,48},{16,44},{20,40},{24,36},{28,32},{32,2... | collective-permute-start | bytes 1572872 | tf_op jit(solution)/shard_map/ppermute | solution.py:385
  22.3 27.0 %copy-start.4 = (f32[32,4096]{1,0:T(8,128)S(1)}, f32[32,4096]{1,0:T(8,128)}, u32[]{:S(2)}) copy-start(f32[32,4096]{1,0:T(8,128)} %get-tuple-element.28) | copy-start | bytes 1572868
  22.3 23.7 %collective-permute-start.3 = (f32[32,4096]{1,0:T(8,128)S(1)}, f32[32,4096]{1,0:T(8,128)S(1)}, u32[]{:S(2)}, u32[]{:S(2)}) collective-permute-start(f32[32,4096]{1,0:T(8,128)S(1)} %pad_maximum_fusion), channel_id=1, source_target_pairs={{0,2},{4,6},{8,10},{12,14},{16,18},{20,22},{24,26},{28,30},{32,34}... | collective-permute-start | bytes 1572872 | tf_op jit(solution)/shard_map/ppermute | solution.py:385
  33.9 15.4 %collective-permute-start.9 = (f32[32,4096]{1,0:T(8,128)S(1)}, f32[32,4096]{1,0:T(8,128)S(1)}, u32[]{:S(2)}, u32[]{:S(2)}) collective-permute-start(f32[32,4096]{1,0:T(8,128)S(1)} %pad_maximum_fusion.1), channel_id=1, source_target_pairs={{0,194},{4,198},{8,202},{12,206},{16,210},{20,214},{24,218},{28,22... | collective-permute-start | bytes 1572872 | tf_op jit(solution)/shard_map/ppermute | solution.py:385
  39.4 17.3 %collective-permute-start = (f32[32,4096]{1,0:T(8,128)S(1)}, f32[32,4096]{1,0:T(8,128)S(1)}, u32[]{:S(2)}, u32[]{:S(2)}) collective-permute-start(f32[32,4096]{1,0:T(8,128)S(1)} %copy-done.11), channel_id=1, source_target_pairs={{0,60},{4,56},{8,52},{12,48},{16,44},{20,40},{24,36},{28,32},{32,1... | collective-permute-start | bytes 1572872 | tf_op jit(solution)/shard_map/ppermute | solution.py:385
  44.0 25.9 %collective-permute-start.6 = (f32[32,4096]{1,0:T(8,128)S(1)}, f32[32,4096]{1,0:T(8,128)S(1)}, u32[]{:S(2)}, u32[]{:S(2)}) collective-permute-start(f32[32,4096]{1,0:T(8,128)S(1)} %copy-done.10), channel_id=1, source_target_pairs={{0,60},{4,56},{8,52},{12,48},{16,44},{20,40},{24,36},{28,32},{32,2... | collective-permute-start | bytes 1572872 | tf_op jit(solution)/shard_map/ppermute | solution.py:385
  46.1 13.4 %collective-permute-start.4 = (f32[32,4096]{1,0:T(8,128)S(1)}, f32[32,4096]{1,0:T(8,128)S(1)}, u32[]{:S(2)}, u32[]{:S(2)}) collective-permute-start(f32[32,4096]{1,0:T(8,128)S(1)} %add.32), channel_id=1, source_target_pairs={{0,2},{4,6},{8,10},{12,14},{16,18},{20,22},{24,26},{28,30},{32,34}... | collective-permute-start | bytes 1572872 | tf_op jit(solution)/shard_map/ppermute | solution.py:385
  49.4 20.6 %collective-permute-start.10 = (f32[32,4096]{1,0:T(8,128)S(1)}, f32[32,4096]{1,0:T(8,128)S(1)}, u32[]{:S(2)}, u32[]{:S(2)}) collective-permute-start(f32[32,4096]{1,0:T(8,128)S(1)} %add.35), channel_id=1, source_target_pairs={{0,194},{4,198},{8,202},{12,206},{16,210},{20,214},{24,218},{28,22... | collective-permute-start | bytes 1572872 | tf_op jit(solution)/shard_map/ppermute | solution.py:385
  59.6 19.9 %collective-permute-start.5 = (f32[32,4096]{1,0:T(8,128)S(1)}, f32[32,4096]{1,0:T(8,128)S(1)}, u32[]{:S(2)}, u32[]{:S(2)}) collective-permute-start(f32[32,4096]{1,0:T(8,128)S(1)} %add.33), channel_id=1, source_target_pairs={{0,2},{4,6},{8,10},{12,14},{16,18},{20,22},{24,26},{28,30},{32,34}... | collective-permute-start | bytes 1572872 | tf_op jit(solution)/shard_map/ppermute | solution.py:385
  70.0 13.1 %collective-permute-start.11 = (f32[32,4096]{1,0:T(8,128)S(1)}, f32[32,4096]{1,0:T(8,128)S(1)}, u32[]{:S(2)}, u32[]{:S(2)}) collective-permute-start(f32[32,4096]{1,0:T(8,128)S(1)} %add.36), channel_id=1, source_target_pairs={{0,194},{4,198},{8,202},{12,206},{16,210},{20,214},{24,218},{28,22... | collective-permute-start | bytes 1572872 | tf_op jit(solution)/shard_map/ppermute | solution.py:385
  79.5 3.5 %copy-start.6 = (f32[32,4096]{1,0:T(8,128)}, f32[32,4096]{1,0:T(8,128)S(1)}, u32[]{:S(2)}) copy-start(f32[32,4096]{1,0:T(8,128)S(1)} %collective-permute-done.5.up_ref) | copy-start | bytes 1572868
  83.1 0.8 copy-start.7
  90.8 87.3 %all-to-all-start = ((f32[128,48,128]{2,1,0:T(8,128)}), f32[128,48,128]{2,1,0:T(8,128)S(1)}, u32[]{:S(2)}, u32[]{:S(2)}) async-start(f32[128,48,128]{2,1,0:T(8,128)} %bitcast.16), calls=%async_computation | async-start | bytes 6291456 | tf_op jit(solution)/shard_map/all_to_all | solution.py:405
  178.1 1.6 copy-start
  185.6 10.2 %collective-permute-start.12 = (f32[6,2,256,128]{3,2,1,0:T(8,128)}, f32[6,2,256,128]{3,2,1,0:T(8,128)S(1)}, u32[]{:S(2)}, u32[]{:S(2)}) collective-permute-start(f32[6,2,256,128]{3,2,1,0:T(8,128)} %get-tuple-element.32), channel_id=1, source_target_pairs={{0,1},{1,0},{2,3},{3,2},{4,5},{5,4},{6,7},{7,6},{8,9},{9,8},{10,11... | collective-permute-start | bytes 4718600 | tf_op jit(solution)/shard_map/ppermute | solution.py:432
  190.9 3.9 %collective-permute-start.13 = (f32[64,128]{1,0:T(8,128)}, f32[64,128]{1,0:T(8,128)S(1)}, u32[]{:S(2)}, u32[]{:S(2)}) collective-permute-start(f32[64,128]{1,0:T(8,128)} %get-tuple-element.33), channel_id=1, source_target_pairs={{0,6},{1,7},{6,0},{7,1},{4,2},{5,3},{2,4},{3,5},{8,14},{9,15},{14,... | collective-permute-start | bytes 98312 | tf_op jit(solution)/shard_map/ppermute | solution.py:430
  190.9 4.9 %collective-permute-start.14 = (f32[64,128]{1,0:T(8,128)}, f32[64,128]{1,0:T(8,128)S(1)}, u32[]{:S(2)}, u32[]{:S(2)}) collective-permute-start(f32[64,128]{1,0:T(8,128)} %get-tuple-element.34), channel_id=1, source_target_pairs={{0,7},{1,6},{6,1},{7,0},{4,3},{5,2},{2,5},{3,4},{8,15},{9,14},{14,... | collective-permute-start | bytes 98312 | tf_op jit(solution)/shard_map/ppermute | solution.py:431
  194.8 1.1 copy-start.8
  195.8 0.6 copy-start.9
  195.8 1.2 copy-start.1
  201.5 11.9 %collective-permute-start.16 = (f32[6,256,128]{2,1,0:T(8,128)}, f32[6,256,128]{2,1,0:T(8,128)S(1)}, u32[]{:S(2)}, u32[]{:S(2)}) collective-permute-start(f32[6,256,128]{2,1,0:T(8,128)} %get-tuple-element.35.first_ref), channel_id=1, source_target_pairs={{0,253},{6,251},{1,0},{7,6},{4,1},{2,7},{5,4},{3,2},{8,5},{14,3},{... | collective-permute-start | bytes 2359304 | tf_op jit(solution)/shard_map/ppermute | solution.py:443
  201.9 11.6 %collective-permute-start.15 = (f32[6,256,128]{2,1,0:T(8,128)}, f32[6,256,128]{2,1,0:T(8,128)S(1)}, u32[]{:S(2)}, u32[]{:S(2)}) collective-permute-start(f32[6,256,128]{2,1,0:T(8,128)} %get-tuple-element.36.second_ref), channel_id=1, source_target_pairs={{0,1},{6,7},{1,4},{7,2},{4,5},{2,3},{5,8},{3,14},{8,9},{14,15},{9,... | collective-permute-start | bytes 2359304 | tf_op jit(solution)/shard_map/ppermute | solution.py:442
  213.5 0.9 copy-start.2
  213.5 1.2 copy-start.3
  219.2 12.9 %collective-permute-start.17 = (f32[2,256,128]{2,1,0:T(8,128)}, f32[2,256,128]{2,1,0:T(8,128)S(1)}, u32[]{:S(2)}, u32[]{:S(2)}) collective-permute-start(f32[2,256,128]{2,1,0:T(8,128)} %get-tuple-element.37), channel_id=1, source_target_pairs={{0,0},{1,2},{6,1},{7,3},{4,4},{5,6},{2,5},{3,7},{8,8},{9,10},{14,9... | collective-permute-start | bytes 786440 | tf_op jit(solution)/shard_map/ppermute | solution.py:456
  223.0 9.1 %collective-permute-start.18 = (f32[2,256,128]{2,1,0:T(8,128)}, f32[2,256,128]{2,1,0:T(8,128)S(1)}, u32[]{:S(2)}, u32[]{:S(2)}) collective-permute-start(f32[2,256,128]{2,1,0:T(8,128)} %get-tuple-element.38), channel_id=1, source_target_pairs={{0,1},{1,3},{6,0},{7,2},{4,5},{5,7},{2,4},{3,6},{8,9},{9,11},{14,8... | collective-permute-start | bytes 786440 | tf_op jit(solution)/shard_map/ppermute | solution.py:457

commit v4 on v3

--- a/solution.py
+++ b/solution.py
@@ -17,7 +17,7 @@
 GROUPS = 4
 SLABS = 32
 SENDERS = GROUPS * SLABS
-PER = BANDS * 8
+PER = BANDS * 4
 LANES = 128
 error_floor = 1.0
 bf16 = jnp.bfloat16
@@ -171,7 +171,8 @@
     kx = ((kx + HALF) & (BOX - 1)) - HALF
     kz = ((kz_ref[0] + HALF) & (BOX - 1)) - HALF
     radius[...] = (ky * ky + kx * kx + kz * kz).astype(f32)
-    upper = lax.broadcasted_iota(jnp.int32, (BLOCKS, 8, LANES), 1) < 4
+    place_in = lax.broadcasted_iota(jnp.int32, (BLOCKS, 8, LANES), 1)
+    upper, even_unit = place_in < 4, (place_in & 2) == 0
 
     @pl.loop(0, BANDS // 2)
     def _(pair):
@@ -199,104 +200,112 @@
                 low = beside(real[1][:, few], imag[1][:, few])
                 mids[odd].append(beside(high, low, high))
         parts = [dot(above(*mids[odd]), above(x_ref[odd, 0], x_ref[odd, 0], x_ref[odd, 1])) for odd in range(2)]
-        for i in range(2):
-            b = pair * 2 + i
-            value = jnp.where(cut_ref[b] >= HALF, last, 0.0)
-            first, second = parts[0][i * BOX : (i + 1) * BOX], parts[1][i * BOX : (i + 1) * BOX]
-            for side, full in enumerate((first + second, first - second)):
+        for side in range(2):
+            units = []
+            for i in range(2):
+                value = jnp.where(cut_ref[pair * 2 + i] >= HALF, last, 0.0)
+                first, second = parts[0][i * BOX : (i + 1) * BOX], parts[1][i * BOX : (i + 1) * BOX]
+                full = first - second if side else first + second
                 even, odd = full[:, :LANES], full[:, LANES:]
                 odd = jnp.where(alone, jnp.broadcast_to(value, odd.shape), odd)
-                even, odd = even.reshape(BLOCKS, 8, LANES), odd.reshape(BLOCKS, 8, LANES)
-                out_ref[:, 3 * side, b] = jnp.where(upper, even, pltpu.roll(odd, 4, 1))
-                out_ref[:, 2 - side, b] = jnp.where(upper, pltpu.roll(even, 4, 1), odd)
-
-
-def depth_kernel(core_ref, come_ref, z_ref, own_ref, other_ref, own_edge_ref, other_edge_ref, own_edge, other_edge):
+                units += [even.reshape(BLOCKS, 8, LANES), odd.reshape(BLOCKS, 8, LANES)]
+            for odd_block in range(2):
+                if odd_block:
+                    halves = [jnp.where(upper, pltpu.roll(units[q], 4, 1), units[q + 2]) for q in range(2)]
+                else:
+                    halves = [jnp.where(upper, units[q], pltpu.roll(units[q + 2], 4, 1)) for q in range(2)]
+                goal = 2 * (2 * (odd_block ^ side) + side)
+                out_ref[:, goal, pair] = jnp.where(even_unit, halves[0], pltpu.roll(halves[1], 2, 1))
+                out_ref[:, goal + 1, pair] = jnp.where(even_unit, pltpu.roll(halves[0], 6, 1), halves[1])
+
+
+def depth_kernel(come_ref, z_ref, low_half_ref, high_half_ref, first_ref, second_ref, edge_ref, edge):
+    pair = pl.program_id(0)
+    lane = lax.broadcasted_iota(jnp.int32, (BOX, LANES), 1)
+    turn = beside(z_ref[0], z_ref[1], z_ref[0])
+    found = jnp.where(pair == 0, 0.0, edge[...])
+    for i in range(2):
+        maps = []
+        for half in range(2):
+            start = half * PER + pair * 8 + i * 4
+            sides = [
+                beside(*[come_ref[pl.ds(start + c * 2 + j, SENDERS, stride=2 * PER), :] for j in range(2)])
+                for c in range(2)
+            ]
+            high, low = two(above(*sides))
+            maps.append(dot(turn, above(high, high, low)))
+        gap = maps[0] - maps[1]
+        gap = gap * gap
+        for row in range(2):
+            cols = slice(row * LANES, (row + 1) * LANES)
+            low_half_ref[i, row] = maps[0][:, cols]
+            high_half_ref[i, row] = maps[1][:, cols]
+            part = gap[:, cols]
+            (first_ref, second_ref)[row][i] = part
+            spot = (pair * 2 + i) * 4 + row * 2
+            found = jnp.where((lane >> 1) == (spot >> 1), pltpu.roll(part, spot + 1, 1), found)
+    edge[...] = found
+
+    @pl.when(pair == BANDS // 2 - 1)
+    def _():
+        narrow = lax.broadcasted_iota(jnp.int32, (64, LANES), 1)
+        packed = edge[0:64, :]
+        for q in range(1, 4):
+            packed = jnp.where((narrow >> 5) == q, pltpu.roll(edge[q * 64 : (q + 1) * 64, :], q * 32, 1), packed)
+        edge_ref[...] = packed
+
+
+def blend_kernel(
+    side_ref,
+    low_half_ref,
+    high_half_ref,
+    first_ref,
+    second_ref,
+    before_ref,
+    after_ref,
+    edge_ref,
+    edge_before_ref,
+    edge_after_ref,
+    out_a_ref,
+    out_b_ref,
+    sums,
+    border,
+):
     step = pl.program_id(0)
     lane = lax.broadcasted_iota(jnp.int32, (BOX, LANES), 1)
-    turn = jnp.concatenate([z_ref[0], z_ref[1], z_ref[0]], axis=1)
-    for out_ref, edge, core in (
-        (own_ref, own_edge, core_ref[0]),
-        (other_ref, other_edge, 1 - core_ref[0]),
-    ):
-        found = jnp.where(step == 0, 0.0, edge[...])
-        for i in range(PACE):
-            start = (step * PACE + i) * 8 + core * 2
-            sides = [
-                jnp.concatenate(
-                    [come_ref[pl.ds(start + c * 4 + j, SENDERS, stride=PER), :] for j in range(2)], axis=1
-                )
-                for c in range(2)
-            ]
-            high, low = two(jnp.concatenate(sides, axis=0))
-            full = dot(turn, jnp.concatenate([high, high, low], axis=0))
-            for row in range(2):
-                part = full[:, row * LANES : (row + 1) * LANES]
-                out_ref[i, row] = part
-                spot = (step * PACE + i) * 4 + row * 2
-                found = jnp.where((lane >> 1) == (spot >> 1), pltpu.roll(part, spot + 1, 1), found)
-        edge[...] = found
-
-    @pl.when(step == BANDS // PACE - 1)
-    def _():
-        narrow = lax.broadcasted_iota(jnp.int32, (64, LANES), 1)
-        for out_ref, edge in ((own_edge_ref, own_edge), (other_edge_ref, other_edge)):
-            packed = edge[0:64, :]
-            for q in range(1, 4):
-                packed = jnp.where((narrow >> 5) == q, pltpu.roll(edge[q * 64 : (q + 1) * 64, :], q * 32, 1), packed)
-            out_ref[...] = packed
-
-
-def square_kernel(own_ref, other_ref, own_edge_ref, other_edge_ref, first_ref, second_ref, border):
-    step = pl.program_id(0)
-    lane = lax.broadcasted_iota(jnp.int32, (BOX, LANES), 1)
-
-    @pl.when(step == 0)
-    def _():
-        gap = own_edge_ref[...] - other_edge_ref[...]
-        gap = gap * gap
-        for q in range(4):
-            border[q * 64 : (q + 1) * 64, :] = pltpu.roll(gap, (LANES - q * 32) % LANES, 1)
-
-    for i in range(PACE):
-        for row, ref in enumerate((first_ref, second_ref)):
-            gap = own_ref[i, row] - other_ref[i, row]
-            square = gap * gap
-            spot = (step * PACE + i) * 4 + row * 2
-            beyond = pltpu.roll(border[...], LANES - 1 - spot, 1)
-            left = pltpu.roll(jnp.where(lane == LANES - 1, beyond, square), 1, 1)
-            right = pltpu.roll(jnp.where(lane == 0, beyond, square), LANES - 1, 1)
-            ref[i] = square + left + right
-
-
-def blend_kernel(
-    swap_ref, own_ref, other_ref, first_ref, second_ref, before_ref, after_ref, out_a_ref, out_b_ref, sums
-):
-    step = pl.program_id(0)
 
     @pl.when(step == 0)
     def _():
         sums[...] = jnp.zeros_like(sums)
+        here = edge_ref[...]
+        here = here + pltpu.roll(here, LANES - 2, 1)
+        for row, packed in enumerate((here + pltpu.roll(edge_before_ref[...], LANES - 2, 1), here + edge_after_ref[...])):
+            for q in range(4):
+                border[row, q * 64 : (q + 1) * 64, :] = pltpu.roll(packed, (LANES - q * 32) % LANES, 1)
 
     for row in range(2):
-        mine, theirs, total = sums[row, 0], sums[row, 1], sums[row, 2]
+        low, high, total = sums[row, 0], sums[row, 1], sums[row, 2]
         for i in range(PACE):
-            wide = first_ref[i] + second_ref[i] + (before_ref if row == 0 else after_ref)[i]
+            tall = first_ref[i] + second_ref[i] + (after_ref if row else before_ref)[i]
+            beyond = pltpu.roll(border[row], LANES - 1 - (step * PACE + i) * 4, 1)
+            left = pltpu.roll(jnp.where(lane == LANES - 1, beyond, tall), 1, 1)
+            right = pltpu.roll(jnp.where(lane == 0, beyond, tall), LANES - 1, 1)
+            wide = tall + left + right
             full = wide + pltpu.roll(wide, 1, 0) + pltpu.roll(wide, BOX - 1, 0)
             weight = 1.0 / (full / 27.0 + error_floor)
-            mine = mine + weight * own_ref[i, row]
-            theirs = theirs + weight * other_ref[i, row]
+            low = low + weight * low_half_ref[i, row]
+            high = high + weight * high_half_ref[i, row]
             total = total + weight
-        sums[row, 0], sums[row, 1], sums[row, 2] = mine, theirs, total
+        sums[row, 0], sums[row, 1], sums[row, 2] = low, high, total
 
     @pl.when(step == BANDS // PACE - 1)
     def _():
-        swap = swap_ref[0] == 1
+        swap = side_ref[0] == 1
         for row in range(2):
-            mine = sums[row, 0] / sums[row, 2]
-            theirs = sums[row, 1] / sums[row, 2]
-            out_a_ref[row] = jnp.where(swap, theirs, mine)
-            out_b_ref[row] = jnp.where(swap, mine, theirs)
+            low = sums[row, 0] / sums[row, 2]
+            high = sums[row, 1] / sums[row, 2]
+            out_a_ref[row] = jnp.where(swap, high, low)
+            out_b_ref[row] = jnp.where(swap, low, high)
 
 
 def chip(depth, spot):
@@ -322,21 +331,12 @@
     return (2 * (block ^ side) + side) * 2 + core
 
 
-def row_pairs(step):
+def row_pairs(step, flip):
     pairs = []
     for n in range(SENDERS):
         goal = (n + step) % SENDERS
-        pairs += [(holder(n // 2, side, n % 2), holder(goal // 2, side, goal % 2)) for side in range(2)]
+        pairs += [(holder(n // 2, side, n % 2), holder(goal // 2, side ^ flip, goal % 2)) for side in range(2)]
     return pairs
-
-
-def edge_pairs(flip):
-    return [
-        (holder(block, side, core), holder(block, 1 - side, core ^ flip))
-        for block in range(64)
-        for side in range(2)
-        for core in range(2)
-    ]
 
 
 def home_pairs(flip):
@@ -396,15 +396,15 @@
     constants = [jnp.asarray(t) for t in tables()]
     sent = pl.pallas_call(
         planes_kernel,
-        out_shape=jax.ShapeDtypeStruct((SENDERS // 4, 4, BANDS, 8, LANES), f32),
+        out_shape=jax.ShapeDtypeStruct((SENDERS // 4, 8, BANDS // 2, 8, LANES), f32),
         in_specs=[SMEM, SMEM] + [VMEM] * 5,
         out_specs=VMEM,
         scratch_shapes=[pltpu.VMEM((2 * BOX, BOX), bf16)] * 2 + [pltpu.VMEM((BOX, BOX), f32)],
         name="planes",
     )(cutoffs, plane, own, rise, sink, *constants[:2])
     gathered = lax.all_to_all(
-        sent.reshape(SENDERS, PER, LANES), ("particle", "slab"), split_axis=0, concat_axis=0, tiled=True
-    ).reshape(SENDERS * PER, LANES)
+        sent.reshape(2 * SENDERS, PER, LANES), everyone, split_axis=0, concat_axis=0, tiled=True
+    ).reshape(2 * SENDERS * PER, LANES)
 
     steps = BANDS // PACE
     rows_spec = pl.BlockSpec((PACE, 2, BOX, LANES), lambda b: (b, 0, 0, 0))
@@ -412,47 +412,32 @@
     row_spec = pl.BlockSpec((PACE, BOX, LANES), lambda b: (b, 0, 0))
     row_shape = jax.ShapeDtypeStruct((BANDS, BOX, LANES), f32)
     edge_spec = pl.BlockSpec((64, LANES), lambda b: (0, 0))
-    edge_shape = jax.ShapeDtypeStruct((64, LANES), f32)
-    edge_room = pltpu.VMEM((BOX, LANES), f32)
-    own, leaving, own_edge, other_edge = pl.pallas_call(
+    low_half, high_half, first, second, edge = pl.pallas_call(
         depth_kernel,
-        grid=(steps,),
-        out_shape=(rows_shape, rows_shape, edge_shape, edge_shape),
+        grid=(BANDS // 2,),
+        out_shape=(rows_shape, rows_shape, row_shape, row_shape, jax.ShapeDtypeStruct((64, LANES), f32)),
         in_specs=[
-            SMEM,
-            pl.BlockSpec((SENDERS * PER, LANES), lambda b: (0, 0)),
+            pl.BlockSpec((2 * SENDERS * PER, LANES), lambda b: (0, 0)),
             pl.BlockSpec((2, BOX, BOX), lambda b: (0, 0, 0)),
         ],
-        out_specs=(rows_spec, rows_spec, edge_spec, edge_spec),
-        scratch_shapes=[edge_room, edge_room],
+        out_specs=(rows_spec, rows_spec, row_spec, row_spec, edge_spec),
+        scratch_shapes=[pltpu.VMEM((BOX, LANES), f32)],
         name="depth",
-    )(half_pos.reshape(1), gathered, constants[2])
-    own_edge = lax.ppermute(own_edge, everyone, edge_pairs(0))
-    other_edge = lax.ppermute(other_edge, everyone, edge_pairs(1))
-    other = lax.ppermute(leaving, "half", [(0, 1), (1, 0)])
-    first, second = pl.pallas_call(
-        square_kernel,
-        grid=(steps,),
-        out_shape=(row_shape, row_shape),
-        in_specs=[rows_spec, rows_spec, edge_spec, edge_spec],
-        out_specs=(row_spec, row_spec),
-        scratch_shapes=[edge_room],
-        name="square",
-    )(own, other, own_edge, other_edge)
-    before = lax.ppermute(second, everyone, row_pairs(1))
-    after = lax.ppermute(first, everyone, row_pairs(-1))
-    swap = (side_pos != half_pos).astype(jnp.int32).reshape(1)
+    )(gathered, constants[2])
+    before = lax.ppermute(second, everyone, row_pairs(1, 0))
+    after = lax.ppermute(first, everyone, row_pairs(-1, 0))
+    edges = [lax.ppermute(edge, everyone, row_pairs(n, 1)) for n in (0, 1, -1)]
     block_spec = pl.BlockSpec((2, BOX, LANES), lambda b: (0, 0, 0))
     block_shape = jax.ShapeDtypeStruct((2, BOX, LANES), f32)
     near, far = pl.pallas_call(
         blend_kernel,
         grid=(steps,),
         out_shape=(block_shape, block_shape),
-        in_specs=[SMEM, rows_spec, rows_spec] + [row_spec] * 4,
+        in_specs=[SMEM, rows_spec, rows_spec] + [row_spec] * 4 + [edge_spec] * 3,
         out_specs=(block_spec, block_spec),
-        scratch_shapes=[pltpu.VMEM((2, 3, BOX, LANES), f32)],
+        scratch_shapes=[pltpu.VMEM((2, 3, BOX, LANES), f32), pltpu.VMEM((2, BOX, LANES), f32)],
         name="blend",
-    )(swap, own, other, first, second, before, after)
+    )(side_pos.reshape(1), low_half, high_half, first, second, before, after, *edges)
     near = lax.ppermute(near, everyone, home_pairs(0))
     far = lax.ppermute(far, everyone, home_pairs(1))
     low = jnp.where(half_pos == 0, near, far)

time: 234 us -> 228 us (0.974)
  blocking collectives: 0 us -> 93.8 us
  waiting for transfers between devices: 141 us -> 67.7 us
  starting transfers between devices: 59.2 us -> 38 us
  local copies, waits for them, and re-layouts: 6.04 us -> 3.14 us
  Pallas kernels: 26.8 us -> 24 us
    all_to_all x0 -> x1, blocking collectives: none -> 93.8 us  [on_device(): lax.all_to_all(sent.reshape(2 * SENDERS, PER, LANES), everyone, split_axi...]
    all_to_all x1 -> x0, waiting for transfers between devices: 72.5 us -> none  [on_device(): lax.all_to_all(sent.reshape(SENDERS, PER, LANES), ('particle', 'slab'), s...]
    all_to_all x1 -> x0, starting transfers between devices: 14.8 us -> none  [on_device(): lax.all_to_all(sent.reshape(SENDERS, PER, LANES), ('particle', 'slab'), s...]
    ppermute x5, starting transfers between devices: 9.64 us -> 4.43 us  [the longest x3 2.68 us: on_device(): edges = [lax.ppermute(edge, everyone, row_pairs(n, 1)) for n in (0, 1, -1)]]
    pallas_call x2 -> x1, Pallas kernels: 10.4 us -> 6.15 us  [on_device(): pl.pallas_call(depth_kernel, grid=(BANDS // 2,), out_shape=(rows_shape, r...]
    ppermute x5, waiting for transfers between devices: 12.5 us -> 9.07 us  [the longest x3 9.07 us: on_device(): edges = [lax.ppermute(edge, everyone, row_pairs(n, 1)) for n in (0, 1, -1)]]
    unnamed x24 -> x22, local copies, waits for them, and re-layouts: 4.84 us -> 1.94 us
    ppermute x1, waiting for transfers between devices: 8.74 us -> 11.5 us  [on_device(): near = lax.ppermute(near, everyone, home_pairs(0))]
  transfers between devices with their start and end apart: 20 -> 19, of which waited for: 13 -> 10; matrix products, arithmetic and copies ran while one was open for 0% -> 0% of each run, Pallas kernels for 0% -> 0%
where the time goes in v4:
time: 228 us; the launch traced here: 227 us
  blocking collectives  93.8 us (41%)
  waiting for transfers between devices  67.7 us (30%)
  starting transfers between devices  38 us (17%)
  Pallas kernels  24 us (11%)
  local copies, waits for them, and re-layouts  3.14 us (1%)
    all_to_all x1, blocking collectives, on_device(): lax.all_to_all(sent.reshape(2 * SENDERS, PER, LANES), everyone, split_axi...  93.8 us
    ppermute x12, waiting for transfers between devices, send(): return lax.ppermute(part, here, pairs)  47.1 us
    ppermute x12, starting transfers between devices, send(): return lax.ppermute(part, here, pairs)  30.5 us
    ppermute x1, waiting for transfers between devices, on_device(): near = lax.ppermute(near, everyone, home_pairs(0))  11.5 us
    ppermute x3, waiting for transfers between devices, on_device(): edges = [lax.ppermute(edge, everyone, row_pairs(n, 1)) for n in (0, 1, -1)]  9.07 us
    pallas_call x1, Pallas kernels, on_device(): pl.pallas_call(planes_kernel, out_shape=jax.ShapeDtypeStruct((SENDERS //...  7.28 us
    pallas_call x1, Pallas kernels, on_device(): pl.pallas_call(depth_kernel, grid=(BANDS // 2,), out_shape=(rows_shape, r...  6.15 us
    pallas_call x1, Pallas kernels, on_device(): pl.pallas_call(blend_kernel, grid=(steps,), out_shape=(block_shape, block...  5.62 us
  transfers between devices with their start and end apart: 19, of which 10 were waited for; matrix products, arithmetic and copies ran while one was open for 0% of the time, Pallas kernels for 0%

profile of v4, /device:TPU:1, one launch (start us, length us, event | category | flops | bytes accessed | tf_op | source)
XLA Modules:
  0.0 227.3 jit_solution(8713302191949044226)
XLA Ops:
  0.0 4.9 %place.1 = (f32[32,4096]{1,0:T(8,128)}, f32[32,4096]{1,0:T(8,128)}, f32[16,4096]{1,0:T(8,128)}, f32[16,4096]{1,0:T(8,128)}, f32[32,4096]{1,0:T(8,128)}, /*index=...) custom-call(s32[1]{0:T(128)} %bitcast.2.slab_ref, s32[1]{0:T(128)} %bitcast.3.group_ref, ...), custom_call_target="tpu_custom_call" | custom-call | tf_op jit(solution)/shard_map/place/pallas_call | solution.py:362
  4.9 5.8 %collective-permute-start.1 = (f32[32,4096]{1,0:T(8,128)}, f32[32,4096]{1,0:T(8,128)S(1)}, u32[]{:S(2)}, u32[]{:S(2)}) collective-permute-start(f32[32,4096]{1,0:T(8,128)} %get-tuple-element.24), channel_id=1, source_target_pairs={{0,60},{4,56},{8,52},{12,48},{16,44},{20,40},{24,36},{28,32},{32,2... | collective-permute-start | bytes 1572872 | tf_op jit(solution)/shard_map/ppermute | solution.py:385
  10.7 1.6 collective-permute-start.2
  12.4 3.9 %collective-permute-start.8 = (f32[16,4096]{1,0:T(8,128)}, f32[16,4096]{1,0:T(8,128)S(1)}, u32[]{:S(2)}, u32[]{:S(2)}) collective-permute-start(f32[16,4096]{1,0:T(8,128)} %get-tuple-element.29), channel_id=1, source_target_pairs={{0,194},{4,198},{8,202},{12,206},{16,210},{20,214},{24,218},{28,22... | collective-permute-start | bytes 786440 | tf_op jit(solution)/shard_map/ppermute | solution.py:385
  16.3 0.0 copy-start.10
  16.3 0.2 collective-permute-start.7
  16.5 5.7 %collective-permute-done.2 = f32[16,4096]{1,0:T(8,128)S(1)} collective-permute-done((f32[16,4096]{1,0:T(8,128)}, f32[16,4096]{1,0:T(8,128)S(1)}, u32[]{:S(2)}, u32[]{:S(2)}) %collective-permute-start.2) | collective-permute-done | bytes 262176 | tf_op jit(solution)/shard_map/ppermute | solution.py:385
  22.2 0.0 collective-permute-done.1
  22.3 0.0 copy-start.2
  22.4 1.9 collective-permute-start.3
  24.3 0.0 collective-permute-done.8
  24.3 9.5 %collective-permute-done.7 = f32[32,4096]{1,0:T(8,128)S(1)} collective-permute-done((f32[32,4096]{1,0:T(8,128)}, f32[32,4096]{1,0:T(8,128)S(1)}, u32[]{:S(2)}, u32[]{:S(2)}) %collective-permute-start.7) | collective-permute-done | bytes 524320 | tf_op jit(solution)/shard_map/ppermute | solution.py:385
  33.9 5.5 %collective-permute-start.9 = (f32[32,4096]{1,0:T(8,128)S(1)}, f32[32,4096]{1,0:T(8,128)S(1)}, u32[]{:S(2)}, u32[]{:S(2)}) collective-permute-start(f32[32,4096]{1,0:T(8,128)S(1)} %pad_maximum_fusion.1), channel_id=1, source_target_pairs={{0,194},{4,198},{8,202},{12,206},{16,210},{20,214},{24,218},{28,22... | collective-permute-start | bytes 1572872 | tf_op jit(solution)/shard_map/ppermute | solution.py:385
  39.4 0.0 copy-done.10
  39.4 4.6 %collective-permute-start = (f32[32,4096]{1,0:T(8,128)S(1)}, f32[32,4096]{1,0:T(8,128)S(1)}, u32[]{:S(2)}, u32[]{:S(2)}) collective-permute-start(f32[32,4096]{1,0:T(8,128)S(1)} %copy-done.10), channel_id=1, source_target_pairs={{0,60},{4,56},{8,52},{12,48},{16,44},{20,40},{24,36},{28,32},{32,1... | collective-permute-start | bytes 1572872 | tf_op jit(solution)/shard_map/ppermute | solution.py:385
  44.1 0.0 copy-done.9
  44.1 1.9 collective-permute-start.6
  46.0 0.0 collective-permute-done.3
  46.0 0.0 copy-done.3
  46.0 0.1 add.32
  46.1 0.1 collective-permute-start.4
  46.2 3.1 %collective-permute-done.9 = f32[32,4096]{1,0:T(8,128)S(1)} collective-permute-done((f32[32,4096]{1,0:T(8,128)S(1)}, f32[32,4096]{1,0:T(8,128)S(1)}, u32[]{:S(2)}, u32[]{:S(2)}) %collective-permute-start.9) | collective-permute-done | bytes 524320 | tf_op jit(solution)/shard_map/ppermute | solution.py:385
  49.3 0.0 copy-done.2
  49.3 0.1 add.35
  49.4 3.5 %collective-permute-start.10 = (f32[32,4096]{1,0:T(8,128)S(1)}, f32[32,4096]{1,0:T(8,128)S(1)}, u32[]{:S(2)}, u32[]{:S(2)}) collective-permute-start(f32[32,4096]{1,0:T(8,128)S(1)} %add.35), channel_id=1, source_target_pairs={{0,194},{4,198},{8,202},{12,206},{16,210},{20,214},{24,218},{28,22... | collective-permute-start | bytes 1572872 | tf_op jit(solution)/shard_map/ppermute | solution.py:385
  52.9 3.8 %collective-permute-done = f32[32,4096]{1,0:T(8,128)S(1)} collective-permute-done((f32[32,4096]{1,0:T(8,128)S(1)}, f32[32,4096]{1,0:T(8,128)S(1)}, u32[]{:S(2)}, u32[]{:S(2)}) %collective-permute-start) | collective-permute-done | bytes 524320 | tf_op jit(solution)/shard_map/ppermute | solution.py:385
  56.7 2.8 %collective-permute-done.4 = f32[32,4096]{1,0:T(8,128)S(1)} collective-permute-done((f32[32,4096]{1,0:T(8,128)S(1)}, f32[32,4096]{1,0:T(8,128)S(1)}, u32[]{:S(2)}, u32[]{:S(2)}) %collective-permute-start.4) | collective-permute-done | bytes 524320 | tf_op jit(solution)/shard_map/ppermute | solution.py:385
  59.5 0.1 add.33
  59.6 0.1 collective-permute-start.5
  59.7 10.3 %collective-permute-done.6 = f32[32,4096]{1,0:T(8,128)S(1)} collective-permute-done((f32[32,4096]{1,0:T(8,128)S(1)}, f32[32,4096]{1,0:T(8,128)S(1)}, u32[]{:S(2)}, u32[]{:S(2)}) %collective-permute-start.6) | collective-permute-done | bytes 524320 | tf_op jit(solution)/shard_map/ppermute | solution.py:385
  69.9 0.0 collective-permute-done.10
  69.9 0.1 add.36
  70.0 1.3 collective-permute-start.11
  71.3 8.2 %collective-permute-done.5.up_ref = f32[32,4096]{1,0:T(8,128)S(1)} collective-permute-done((f32[32,4096]{1,0:T(8,128)S(1)}, f32[32,4096]{1,0:T(8,128)S(1)}, u32[]{:S(2)}, u32[]{:S(2)}) %collective-permute-start.5) | collective-permute-done | bytes 524320 | tf_op jit(solution)/shard_map/ppermute | solution.py:385
  79.5 3.5 %collective-permute-done.11.down_ref = f32[32,4096]{1,0:T(8,128)S(1)} collective-permute-done((f32[32,4096]{1,0:T(8,128)S(1)}, f32[32,4096]{1,0:T(8,128)S(1)}, u32[]{:S(2)}, u32[]{:S(2)}) %collective-permute-start.11) | collective-permute-done | bytes 524320 | tf_op jit(solution)/shard_map/ppermute | solution.py:385
  83.1 0.0 copy-done.4
  83.1 0.8 copy-done.5
  83.9 7.3 %planes.1 = f32[32,8,3,8,128]{4,3,2,1,0:T(8,128)} custom-call(s32[6]{0:T(128)} %cut_ref.1, s32[1]{0:T(128)} %bitcast.1.kz_ref, f32[32,4096]{1,0:T(8,128)} %get-tuple-element.21.own_ref, f32[32,4096]{1,0:T(8,128)} %copy-done.4, f32[32,4096]{1,0:T(8,128)} %copy-done.5, bf16[2,2,256,256]{3,2,1,0:T(8,128)(2,1)} %constant.38.clone.y_ref, ...), custom_call_target="tpu_custom_call" | custom-call | tf_op jit(solution)/shard_map/planes/pallas_call | solution.py:397
  91.1 93.8 %all_to_all.5 = f32[256,24,128]{2,1,0:T(8,128)} all-to-all(f32[256,24,128]{2,1,0:T(8,128)} %bitcast.15), channel_id=1, replica_groups=mesh['particle'=4,'slab'=32,'half'=2] {'particle','slab','half'}, dimensions={0} | all-to-all | bytes 6291456 | tf_op jit(solution)/shard_map/all_to_all | solution.py:405
  184.9 6.1 %depth.1 = (f32[6,2,256,128]{3,2,1,0:T(8,128)}, f32[6,2,256,128]{3,2,1,0:T(8,128)}, f32[6,256,128]{2,1,0:T(8,128)}, f32[6,256,128]{2,1,0:T(8,128)}, f32[64,128]{1,0:T(8,128)}) custom-call(f32[6144,128]{1,0:T(8,128)} %bitcast.14, bf16[2,256,256]{2,1,0:T(8,128)(2,1)} %constant.40.clone.z_ref), custom_call_target="tpu_custom_call" | custom-call | tf_op jit(solution)/shard_map/depth/pallas_call | solution.py:415
  191.1 0.0 collective-permute-start.13
  191.1 1.7 collective-permute-start.12
  192.8 0.0 collective-permute-start.16
  192.8 1.7 collective-permute-start.15
  194.6 0.9 collective-permute-start.14
  195.5 9.1 %collective-permute-done.16.edge_after_ref = f32[64,128]{1,0:T(8,128)S(1)} collective-permute-done((f32[64,128]{1,0:T(8,128)}, f32[64,128]{1,0:T(8,128)S(1)}, u32[]{:S(2)}, u32[]{:S(2)}) %collective-permute-start.16) | collective-permute-done | bytes 32800 | tf_op jit(solution)/shard_map/ppermute | solution.py:429
  204.6 0.0 collective-permute-done.15.edge_before_ref
  204.6 0.0 collective-permute-done.14.edge_ref
  204.6 0.0 copy-start.8
  204.6 0.0 collective-permute-done.13.after_ref
  204.6 0.0 copy-start
  204.6 0.0 collective-permute-done.12.before_ref
  204.6 0.0 copy-start.1
  204.6 0.5 copy-done.6
  205.2 0.0 copy-done.7
  205.2 0.0 copy-done.8
  205.2 0.3 copy-done
  205.5 0.2 copy-done.1
  205.7 5.6 %blend.1 = (f32[2,256,128]{2,1,0:T(8,128)}, f32[2,256,128]{2,1,0:T(8,128)}) custom-call(s32[1]{0:T(128)} %bitcast.side_ref, f32[6,2,256,128]{3,2,1,0:T(8,128)} %get-tuple-element.30.low_half_ref, f32[6,2,256,128]{3,2,1,0:T(8,128)} %get-tuple-element.31.high_half_ref, f32[6,256,128]{2,1,0:T(8,128)} %get-tuple-element.32.first_ref, ...), custom_call_target="tpu_custom_call" | custom-call | tf_op jit(solution)/shard_map/blend/pallas_call | solution.py:432
  211.4 3.0 %collective-permute-start.17 = (f32[2,256,128]{2,1,0:T(8,128)}, f32[2,256,128]{2,1,0:T(8,128)S(1)}, u32[]{:S(2)}, u32[]{:S(2)}) collective-permute-start(f32[2,256,128]{2,1,0:T(8,128)} %get-tuple-element.35), channel_id=1, source_target_pairs={{0,0},{1,2},{6,1},{7,3},{4,4},{5,6},{2,5},{3,7},{8,8},{9,10},{14,9... | collective-permute-start | bytes 786440 | tf_op jit(solution)/shard_map/ppermute | solution.py:441
  214.4 0.1 collective-permute-start.18
  214.5 11.5 %collective-permute-done.17 = f32[2,256,128]{2,1,0:T(8,128)S(1)} collective-permute-done((f32[2,256,128]{2,1,0:T(8,128)}, f32[2,256,128]{2,1,0:T(8,128)S(1)}, u32[]{:S(2)}, u32[]{:S(2)}) %collective-permute-start.17) | collective-permute-done | bytes 262176 | tf_op jit(solution)/shard_map/ppermute | solution.py:441
  226.0 0.0 collective-permute-done.18
  226.1 1.2 copy.9
  (12 shorter events, 0.2 us)
Async XLA Ops:
  4.9 17.3 %collective-permute-start.1 = (f32[32,4096]{1,0:T(8,128)}, f32[32,4096]{1,0:T(8,128)S(1)}, u32[]{:S(2)}, u32[]{:S(2)}) collective-permute-start(f32[32,4096]{1,0:T(8,128)} %get-tuple-element.24), channel_id=1, source_target_pairs={{0,60},{4,56},{8,52},{12,48},{16,44},{20,40},{24,36},{28,32},{32,2... | collective-permute-start | bytes 1572872 | tf_op jit(solution)/shard_map/ppermute | solution.py:385
  10.7 11.5 %collective-permute-start.2 = (f32[16,4096]{1,0:T(8,128)}, f32[16,4096]{1,0:T(8,128)S(1)}, u32[]{:S(2)}, u32[]{:S(2)}) collective-permute-start(f32[16,4096]{1,0:T(8,128)} %get-tuple-element.25), channel_id=1, source_target_pairs={{0,2},{4,6},{8,10},{12,14},{16,18},{20,22},{24,26},{28,30},{32,34}... | collective-permute-start | bytes 786440 | tf_op jit(solution)/shard_map/ppermute | solution.py:385
  12.4 11.9 %collective-permute-start.8 = (f32[16,4096]{1,0:T(8,128)}, f32[16,4096]{1,0:T(8,128)S(1)}, u32[]{:S(2)}, u32[]{:S(2)}) collective-permute-start(f32[16,4096]{1,0:T(8,128)} %get-tuple-element.29), channel_id=1, source_target_pairs={{0,194},{4,198},{8,202},{12,206},{16,210},{20,214},{24,218},{28,22... | collective-permute-start | bytes 786440 | tf_op jit(solution)/shard_map/ppermute | solution.py:385
  16.3 23.1 %copy-start.10 = (f32[32,4096]{1,0:T(8,128)S(1)}, f32[32,4096]{1,0:T(8,128)}, u32[]{:S(2)}) copy-start(f32[32,4096]{1,0:T(8,128)} %get-tuple-element.22) | copy-start | bytes 1572868
  16.3 27.7 %copy-start.9 = (f32[32,4096]{1,0:T(8,128)S(1)}, f32[32,4096]{1,0:T(8,128)}, u32[]{:S(2)}) copy-start(f32[32,4096]{1,0:T(8,128)} %get-tuple-element.26) | copy-start | bytes 1572868
  16.3 29.7 %copy-start.3 = (f32[32,4096]{1,0:T(8,128)S(1)}, f32[32,4096]{1,0:T(8,128)}, u32[]{:S(2)}) copy-start(f32[32,4096]{1,0:T(8,128)} %get-tuple-element.23) | copy-start | bytes 1572868
  16.3 17.5 %collective-permute-start.7 = (f32[32,4096]{1,0:T(8,128)}, f32[32,4096]{1,0:T(8,128)S(1)}, u32[]{:S(2)}, u32[]{:S(2)}) collective-permute-start(f32[32,4096]{1,0:T(8,128)} %get-tuple-element.28), channel_id=1, source_target_pairs={{0,60},{4,56},{8,52},{12,48},{16,44},{20,40},{24,36},{28,32},{32,2... | collective-permute-start | bytes 1572872 | tf_op jit(solution)/shard_map/ppermute | solution.py:385
  22.3 27.0 %copy-start.2 = (f32[32,4096]{1,0:T(8,128)S(1)}, f32[32,4096]{1,0:T(8,128)}, u32[]{:S(2)}) copy-start(f32[32,4096]{1,0:T(8,128)} %get-tuple-element.27) | copy-start | bytes 1572868
  22.4 23.7 %collective-permute-start.3 = (f32[32,4096]{1,0:T(8,128)S(1)}, f32[32,4096]{1,0:T(8,128)S(1)}, u32[]{:S(2)}, u32[]{:S(2)}) collective-permute-start(f32[32,4096]{1,0:T(8,128)S(1)} %pad_maximum_fusion), channel_id=1, source_target_pairs={{0,2},{4,6},{8,10},{12,14},{16,18},{20,22},{24,26},{28,30},{32,34}... | collective-permute-start | bytes 1572872 | tf_op jit(solution)/shard_map/ppermute | solution.py:385
  33.9 15.4 %collective-permute-start.9 = (f32[32,4096]{1,0:T(8,128)S(1)}, f32[32,4096]{1,0:T(8,128)S(1)}, u32[]{:S(2)}, u32[]{:S(2)}) collective-permute-start(f32[32,4096]{1,0:T(8,128)S(1)} %pad_maximum_fusion.1), channel_id=1, source_target_pairs={{0,194},{4,198},{8,202},{12,206},{16,210},{20,214},{24,218},{28,22... | collective-permute-start | bytes 1572872 | tf_op jit(solution)/shard_map/ppermute | solution.py:385
  39.4 17.3 %collective-permute-start = (f32[32,4096]{1,0:T(8,128)S(1)}, f32[32,4096]{1,0:T(8,128)S(1)}, u32[]{:S(2)}, u32[]{:S(2)}) collective-permute-start(f32[32,4096]{1,0:T(8,128)S(1)} %copy-done.10), channel_id=1, source_target_pairs={{0,60},{4,56},{8,52},{12,48},{16,44},{20,40},{24,36},{28,32},{32,1... | collective-permute-start | bytes 1572872 | tf_op jit(solution)/shard_map/ppermute | solution.py:385
  44.1 25.9 %collective-permute-start.6 = (f32[32,4096]{1,0:T(8,128)S(1)}, f32[32,4096]{1,0:T(8,128)S(1)}, u32[]{:S(2)}, u32[]{:S(2)}) collective-permute-start(f32[32,4096]{1,0:T(8,128)S(1)} %copy-done.9), channel_id=1, source_target_pairs={{0,60},{4,56},{8,52},{12,48},{16,44},{20,40},{24,36},{28,32},{32,2... | collective-permute-start | bytes 1572872 | tf_op jit(solution)/shard_map/ppermute | solution.py:385
  46.1 13.4 %collective-permute-start.4 = (f32[32,4096]{1,0:T(8,128)S(1)}, f32[32,4096]{1,0:T(8,128)S(1)}, u32[]{:S(2)}, u32[]{:S(2)}) collective-permute-start(f32[32,4096]{1,0:T(8,128)S(1)} %add.32), channel_id=1, source_target_pairs={{0,2},{4,6},{8,10},{12,14},{16,18},{20,22},{24,26},{28,30},{32,34}... | collective-permute-start | bytes 1572872 | tf_op jit(solution)/shard_map/ppermute | solution.py:385
  49.4 20.6 %collective-permute-start.10 = (f32[32,4096]{1,0:T(8,128)S(1)}, f32[32,4096]{1,0:T(8,128)S(1)}, u32[]{:S(2)}, u32[]{:S(2)}) collective-permute-start(f32[32,4096]{1,0:T(8,128)S(1)} %add.35), channel_id=1, source_target_pairs={{0,194},{4,198},{8,202},{12,206},{16,210},{20,214},{24,218},{28,22... | collective-permute-start | bytes 1572872 | tf_op jit(solution)/shard_map/ppermute | solution.py:385
  59.6 19.9 %collective-permute-start.5 = (f32[32,4096]{1,0:T(8,128)S(1)}, f32[32,4096]{1,0:T(8,128)S(1)}, u32[]{:S(2)}, u32[]{:S(2)}) collective-permute-start(f32[32,4096]{1,0:T(8,128)S(1)} %add.33), channel_id=1, source_target_pairs={{0,2},{4,6},{8,10},{12,14},{16,18},{20,22},{24,26},{28,30},{32,34}... | collective-permute-start | bytes 1572872 | tf_op jit(solution)/shard_map/ppermute | solution.py:385
  70.0 13.1 %collective-permute-start.11 = (f32[32,4096]{1,0:T(8,128)S(1)}, f32[32,4096]{1,0:T(8,128)S(1)}, u32[]{:S(2)}, u32[]{:S(2)}) collective-permute-start(f32[32,4096]{1,0:T(8,128)S(1)} %add.36), channel_id=1, source_target_pairs={{0,194},{4,198},{8,202},{12,206},{16,210},{20,214},{24,218},{28,22... | collective-permute-start | bytes 1572872 | tf_op jit(solution)/shard_map/ppermute | solution.py:385
  79.5 3.5 %copy-start.4 = (f32[32,4096]{1,0:T(8,128)}, f32[32,4096]{1,0:T(8,128)S(1)}, u32[]{:S(2)}) copy-start(f32[32,4096]{1,0:T(8,128)S(1)} %collective-permute-done.5.up_ref) | copy-start | bytes 1572868
  83.1 0.8 copy-start.5
  191.1 13.5 %collective-permute-start.13 = (f32[6,256,128]{2,1,0:T(8,128)}, f32[6,256,128]{2,1,0:T(8,128)S(1)}, u32[]{:S(2)}, u32[]{:S(2)}) collective-permute-start(f32[6,256,128]{2,1,0:T(8,128)} %get-tuple-element.32.first_ref), channel_id=1, source_target_pairs={{0,253},{6,251},{1,0},{7,6},{4,1},{2,7},{5,4},{3,2},{8,5},{14,3},{... | collective-permute-start | bytes 2359304 | tf_op jit(solution)/shard_map/ppermute | solution.py:428
  191.1 13.5 %collective-permute-start.12 = (f32[6,256,128]{2,1,0:T(8,128)}, f32[6,256,128]{2,1,0:T(8,128)S(1)}, u32[]{:S(2)}, u32[]{:S(2)}) collective-permute-start(f32[6,256,128]{2,1,0:T(8,128)} %get-tuple-element.33.second_ref), channel_id=1, source_target_pairs={{0,1},{6,7},{1,4},{7,2},{4,5},{2,3},{5,8},{3,14},{8,9},{14,15},{9,... | collective-permute-start | bytes 2359304 | tf_op jit(solution)/shard_map/ppermute | solution.py:427
  192.8 11.7 %collective-permute-start.16 = (f32[64,128]{1,0:T(8,128)}, f32[64,128]{1,0:T(8,128)S(1)}, u32[]{:S(2)}, u32[]{:S(2)}) collective-permute-start(f32[64,128]{1,0:T(8,128)} %get-tuple-element.34), channel_id=1, source_target_pairs={{0,251},{6,253},{1,6},{7,0},{4,7},{2,1},{5,2},{3,4},{8,3},{14,5},{... | collective-permute-start | bytes 98312 | tf_op jit(solution)/shard_map/ppermute | solution.py:429
  192.8 11.7 %collective-permute-start.15 = (f32[64,128]{1,0:T(8,128)}, f32[64,128]{1,0:T(8,128)S(1)}, u32[]{:S(2)}, u32[]{:S(2)}) collective-permute-start(f32[64,128]{1,0:T(8,128)} %get-tuple-element.34), channel_id=1, source_target_pairs={{0,7},{6,1},{1,2},{7,4},{4,3},{2,5},{5,14},{3,8},{8,15},{14,9},{9,... | collective-permute-start | bytes 98312 | tf_op jit(solution)/shard_map/ppermute | solution.py:429
  194.6 10.0 %collective-permute-start.14 = (f32[64,128]{1,0:T(8,128)}, f32[64,128]{1,0:T(8,128)S(1)}, u32[]{:S(2)}, u32[]{:S(2)}) collective-permute-start(f32[64,128]{1,0:T(8,128)} %get-tuple-element.34), channel_id=1, source_target_pairs={{0,6},{6,0},{1,7},{7,1},{4,2},{2,4},{5,3},{3,5},{8,14},{14,8},{9,1... | collective-permute-start | bytes 98312 | tf_op jit(solution)/shard_map/ppermute | solution.py:429
  204.6 0.6 copy-start.6
  204.6 0.6 copy-start.7
  204.6 0.6 copy-start.8
  204.6 0.9 copy-start
  204.6 1.1 copy-start.1
  211.4 14.7 %collective-permute-start.17 = (f32[2,256,128]{2,1,0:T(8,128)}, f32[2,256,128]{2,1,0:T(8,128)S(1)}, u32[]{:S(2)}, u32[]{:S(2)}) collective-permute-start(f32[2,256,128]{2,1,0:T(8,128)} %get-tuple-element.35), channel_id=1, source_target_pairs={{0,0},{1,2},{6,1},{7,3},{4,4},{5,6},{2,5},{3,7},{8,8},{9,10},{14,9... | collective-permute-start | bytes 786440 | tf_op jit(solution)/shard_map/ppermute | solution.py:441
  214.4 11.7 %collective-permute-start.18 = (f32[2,256,128]{2,1,0:T(8,128)}, f32[2,256,128]{2,1,0:T(8,128)S(1)}, u32[]{:S(2)}, u32[]{:S(2)}) collective-permute-start(f32[2,256,128]{2,1,0:T(8,128)} %get-tuple-element.36), channel_id=1, source_target_pairs={{0,1},{1,3},{6,0},{7,2},{4,5},{5,7},{2,4},{3,6},{8,9},{9,11},{14,8... | collective-permute-start | bytes 786440 | tf_op jit(solution)/shard_map/ppermute | solution.py:442

commit v5 on v4

--- a/solution.py
+++ b/solution.py
@@ -50,10 +50,10 @@
     along_y, along_x = np.stack(along_y), np.stack(along_x)
     sender = np.arange(SENDERS)
     group, slab = sender // SLABS, sender % SLABS
-    plane = slab * 8 + group * 2 + (slab >= SLABS // 2)
+    plane = (slab ^ 1) * 8 + group * 2 + (slab >= SLABS // 2)
     turn = angles(places, plane)
     even, odd = np.cos(turn), -np.sin(turn)
-    odd[:, 0] = np.cos(math.pi * places)
+    odd[:, plane == 0] = np.cos(math.pi * places)[:, None]
     along_z = np.stack(split(np.concatenate([even, odd], axis=1) / BOX))
     return along_y, along_x, along_z
 
@@ -78,8 +78,8 @@
     depth, late = group * 2 + slab % 2, slab // (SLABS // 2)
     row = lax.broadcasted_iota(jnp.int32, (BLOCKS, BOX), 0)
     col = lax.broadcasted_iota(jnp.int32, (BLOCKS, BOX), 1)
-    own_line = [((depth + d) & 7) // 2 for d in (0, 2, 4, 6)]
-    sent_line = [((depth + d) & 7) // 2 for d in (3, 5, 1, 7)]
+    own_line = [((depth + d) & 7) // 2 for d in (3, 5, 1, 7)]
+    sent_line = [((depth + d) & 7) // 2 for d in (4, 2, 6, 0)]
 
     @pl.when(step == 0)
     def _():
@@ -140,7 +140,7 @@
             if r == 0:
                 alone = jnp.where(first & (step == 1), last_sent[i * BLOCKS : (i + 1) * BLOCKS], 0.0)
             parts.append(jnp.where((slab == SLABS // 2) & (sent_line[i] == 0), alone, part))
-        parts[2:3] = [parts[2][: BLOCKS // 2], parts[2][BLOCKS // 2 :]]
+        parts[4:5] = [parts[4][: BLOCKS // 2], parts[4][BLOCKS // 2 :]]
         for out_ref, part in zip(outs, parts):
             out_ref[:, cols] = part
 
@@ -318,7 +318,7 @@
         for spot in range(16):
             goal = (depth, 15 - spot)
             if spot >= 8 and (depth + ahead) % 8 // 2 == 0:
-                goal = ((depth + 1) % 8, 15 - spot) if depth % 2 else ((depth - 1) % 8, (16 - spot) % 8)
+                goal = (depth ^ 1, 15 - spot if depth % 2 else (16 - spot) % 8)
             pairs.append((chip(depth, spot), chip(*goal)))
     return pairs
 
@@ -358,8 +358,8 @@
     _, particles, touched, _ = tiles.shape
     entries = particles * touched
     late = (slab_pos >= SLABS // 2).astype(jnp.int32)
-    heights = [BLOCKS, BLOCKS, BLOCKS // 2, BLOCKS // 2] + [BLOCKS] * 5
-    own, ahead, far_a, far_b, behind, *sent = pl.pallas_call(
+    heights = [BLOCKS] * 4 + [BLOCKS // 2] * 2 + [BLOCKS] * 3
+    *own, far_a, far_b, ahead, behind, home = pl.pallas_call(
         place_kernel,
         grid=(2,),
         out_shape=tuple(jax.ShapeDtypeStruct((h, tile_width), f32) for h in heights),
@@ -384,14 +384,18 @@
     def send(part, pairs):
         return lax.ppermute(part, here, pairs)
 
-    come = [send(sent[i], mirror_pairs(e)) for i, e in enumerate((3, -3, 1, -1))]
-    rise, sink = send(far_a, up), send(far_b, down)
-    rise = jnp.concatenate([come[0][:cut] + rise, come[0][cut:]], axis=0)
-    sink = jnp.concatenate([come[1][:cut], come[1][cut:] + sink], axis=0)
+    rise = send(far_a, mirror_pairs(4))
+    sink = send(far_b, mirror_pairs(4))
+    ahead = send(ahead, mirror_pairs(2))
+    behind = send(behind, mirror_pairs(-2))
+    home = send(home, mirror_pairs(0))
+    rise, sink = send(rise, up), send(sink, down)
+    rise = jnp.concatenate([own[0][:cut] + rise, own[0][cut:]], axis=0)
+    sink = jnp.concatenate([own[1][:cut], own[1][cut:] + sink], axis=0)
     rise, sink = send(rise, up), send(sink, down)
     rise, sink = send(ahead + rise, up), send(behind + sink, down)
-    rise, sink = send(come[2] + rise, up), send(come[3] + sink, down)
-    plane = (slab_pos * 8 + group_pos * 2 + late).reshape(1)
+    rise, sink = send(own[2] + rise, up), send(own[3] + sink, down)
+    plane = ((slab_pos ^ 1) * 8 + group_pos * 2 + late).reshape(1)
 
     constants = [jnp.asarray(t) for t in tables()]
     sent = pl.pallas_call(
@@ -401,10 +405,10 @@
         out_specs=VMEM,
         scratch_shapes=[pltpu.VMEM((2 * BOX, BOX), bf16)] * 2 + [pltpu.VMEM((BOX, BOX), f32)],
         name="planes",
-    )(cutoffs, plane, own, rise, sink, *constants[:2])
-    gathered = lax.all_to_all(
-        sent.reshape(2 * SENDERS, PER, LANES), everyone, split_axis=0, concat_axis=0, tiled=True
-    ).reshape(2 * SENDERS * PER, LANES)
+    )(cutoffs, plane, home, rise, sink, *constants[:2])
+    gathered = lax.all_to_all(sent.reshape(2 * SENDERS, PER, LANES), everyone, split_axis=0, concat_axis=0, tiled=True)
+    gathered = gathered.reshape(2 * SENDERS * PER, LANES)
+    side_flag = jnp.where(jnp.arange(LANES, dtype=jnp.int32) == 0, side_pos, 0)
 
     steps = BANDS // PACE
     rows_spec = pl.BlockSpec((PACE, 2, BOX, LANES), lambda b: (b, 0, 0, 0))
@@ -437,7 +441,7 @@
         out_specs=(block_spec, block_spec),
         scratch_shapes=[pltpu.VMEM((2, 3, BOX, LANES), f32), pltpu.VMEM((2, BOX, LANES), f32)],
         name="blend",
-    )(side_pos.reshape(1), low_half, high_half, first, second, before, after, *edges)
+    )(side_flag, low_half, high_half, first, second, before, after, *edges)
     near = lax.ppermute(near, everyone, home_pairs(0))
     far = lax.ppermute(far, everyone, home_pairs(1))
     low = jnp.where(half_pos == 0, near, far)

time: 228 us -> 227 us (level)
  waiting for transfers between devices: 67.7 us -> 45 us
  starting transfers between devices: 38 us -> 47.7 us
  blocking collectives: 93.8 us -> 103 us
    ppermute x12 -> x13, waiting for transfers between devices: 47.1 us -> 24.9 us  [send(): return lax.ppermute(part, here, pairs)]
    ppermute x12 -> x13, starting transfers between devices: 30.5 us -> 40.2 us  [send(): return lax.ppermute(part, here, pairs)]
    all_to_all x1, blocking collectives: 93.8 us -> 103 us  [on_device(): lax.all_to_all(sent.reshape(2 * SENDERS, PER, LANES), everyone, split_axi...]
  transfers between devices with their start and end apart: 19 -> 20, of which waited for: 10 -> 7; matrix products, arithmetic and copies ran while one was open for 0% -> 1% of each run, Pallas kernels for 0% -> 0%
where the time goes in v5:
time: 227 us; the launch traced here: 226 us
  blocking collectives  103 us (45%)
  starting transfers between devices  47.7 us (21%)
  waiting for transfers between devices  45 us (20%)
  Pallas kernels  24 us (11%)
  local copies, waits for them, and re-layouts  3.46 us (2%)
    all_to_all x1, blocking collectives, on_device(): lax.all_to_all(sent.reshape(2 * SENDERS, PER, LANES), everyone, split_axi...  103 us
    ppermute x13, starting transfers between devices, send(): return lax.ppermute(part, here, pairs)  40.2 us
    ppermute x13, waiting for transfers between devices, send(): return lax.ppermute(part, here, pairs)  24.9 us
    ppermute x1, waiting for transfers between devices, on_device(): near = lax.ppermute(near, everyone, home_pairs(0))  11.5 us
    ppermute x3, waiting for transfers between devices, on_device(): edges = [lax.ppermute(edge, everyone, row_pairs(n, 1)) for n in (0, 1, -1)]  8.52 us
    pallas_call x1, Pallas kernels, on_device(): pl.pallas_call(planes_kernel, out_shape=jax.ShapeDtypeStruct((SENDERS //...  7.27 us
    pallas_call x1, Pallas kernels, on_device(): pl.pallas_call(depth_kernel, grid=(BANDS // 2,), out_shape=(rows_shape, r...  6.15 us
    pallas_call x1, Pallas kernels, on_device(): pl.pallas_call(blend_kernel, grid=(steps,), out_shape=(block_shape, block...  5.63 us
  transfers between devices with their start and end apart: 20, of which 7 were waited for; matrix products, arithmetic and copies ran while one was open for 1% of the time, Pallas kernels for 0%

profile of v5, /device:TPU:1, one launch (start us, length us, event | category | flops | bytes accessed | tf_op | source)
XLA Modules:
  0.0 225.8 jit_solution(2176334127546937396)
XLA Ops:
  0.0 5.0 %place.1 = (f32[32,4096]{1,0:T(8,128)}, f32[32,4096]{1,0:T(8,128)}, f32[32,4096]{1,0:T(8,128)}, f32[32,4096]{1,0:T(8,128)}, f32[16,4096]{1,0:T(8,128)}, /*index=...) custom-call(s32[1]{0:T(128)} %bitcast.1.slab_ref, s32[1]{0:T(128)} %bitcast.2.group_ref, ...), custom_call_target="tpu_custom_call" | custom-call | tf_op jit(solution)/shard_map/place/pallas_call | solution.py:362
  5.0 5.8 %collective-permute-start.2 = (f32[16,4096]{1,0:T(8,128)}, f32[16,4096]{1,0:T(8,128)S(1)}, u32[]{:S(2)}, u32[]{:S(2)}) collective-permute-start(f32[16,4096]{1,0:T(8,128)} %get-tuple-element.25), channel_id=1, source_target_pairs={{0,60},{4,56},{8,52},{12,48},{16,44},{20,40},{24,36},{28,32},{32,2... | collective-permute-start | bytes 786440 | tf_op jit(solution)/shard_map/ppermute | solution.py:385
  10.8 0.1 collective-permute-start.8
  10.9 5.2 %collective-permute-done.2 = f32[16,4096]{1,0:T(8,128)S(1)} collective-permute-done((f32[16,4096]{1,0:T(8,128)}, f32[16,4096]{1,0:T(8,128)S(1)}, u32[]{:S(2)}, u32[]{:S(2)}) %collective-permute-start.2) | collective-permute-done | bytes 262176 | tf_op jit(solution)/shard_map/ppermute | solution.py:385
  16.1 2.4 %collective-permute-start.3 = (f32[16,4096]{1,0:T(8,128)S(1)}, f32[16,4096]{1,0:T(8,128)S(1)}, u32[]{:S(2)}, u32[]{:S(2)}) collective-permute-start(f32[16,4096]{1,0:T(8,128)S(1)} %collective-permute-done.2), channel_id=1, source_target_pairs={{0,2},{4,6},{8,10},{12,14},{16,18},{20,22},{24,26},{28,30},{32,34}... | collective-permute-start | bytes 786440 | tf_op jit(solution)/shard_map/ppermute | solution.py:385
  18.5 4.6 %collective-permute-start.1 = (f32[32,4096]{1,0:T(8,128)}, f32[32,4096]{1,0:T(8,128)S(1)}, u32[]{:S(2)}, u32[]{:S(2)}) collective-permute-start(f32[32,4096]{1,0:T(8,128)} %get-tuple-element.23), channel_id=1, source_target_pairs={{0,60},{4,56},{8,52},{12,48},{16,44},{20,40},{24,36},{28,32},{32,2... | collective-permute-start | bytes 1572872 | tf_op jit(solution)/shard_map/ppermute | solution.py:385
  23.2 0.2 collective-permute-start.7
  23.3 0.0 collective-permute-done.8
  23.3 5.1 %collective-permute-start.9 = (f32[16,4096]{1,0:T(8,128)S(1)}, f32[16,4096]{1,0:T(8,128)S(1)}, u32[]{:S(2)}, u32[]{:S(2)}) collective-permute-start(f32[16,4096]{1,0:T(8,128)S(1)} %collective-permute-done.8), channel_id=1, source_target_pairs={{0,194},{4,198},{8,202},{12,206},{16,210},{20,214},{24,218},{28,22... | collective-permute-start | bytes 786440 | tf_op jit(solution)/shard_map/ppermute | solution.py:385
  28.4 0.0 collective-permute-done.3
  28.4 1.1 slice_add_fusion.1
  29.6 0.1 collective-permute-start.4
  29.7 2.1 collective-permute-done.9
  31.8 0.0 copy-done.7
  31.8 0.0 copy-start.11
  31.8 0.0 copy-start.3
  31.9 3.5 %collective-permute-start.10 = (f32[32,4096]{1,0:T(8,128)S(1)}, f32[32,4096]{1,0:T(8,128)S(1)}, u32[]{:S(2)}, u32[]{:S(2)}) collective-permute-start(f32[32,4096]{1,0:T(8,128)S(1)} %pad_maximum_fusion.1), channel_id=1, source_target_pairs={{0,194},{4,198},{8,202},{12,206},{16,210},{20,214},{24,218},{28,22... | collective-permute-start | bytes 1572872 | tf_op jit(solution)/shard_map/ppermute | solution.py:385
  35.4 0.0 collective-permute-done.1
  35.4 5.6 %collective-permute-done.4 = f32[32,4096]{1,0:T(8,128)S(1)} collective-permute-done((f32[32,4096]{1,0:T(8,128)S(1)}, f32[32,4096]{1,0:T(8,128)S(1)}, u32[]{:S(2)}, u32[]{:S(2)}) %collective-permute-start.4) | collective-permute-done | bytes 524320 | tf_op jit(solution)/shard_map/ppermute | solution.py:385
  41.0 0.1 add.32
  41.1 0.1 collective-permute-start.5
  41.2 3.1 %collective-permute-done.7 = f32[32,4096]{1,0:T(8,128)S(1)} collective-permute-done((f32[32,4096]{1,0:T(8,128)}, f32[32,4096]{1,0:T(8,128)S(1)}, u32[]{:S(2)}, u32[]{:S(2)}) %collective-permute-start.7) | collective-permute-done | bytes 524320 | tf_op jit(solution)/shard_map/ppermute | solution.py:385
  44.3 0.0 collective-permute-done.10
  44.3 0.1 add.35
  44.3 4.1 %collective-permute-start.11 = (f32[32,4096]{1,0:T(8,128)S(1)}, f32[32,4096]{1,0:T(8,128)S(1)}, u32[]{:S(2)}, u32[]{:S(2)}) collective-permute-start(f32[32,4096]{1,0:T(8,128)S(1)} %add.35), channel_id=1, source_target_pairs={{0,194},{4,198},{8,202},{12,206},{16,210},{20,214},{24,218},{28,22... | collective-permute-start | bytes 1572872 | tf_op jit(solution)/shard_map/ppermute | solution.py:385
  48.4 6.6 %collective-permute-start = (f32[32,4096]{1,0:T(8,128)S(1)}, f32[32,4096]{1,0:T(8,128)S(1)}, u32[]{:S(2)}, u32[]{:S(2)}) collective-permute-start(f32[32,4096]{1,0:T(8,128)S(1)} %copy-done.11), channel_id=1, source_target_pairs={{0,60},{4,56},{8,52},{12,48},{16,44},{20,40},{24,36},{28,32},{32,2... | collective-permute-start | bytes 1572872 | tf_op jit(solution)/shard_map/ppermute | solution.py:385
  55.1 0.0 collective-permute-done.5
  55.1 0.0 copy-done.3
  55.1 0.1 add.33
  55.2 0.1 collective-permute-start.6
  55.3 0.0 collective-permute-done.11
  55.3 0.1 add.36
  55.4 7.5 %collective-permute-start.12 = (f32[32,4096]{1,0:T(8,128)S(1)}, f32[32,4096]{1,0:T(8,128)S(1)}, u32[]{:S(2)}, u32[]{:S(2)}) collective-permute-start(f32[32,4096]{1,0:T(8,128)S(1)} %add.36), channel_id=1, source_target_pairs={{0,194},{4,198},{8,202},{12,206},{16,210},{20,214},{24,218},{28,22... | collective-permute-start | bytes 1572872 | tf_op jit(solution)/shard_map/ppermute | solution.py:385
  62.8 8.8 %collective-permute-done.own_ref = f32[32,4096]{1,0:T(8,128)S(1)} collective-permute-done((f32[32,4096]{1,0:T(8,128)S(1)}, f32[32,4096]{1,0:T(8,128)S(1)}, u32[]{:S(2)}, u32[]{:S(2)}) %collective-permute-start) | collective-permute-done | bytes 524320 | tf_op jit(solution)/shard_map/ppermute | solution.py:385
  71.7 0.0 collective-permute-done.6.up_ref
  71.7 0.0 collective-permute-done.12.down_ref
  71.7 0.8 copy-done.4
  72.4 0.2 copy-done.5
  72.6 0.2 copy-done.6
  72.8 7.3 %planes.1 = f32[32,8,3,8,128]{4,3,2,1,0:T(8,128)} custom-call(s32[6]{0:T(128)} %cut_ref.1, s32[1]{0:T(128)} %bitcast.kz_ref, f32[32,4096]{1,0:T(8,128)} %copy-done.4, f32[32,4096]{1,0:T(8,128)} %copy-done.5, f32[32,4096]{1,0:T(8,128)} %copy-done.6, bf16[2,2,256,256]{3,2,1,0:T(8,128)(2,1)} %constant.40.clone.y_ref, bf16[2,2,256,256]{3,2,1,0:T(8,128)(2,1)} %constant.41.clone.x_ref), custom_call_target="tpu_custom_call" | custom-call | tf_op jit(solution)/shard_map/planes/pallas_call | solution.py:401
  80.1 103.3 %all_to_all.5 = f32[256,24,128]{2,1,0:T(8,128)} all-to-all(f32[256,24,128]{2,1,0:T(8,128)} %bitcast.14), channel_id=1, replica_groups=mesh['particle'=4,'slab'=32,'half'=2] {'particle','slab','half'}, dimensions={0} | all-to-all | bytes 6291456 | tf_op jit(solution)/shard_map/all_to_all | solution.py:409
  183.4 6.1 %depth.1 = (f32[6,2,256,128]{3,2,1,0:T(8,128)}, f32[6,2,256,128]{3,2,1,0:T(8,128)}, f32[6,256,128]{2,1,0:T(8,128)}, f32[6,256,128]{2,1,0:T(8,128)}, f32[64,128]{1,0:T(8,128)}) custom-call(f32[6144,128]{1,0:T(8,128)} %bitcast.13, bf16[2,256,256]{2,1,0:T(8,128)(2,1)} %constant.42.clone.z_ref), custom_call_target="tpu_custom_call" | custom-call | tf_op jit(solution)/shard_map/depth/pallas_call | solution.py:419
  189.5 0.0 collective-permute-start.14
  189.5 1.7 collective-permute-start.13
  191.3 0.0 collective-permute-start.17
  191.3 1.7 collective-permute-start.16
  193.0 0.9 collective-permute-start.15
  194.0 0.5 compare_select_fusion.side_ref
  194.5 8.5 %collective-permute-done.17.edge_after_ref = f32[64,128]{1,0:T(8,128)S(1)} collective-permute-done((f32[64,128]{1,0:T(8,128)}, f32[64,128]{1,0:T(8,128)S(1)}, u32[]{:S(2)}, u32[]{:S(2)}) %collective-permute-start.17) | collective-permute-done | bytes 32800 | tf_op jit(solution)/shard_map/ppermute | solution.py:433
  203.0 0.0 collective-permute-done.16.edge_before_ref
  203.0 0.0 collective-permute-done.15.edge_ref
  203.0 0.0 collective-permute-done.14.after_ref
  203.1 0.0 collective-permute-done.13.before_ref
  203.1 0.5 copy-done.8
  203.6 0.0 copy-done.9
  203.6 0.0 copy-done.10
  203.6 0.3 copy-done
  204.0 0.2 copy-done.1
  204.2 5.6 %blend.1 = (f32[2,256,128]{2,1,0:T(8,128)}, f32[2,256,128]{2,1,0:T(8,128)}) custom-call(s32[128]{0:T(128)} %compare_select_fusion.side_ref, f32[6,2,256,128]{3,2,1,0:T(8,128)} %get-tuple-element.30.low_half_ref, f32[6,2,256,128]{3,2,1,0:T(8,128)} %get-tuple-element.31.high_half_ref, f32[6,256,128]{2,1,0:T(8,128)} %get-tuple-element.32.first_ref, ...), custom_call_target="tpu_custom_call" | custom-call | tf_op jit(solution)/shard_map/blend/pallas_call | solution.py:436
  209.8 3.0 %collective-permute-start.18 = (f32[2,256,128]{2,1,0:T(8,128)}, f32[2,256,128]{2,1,0:T(8,128)S(1)}, u32[]{:S(2)}, u32[]{:S(2)}) collective-permute-start(f32[2,256,128]{2,1,0:T(8,128)} %get-tuple-element.35), channel_id=1, source_target_pairs={{0,0},{1,2},{6,1},{7,3},{4,4},{5,6},{2,5},{3,7},{8,8},{9,10},{14,9... | collective-permute-start | bytes 786440 | tf_op jit(solution)/shard_map/ppermute | solution.py:445
  212.8 0.1 collective-permute-start.19
  212.9 11.5 %collective-permute-done.18 = f32[2,256,128]{2,1,0:T(8,128)S(1)} collective-permute-done((f32[2,256,128]{2,1,0:T(8,128)}, f32[2,256,128]{2,1,0:T(8,128)S(1)}, u32[]{:S(2)}, u32[]{:S(2)}) %collective-permute-start.18) | collective-permute-done | bytes 262176 | tf_op jit(solution)/shard_map/ppermute | solution.py:445
  224.5 0.0 collective-permute-done.19
  224.6 1.2 copy.9
  (17 shorter events, 0.2 us)
Async XLA Ops:
  5.0 26.8 %copy-start.7 = (f32[32,4096]{1,0:T(8,128)S(1)}, f32[32,4096]{1,0:T(8,128)}, u32[]{:S(2)}) copy-start(f32[32,4096]{1,0:T(8,128)} %get-tuple-element.28) | copy-start | bytes 1572868
  5.0 11.1 %collective-permute-start.2 = (f32[16,4096]{1,0:T(8,128)}, f32[16,4096]{1,0:T(8,128)S(1)}, u32[]{:S(2)}, u32[]{:S(2)}) collective-permute-start(f32[16,4096]{1,0:T(8,128)} %get-tuple-element.25), channel_id=1, source_target_pairs={{0,60},{4,56},{8,52},{12,48},{16,44},{20,40},{24,36},{28,32},{32,2... | collective-permute-start | bytes 786440 | tf_op jit(solution)/shard_map/ppermute | solution.py:385
  10.8 12.5 %collective-permute-start.8 = (f32[16,4096]{1,0:T(8,128)}, f32[16,4096]{1,0:T(8,128)S(1)}, u32[]{:S(2)}, u32[]{:S(2)}) collective-permute-start(f32[16,4096]{1,0:T(8,128)} %get-tuple-element.29), channel_id=1, source_target_pairs={{0,60},{4,56},{8,52},{12,48},{16,44},{20,40},{24,36},{28,32},{32,2... | collective-permute-start | bytes 786440 | tf_op jit(solution)/shard_map/ppermute | solution.py:385
  16.1 12.3 %collective-permute-start.3 = (f32[16,4096]{1,0:T(8,128)S(1)}, f32[16,4096]{1,0:T(8,128)S(1)}, u32[]{:S(2)}, u32[]{:S(2)}) collective-permute-start(f32[16,4096]{1,0:T(8,128)S(1)} %collective-permute-done.2), channel_id=1, source_target_pairs={{0,2},{4,6},{8,10},{12,14},{16,18},{20,22},{24,26},{28,30},{32,34}... | collective-permute-start | bytes 786440 | tf_op jit(solution)/shard_map/ppermute | solution.py:385
  18.5 16.8 %collective-permute-start.1 = (f32[32,4096]{1,0:T(8,128)}, f32[32,4096]{1,0:T(8,128)S(1)}, u32[]{:S(2)}, u32[]{:S(2)}) collective-permute-start(f32[32,4096]{1,0:T(8,128)} %get-tuple-element.23), channel_id=1, source_target_pairs={{0,60},{4,56},{8,52},{12,48},{16,44},{20,40},{24,36},{28,32},{32,2... | collective-permute-start | bytes 1572872 | tf_op jit(solution)/shard_map/ppermute | solution.py:385
  23.2 21.1 %collective-permute-start.7 = (f32[32,4096]{1,0:T(8,128)}, f32[32,4096]{1,0:T(8,128)S(1)}, u32[]{:S(2)}, u32[]{:S(2)}) collective-permute-start(f32[32,4096]{1,0:T(8,128)} %get-tuple-element.27), channel_id=1, source_target_pairs={{0,60},{4,56},{8,52},{12,48},{16,44},{20,40},{24,36},{28,32},{32,2... | collective-permute-start | bytes 1572872 | tf_op jit(solution)/shard_map/ppermute | solution.py:385
  23.3 8.4 %collective-permute-start.9 = (f32[16,4096]{1,0:T(8,128)S(1)}, f32[16,4096]{1,0:T(8,128)S(1)}, u32[]{:S(2)}, u32[]{:S(2)}) collective-permute-start(f32[16,4096]{1,0:T(8,128)S(1)} %collective-permute-done.8), channel_id=1, source_target_pairs={{0,194},{4,198},{8,202},{12,206},{16,210},{20,214},{24,218},{28,22... | collective-permute-start | bytes 786440 | tf_op jit(solution)/shard_map/ppermute | solution.py:385
  29.6 11.4 %collective-permute-start.4 = (f32[32,4096]{1,0:T(8,128)S(1)}, f32[32,4096]{1,0:T(8,128)S(1)}, u32[]{:S(2)}, u32[]{:S(2)}) collective-permute-start(f32[32,4096]{1,0:T(8,128)S(1)} %pad_maximum_fusion), channel_id=1, source_target_pairs={{0,2},{4,6},{8,10},{12,14},{16,18},{20,22},{24,26},{28,30},{32,34}... | collective-permute-start | bytes 1572872 | tf_op jit(solution)/shard_map/ppermute | solution.py:385
  31.8 16.6 %copy-start.11 = (f32[32,4096]{1,0:T(8,128)S(1)}, f32[32,4096]{1,0:T(8,128)}, u32[]{:S(2)}) copy-start(f32[32,4096]{1,0:T(8,128)} %get-tuple-element.21) | copy-start | bytes 1572868
  31.8 23.3 %copy-start.3 = (f32[32,4096]{1,0:T(8,128)S(1)}, f32[32,4096]{1,0:T(8,128)}, u32[]{:S(2)}) copy-start(f32[32,4096]{1,0:T(8,128)} %get-tuple-element.22) | copy-start | bytes 1572868
  31.9 23.4 %copy-start.2 = (f32[32,4096]{1,0:T(8,128)S(1)}, f32[32,4096]{1,0:T(8,128)}, u32[]{:S(2)}) copy-start(f32[32,4096]{1,0:T(8,128)} %get-tuple-element.26) | copy-start | bytes 1572868
  31.9 12.4 %collective-permute-start.10 = (f32[32,4096]{1,0:T(8,128)S(1)}, f32[32,4096]{1,0:T(8,128)S(1)}, u32[]{:S(2)}, u32[]{:S(2)}) collective-permute-start(f32[32,4096]{1,0:T(8,128)S(1)} %pad_maximum_fusion.1), channel_id=1, source_target_pairs={{0,194},{4,198},{8,202},{12,206},{16,210},{20,214},{24,218},{28,22... | collective-permute-start | bytes 1572872 | tf_op jit(solution)/shard_map/ppermute | solution.py:385
  41.1 14.0 %collective-permute-start.5 = (f32[32,4096]{1,0:T(8,128)S(1)}, f32[32,4096]{1,0:T(8,128)S(1)}, u32[]{:S(2)}, u32[]{:S(2)}) collective-permute-start(f32[32,4096]{1,0:T(8,128)S(1)} %add.32), channel_id=1, source_target_pairs={{0,2},{4,6},{8,10},{12,14},{16,18},{20,22},{24,26},{28,30},{32,34}... | collective-permute-start | bytes 1572872 | tf_op jit(solution)/shard_map/ppermute | solution.py:385
  44.3 10.9 %collective-permute-start.11 = (f32[32,4096]{1,0:T(8,128)S(1)}, f32[32,4096]{1,0:T(8,128)S(1)}, u32[]{:S(2)}, u32[]{:S(2)}) collective-permute-start(f32[32,4096]{1,0:T(8,128)S(1)} %add.35), channel_id=1, source_target_pairs={{0,194},{4,198},{8,202},{12,206},{16,210},{20,214},{24,218},{28,22... | collective-permute-start | bytes 1572872 | tf_op jit(solution)/shard_map/ppermute | solution.py:385
  48.4 23.2 %collective-permute-start = (f32[32,4096]{1,0:T(8,128)S(1)}, f32[32,4096]{1,0:T(8,128)S(1)}, u32[]{:S(2)}, u32[]{:S(2)}) collective-permute-start(f32[32,4096]{1,0:T(8,128)S(1)} %copy-done.11), channel_id=1, source_target_pairs={{0,60},{4,56},{8,52},{12,48},{16,44},{20,40},{24,36},{28,32},{32,2... | collective-permute-start | bytes 1572872 | tf_op jit(solution)/shard_map/ppermute | solution.py:385
  55.2 16.5 %collective-permute-start.6 = (f32[32,4096]{1,0:T(8,128)S(1)}, f32[32,4096]{1,0:T(8,128)S(1)}, u32[]{:S(2)}, u32[]{:S(2)}) collective-permute-start(f32[32,4096]{1,0:T(8,128)S(1)} %add.33), channel_id=1, source_target_pairs={{0,2},{4,6},{8,10},{12,14},{16,18},{20,22},{24,26},{28,30},{32,34}... | collective-permute-start | bytes 1572872 | tf_op jit(solution)/shard_map/ppermute | solution.py:385
  55.4 16.3 %collective-permute-start.12 = (f32[32,4096]{1,0:T(8,128)S(1)}, f32[32,4096]{1,0:T(8,128)S(1)}, u32[]{:S(2)}, u32[]{:S(2)}) collective-permute-start(f32[32,4096]{1,0:T(8,128)S(1)} %add.36), channel_id=1, source_target_pairs={{0,194},{4,198},{8,202},{12,206},{16,210},{20,214},{24,218},{28,22... | collective-permute-start | bytes 1572872 | tf_op jit(solution)/shard_map/ppermute | solution.py:385
  71.7 0.8 copy-start.4
  71.7 1.0 copy-start.5
  71.7 1.1 copy-start.6
  189.5 13.5 %collective-permute-start.14 = (f32[6,256,128]{2,1,0:T(8,128)}, f32[6,256,128]{2,1,0:T(8,128)S(1)}, u32[]{:S(2)}, u32[]{:S(2)}) collective-permute-start(f32[6,256,128]{2,1,0:T(8,128)} %get-tuple-element.32.first_ref), channel_id=1, source_target_pairs={{0,253},{6,251},{1,0},{7,6},{4,1},{2,7},{5,4},{3,2},{8,5},{14,3},{... | collective-permute-start | bytes 2359304 | tf_op jit(solution)/shard_map/ppermute | solution.py:432
  189.5 13.5 %collective-permute-start.13 = (f32[6,256,128]{2,1,0:T(8,128)}, f32[6,256,128]{2,1,0:T(8,128)S(1)}, u32[]{:S(2)}, u32[]{:S(2)}) collective-permute-start(f32[6,256,128]{2,1,0:T(8,128)} %get-tuple-element.33.second_ref), channel_id=1, source_target_pairs={{0,1},{6,7},{1,4},{7,2},{4,5},{2,3},{5,8},{3,14},{8,9},{14,15},{9,... | collective-permute-start | bytes 2359304 | tf_op jit(solution)/shard_map/ppermute | solution.py:431
  191.3 11.8 %collective-permute-start.17 = (f32[64,128]{1,0:T(8,128)}, f32[64,128]{1,0:T(8,128)S(1)}, u32[]{:S(2)}, u32[]{:S(2)}) collective-permute-start(f32[64,128]{1,0:T(8,128)} %get-tuple-element.34), channel_id=1, source_target_pairs={{0,251},{6,253},{1,6},{7,0},{4,7},{2,1},{5,2},{3,4},{8,3},{14,5},{... | collective-permute-start | bytes 98312 | tf_op jit(solution)/shard_map/ppermute | solution.py:433
  191.3 11.8 %collective-permute-start.16 = (f32[64,128]{1,0:T(8,128)}, f32[64,128]{1,0:T(8,128)S(1)}, u32[]{:S(2)}, u32[]{:S(2)}) collective-permute-start(f32[64,128]{1,0:T(8,128)} %get-tuple-element.34), channel_id=1, source_target_pairs={{0,7},{6,1},{1,2},{7,4},{4,3},{2,5},{5,14},{3,8},{8,15},{14,9},{9,... | collective-permute-start | bytes 98312 | tf_op jit(solution)/shard_map/ppermute | solution.py:433
  193.0 10.0 %collective-permute-start.15 = (f32[64,128]{1,0:T(8,128)}, f32[64,128]{1,0:T(8,128)S(1)}, u32[]{:S(2)}, u32[]{:S(2)}) collective-permute-start(f32[64,128]{1,0:T(8,128)} %get-tuple-element.34), channel_id=1, source_target_pairs={{0,6},{6,0},{1,7},{7,1},{4,2},{2,4},{5,3},{3,5},{8,14},{14,8},{9,1... | collective-permute-start | bytes 98312 | tf_op jit(solution)/shard_map/ppermute | solution.py:433
  203.0 0.6 copy-start.8
  203.0 0.6 copy-start.9
  203.0 0.6 copy-start.10
  203.1 0.9 copy-start
  203.1 1.1 copy-start.1
  209.8 14.7 %collective-permute-start.18 = (f32[2,256,128]{2,1,0:T(8,128)}, f32[2,256,128]{2,1,0:T(8,128)S(1)}, u32[]{:S(2)}, u32[]{:S(2)}) collective-permute-start(f32[2,256,128]{2,1,0:T(8,128)} %get-tuple-element.35), channel_id=1, source_target_pairs={{0,0},{1,2},{6,1},{7,3},{4,4},{5,6},{2,5},{3,7},{8,8},{9,10},{14,9... | collective-permute-start | bytes 786440 | tf_op jit(solution)/shard_map/ppermute | solution.py:445
  212.8 11.7 %collective-permute-start.19 = (f32[2,256,128]{2,1,0:T(8,128)}, f32[2,256,128]{2,1,0:T(8,128)S(1)}, u32[]{:S(2)}, u32[]{:S(2)}) collective-permute-start(f32[2,256,128]{2,1,0:T(8,128)} %get-tuple-element.36), channel_id=1, source_target_pairs={{0,1},{1,3},{6,0},{7,2},{4,5},{5,7},{2,4},{3,6},{8,9},{9,11},{14,8... | collective-permute-start | bytes 786440 | tf_op jit(solution)/shard_map/ppermute | solution.py:446

commit v6 on v4

--- a/solution.py
+++ b/solution.py
@@ -402,9 +402,9 @@
         scratch_shapes=[pltpu.VMEM((2 * BOX, BOX), bf16)] * 2 + [pltpu.VMEM((BOX, BOX), f32)],
         name="planes",
     )(cutoffs, plane, own, rise, sink, *constants[:2])
-    gathered = lax.all_to_all(
-        sent.reshape(2 * SENDERS, PER, LANES), everyone, split_axis=0, concat_axis=0, tiled=True
-    ).reshape(2 * SENDERS * PER, LANES)
+    gathered = lax.all_to_all(sent.reshape(2 * SENDERS, PER, LANES), everyone, split_axis=0, concat_axis=0, tiled=True)
+    gathered = gathered.reshape(2 * SENDERS * PER, LANES)
+    side_flag = jnp.where(jnp.arange(LANES, dtype=jnp.int32) == 0, side_pos, 0)
 
     steps = BANDS // PACE
     rows_spec = pl.BlockSpec((PACE, 2, BOX, LANES), lambda b: (b, 0, 0, 0))
@@ -437,7 +437,7 @@
         out_specs=(block_spec, block_spec),
         scratch_shapes=[pltpu.VMEM((2, 3, BOX, LANES), f32), pltpu.VMEM((2, BOX, LANES), f32)],
         name="blend",
-    )(side_pos.reshape(1), low_half, high_half, first, second, before, after, *edges)
+    )(side_flag, low_half, high_half, first, second, before, after, *edges)
     near = lax.ppermute(near, everyone, home_pairs(0))
     far = lax.ppermute(far, everyone, home_pairs(1))
     low = jnp.where(half_pos == 0, near, far)

time: 228 us -> 228 us (level)
  no operation moved by 1% of the time
where the time goes in v6:
time: 228 us; the launch traced here: 227 us
  blocking collectives  93.8 us (41%)
  waiting for transfers between devices  67.2 us (29%)
  starting transfers between devices  38 us (17%)
  Pallas kernels  24 us (11%)
  local copies, waits for them, and re-layouts  3.14 us (1%)
    all_to_all x1, blocking collectives, on_device(): lax.all_to_all(sent.reshape(2 * SENDERS, PER, LANES), everyone, split_axi...  93.8 us
    ppermute x12, waiting for transfers between devices, send(): return lax.ppermute(part, here, pairs)  47.1 us
    ppermute x12, starting transfers between devices, send(): return lax.ppermute(part, here, pairs)  30.5 us
    ppermute x1, waiting for transfers between devices, on_device(): near = lax.ppermute(near, everyone, home_pairs(0))  11.5 us
    ppermute x3, waiting for transfers between devices, on_device(): edges = [lax.ppermute(edge, everyone, row_pairs(n, 1)) for n in (0, 1, -1)]  8.53 us
    pallas_call x1, Pallas kernels, on_device(): pl.pallas_call(planes_kernel, out_shape=jax.ShapeDtypeStruct((SENDERS //...  7.28 us
    pallas_call x1, Pallas kernels, on_device(): pl.pallas_call(depth_kernel, grid=(BANDS // 2,), out_shape=(rows_shape, r...  6.15 us
    pallas_call x1, Pallas kernels, on_device(): pl.pallas_call(blend_kernel, grid=(steps,), out_shape=(block_shape, block...  5.64 us
  transfers between devices with their start and end apart: 19, of which 10 were waited for; matrix products, arithmetic and copies ran while one was open for 0% of the time, Pallas kernels for 0%

profile of v6, /device:TPU:1, one launch (start us, length us, event | category | flops | bytes accessed | tf_op | source)
XLA Modules:
  0.0 227.3 jit_solution(11612359095123228621)
XLA Ops:
  0.0 4.9 %place.1 = (f32[32,4096]{1,0:T(8,128)}, f32[32,4096]{1,0:T(8,128)}, f32[16,4096]{1,0:T(8,128)}, f32[16,4096]{1,0:T(8,128)}, f32[32,4096]{1,0:T(8,128)}, /*index=...) custom-call(s32[1]{0:T(128)} %bitcast.1.slab_ref, s32[1]{0:T(128)} %bitcast.2.group_ref, ...), custom_call_target="tpu_custom_call" | custom-call | tf_op jit(solution)/shard_map/place/pallas_call | solution.py:362
  4.9 5.8 %collective-permute-start.1 = (f32[32,4096]{1,0:T(8,128)}, f32[32,4096]{1,0:T(8,128)S(1)}, u32[]{:S(2)}, u32[]{:S(2)}) collective-permute-start(f32[32,4096]{1,0:T(8,128)} %get-tuple-element.24), channel_id=1, source_target_pairs={{0,60},{4,56},{8,52},{12,48},{16,44},{20,40},{24,36},{28,32},{32,2... | collective-permute-start | bytes 1572872 | tf_op jit(solution)/shard_map/ppermute | solution.py:385
  10.7 1.6 collective-permute-start.2
  12.4 3.9 %collective-permute-start.8 = (f32[16,4096]{1,0:T(8,128)}, f32[16,4096]{1,0:T(8,128)S(1)}, u32[]{:S(2)}, u32[]{:S(2)}) collective-permute-start(f32[16,4096]{1,0:T(8,128)} %get-tuple-element.29), channel_id=1, source_target_pairs={{0,194},{4,198},{8,202},{12,206},{16,210},{20,214},{24,218},{28,22... | collective-permute-start | bytes 786440 | tf_op jit(solution)/shard_map/ppermute | solution.py:385
  16.3 0.2 collective-permute-start.7
  16.5 5.7 %collective-permute-done.2 = f32[16,4096]{1,0:T(8,128)S(1)} collective-permute-done((f32[16,4096]{1,0:T(8,128)}, f32[16,4096]{1,0:T(8,128)S(1)}, u32[]{:S(2)}, u32[]{:S(2)}) %collective-permute-start.2) | collective-permute-done | bytes 262176 | tf_op jit(solution)/shard_map/ppermute | solution.py:385
  22.2 0.0 collective-permute-done.1
  22.3 0.0 copy-start.2
  22.4 1.9 collective-permute-start.3
  24.3 0.0 collective-permute-done.8
  24.3 9.5 %collective-permute-done.7 = f32[32,4096]{1,0:T(8,128)S(1)} collective-permute-done((f32[32,4096]{1,0:T(8,128)}, f32[32,4096]{1,0:T(8,128)S(1)}, u32[]{:S(2)}, u32[]{:S(2)}) %collective-permute-start.7) | collective-permute-done | bytes 524320 | tf_op jit(solution)/shard_map/ppermute | solution.py:385
  33.9 5.5 %collective-permute-start.9 = (f32[32,4096]{1,0:T(8,128)S(1)}, f32[32,4096]{1,0:T(8,128)S(1)}, u32[]{:S(2)}, u32[]{:S(2)}) collective-permute-start(f32[32,4096]{1,0:T(8,128)S(1)} %pad_maximum_fusion.1), channel_id=1, source_target_pairs={{0,194},{4,198},{8,202},{12,206},{16,210},{20,214},{24,218},{28,22... | collective-permute-start | bytes 1572872 | tf_op jit(solution)/shard_map/ppermute | solution.py:385
  39.4 0.0 copy-done.10
  39.4 4.6 %collective-permute-start = (f32[32,4096]{1,0:T(8,128)S(1)}, f32[32,4096]{1,0:T(8,128)S(1)}, u32[]{:S(2)}, u32[]{:S(2)}) collective-permute-start(f32[32,4096]{1,0:T(8,128)S(1)} %copy-done.10), channel_id=1, source_target_pairs={{0,60},{4,56},{8,52},{12,48},{16,44},{20,40},{24,36},{28,32},{32,1... | collective-permute-start | bytes 1572872 | tf_op jit(solution)/shard_map/ppermute | solution.py:385
  44.1 0.0 copy-done.9
  44.1 1.9 collective-permute-start.6
  46.0 0.0 collective-permute-done.3
  46.0 0.0 copy-done.3
  46.0 0.1 add.32
  46.1 0.1 collective-permute-start.4
  46.2 3.1 %collective-permute-done.9 = f32[32,4096]{1,0:T(8,128)S(1)} collective-permute-done((f32[32,4096]{1,0:T(8,128)S(1)}, f32[32,4096]{1,0:T(8,128)S(1)}, u32[]{:S(2)}, u32[]{:S(2)}) %collective-permute-start.9) | collective-permute-done | bytes 524320 | tf_op jit(solution)/shard_map/ppermute | solution.py:385
  49.3 0.0 copy-done.2
  49.3 0.1 add.35
  49.4 3.5 %collective-permute-start.10 = (f32[32,4096]{1,0:T(8,128)S(1)}, f32[32,4096]{1,0:T(8,128)S(1)}, u32[]{:S(2)}, u32[]{:S(2)}) collective-permute-start(f32[32,4096]{1,0:T(8,128)S(1)} %add.35), channel_id=1, source_target_pairs={{0,194},{4,198},{8,202},{12,206},{16,210},{20,214},{24,218},{28,22... | collective-permute-start | bytes 1572872 | tf_op jit(solution)/shard_map/ppermute | solution.py:385
  52.9 3.8 %collective-permute-done = f32[32,4096]{1,0:T(8,128)S(1)} collective-permute-done((f32[32,4096]{1,0:T(8,128)S(1)}, f32[32,4096]{1,0:T(8,128)S(1)}, u32[]{:S(2)}, u32[]{:S(2)}) %collective-permute-start) | collective-permute-done | bytes 524320 | tf_op jit(solution)/shard_map/ppermute | solution.py:385
  56.7 2.8 %collective-permute-done.4 = f32[32,4096]{1,0:T(8,128)S(1)} collective-permute-done((f32[32,4096]{1,0:T(8,128)S(1)}, f32[32,4096]{1,0:T(8,128)S(1)}, u32[]{:S(2)}, u32[]{:S(2)}) %collective-permute-start.4) | collective-permute-done | bytes 524320 | tf_op jit(solution)/shard_map/ppermute | solution.py:385
  59.5 0.1 add.33
  59.6 0.1 collective-permute-start.5
  59.7 10.3 %collective-permute-done.6 = f32[32,4096]{1,0:T(8,128)S(1)} collective-permute-done((f32[32,4096]{1,0:T(8,128)S(1)}, f32[32,4096]{1,0:T(8,128)S(1)}, u32[]{:S(2)}, u32[]{:S(2)}) %collective-permute-start.6) | collective-permute-done | bytes 524320 | tf_op jit(solution)/shard_map/ppermute | solution.py:385
  69.9 0.0 collective-permute-done.10
  69.9 0.1 add.36
  70.0 1.3 collective-permute-start.11
  71.3 8.2 %collective-permute-done.5.up_ref = f32[32,4096]{1,0:T(8,128)S(1)} collective-permute-done((f32[32,4096]{1,0:T(8,128)S(1)}, f32[32,4096]{1,0:T(8,128)S(1)}, u32[]{:S(2)}, u32[]{:S(2)}) %collective-permute-start.5) | collective-permute-done | bytes 524320 | tf_op jit(solution)/shard_map/ppermute | solution.py:385
  79.5 3.5 %collective-permute-done.11.down_ref = f32[32,4096]{1,0:T(8,128)S(1)} collective-permute-done((f32[32,4096]{1,0:T(8,128)S(1)}, f32[32,4096]{1,0:T(8,128)S(1)}, u32[]{:S(2)}, u32[]{:S(2)}) %collective-permute-start.11) | collective-permute-done | bytes 524320 | tf_op jit(solution)/shard_map/ppermute | solution.py:385
  83.1 0.0 copy-done.4
  83.1 0.8 copy-done.5
  83.9 7.3 %planes.1 = f32[32,8,3,8,128]{4,3,2,1,0:T(8,128)} custom-call(s32[6]{0:T(128)} %cut_ref.1, s32[1]{0:T(128)} %bitcast.kz_ref, f32[32,4096]{1,0:T(8,128)} %get-tuple-element.21.own_ref, f32[32,4096]{1,0:T(8,128)} %copy-done.4, f32[32,4096]{1,0:T(8,128)} %copy-done.5, bf16[2,2,256,256]{3,2,1,0:T(8,128)(2,1)} %constant.39.clone.y_ref, ...), custom_call_target="tpu_custom_call" | custom-call | tf_op jit(solution)/shard_map/planes/pallas_call | solution.py:397
  91.1 93.8 %all_to_all.5 = f32[256,24,128]{2,1,0:T(8,128)} all-to-all(f32[256,24,128]{2,1,0:T(8,128)} %bitcast.14), channel_id=1, replica_groups=mesh['particle'=4,'slab'=32,'half'=2] {'particle','slab','half'}, dimensions={0} | all-to-all | bytes 6291456 | tf_op jit(solution)/shard_map/all_to_all | solution.py:405
  184.9 6.1 %depth.1 = (f32[6,2,256,128]{3,2,1,0:T(8,128)}, f32[6,2,256,128]{3,2,1,0:T(8,128)}, f32[6,256,128]{2,1,0:T(8,128)}, f32[6,256,128]{2,1,0:T(8,128)}, f32[64,128]{1,0:T(8,128)}) custom-call(f32[6144,128]{1,0:T(8,128)} %bitcast.13, bf16[2,256,256]{2,1,0:T(8,128)(2,1)} %constant.41.clone.z_ref), custom_call_target="tpu_custom_call" | custom-call | tf_op jit(solution)/shard_map/depth/pallas_call | solution.py:415
  191.1 0.0 collective-permute-start.13
  191.1 1.7 collective-permute-start.12
  192.8 0.0 collective-permute-start.16
  192.8 1.7 collective-permute-start.15
  194.6 0.9 collective-permute-start.14
  195.5 0.5 compare_select_fusion.side_ref
  196.0 8.5 %collective-permute-done.16.edge_after_ref = f32[64,128]{1,0:T(8,128)S(1)} collective-permute-done((f32[64,128]{1,0:T(8,128)}, f32[64,128]{1,0:T(8,128)S(1)}, u32[]{:S(2)}, u32[]{:S(2)}) %collective-permute-start.16) | collective-permute-done | bytes 32800 | tf_op jit(solution)/shard_map/ppermute | solution.py:429
  204.6 0.0 collective-permute-done.15.edge_before_ref
  204.6 0.0 collective-permute-done.14.edge_ref
  204.6 0.0 copy-start.8
  204.6 0.0 collective-permute-done.13.after_ref
  204.6 0.0 copy-start
  204.6 0.0 collective-permute-done.12.before_ref
  204.6 0.0 copy-start.1
  204.6 0.5 copy-done.6
  205.2 0.0 copy-done.7
  205.2 0.0 copy-done.8
  205.2 0.3 copy-done
  205.5 0.2 copy-done.1
  205.7 5.6 %blend.1 = (f32[2,256,128]{2,1,0:T(8,128)}, f32[2,256,128]{2,1,0:T(8,128)}) custom-call(s32[128]{0:T(128)} %compare_select_fusion.side_ref, f32[6,2,256,128]{3,2,1,0:T(8,128)} %get-tuple-element.30.low_half_ref, f32[6,2,256,128]{3,2,1,0:T(8,128)} %get-tuple-element.31.high_half_ref, f32[6,256,128]{2,1,0:T(8,128)} %get-tuple-element.32.first_ref, ...), custom_call_target="tpu_custom_call" | custom-call | tf_op jit(solution)/shard_map/blend/pallas_call | solution.py:432
  211.4 3.0 %collective-permute-start.17 = (f32[2,256,128]{2,1,0:T(8,128)}, f32[2,256,128]{2,1,0:T(8,128)S(1)}, u32[]{:S(2)}, u32[]{:S(2)}) collective-permute-start(f32[2,256,128]{2,1,0:T(8,128)} %get-tuple-element.35), channel_id=1, source_target_pairs={{0,0},{1,2},{6,1},{7,3},{4,4},{5,6},{2,5},{3,7},{8,8},{9,10},{14,9... | collective-permute-start | bytes 786440 | tf_op jit(solution)/shard_map/ppermute | solution.py:441
  214.4 0.1 collective-permute-start.18
  214.5 11.5 %collective-permute-done.17 = f32[2,256,128]{2,1,0:T(8,128)S(1)} collective-permute-done((f32[2,256,128]{2,1,0:T(8,128)}, f32[2,256,128]{2,1,0:T(8,128)S(1)}, u32[]{:S(2)}, u32[]{:S(2)}) %collective-permute-start.17) | collective-permute-done | bytes 262176 | tf_op jit(solution)/shard_map/ppermute | solution.py:441
  226.0 0.0 collective-permute-done.18
  226.1 1.2 copy.9
  (13 shorter events, 0.2 us)
Async XLA Ops:
  4.9 17.3 %collective-permute-start.1 = (f32[32,4096]{1,0:T(8,128)}, f32[32,4096]{1,0:T(8,128)S(1)}, u32[]{:S(2)}, u32[]{:S(2)}) collective-permute-start(f32[32,4096]{1,0:T(8,128)} %get-tuple-element.24), channel_id=1, source_target_pairs={{0,60},{4,56},{8,52},{12,48},{16,44},{20,40},{24,36},{28,32},{32,2... | collective-permute-start | bytes 1572872 | tf_op jit(solution)/shard_map/ppermute | solution.py:385
  10.7 11.5 %collective-permute-start.2 = (f32[16,4096]{1,0:T(8,128)}, f32[16,4096]{1,0:T(8,128)S(1)}, u32[]{:S(2)}, u32[]{:S(2)}) collective-permute-start(f32[16,4096]{1,0:T(8,128)} %get-tuple-element.25), channel_id=1, source_target_pairs={{0,2},{4,6},{8,10},{12,14},{16,18},{20,22},{24,26},{28,30},{32,34}... | collective-permute-start | bytes 786440 | tf_op jit(solution)/shard_map/ppermute | solution.py:385
  12.4 11.9 %collective-permute-start.8 = (f32[16,4096]{1,0:T(8,128)}, f32[16,4096]{1,0:T(8,128)S(1)}, u32[]{:S(2)}, u32[]{:S(2)}) collective-permute-start(f32[16,4096]{1,0:T(8,128)} %get-tuple-element.29), channel_id=1, source_target_pairs={{0,194},{4,198},{8,202},{12,206},{16,210},{20,214},{24,218},{28,22... | collective-permute-start | bytes 786440 | tf_op jit(solution)/shard_map/ppermute | solution.py:385
  16.3 23.1 %copy-start.10 = (f32[32,4096]{1,0:T(8,128)S(1)}, f32[32,4096]{1,0:T(8,128)}, u32[]{:S(2)}) copy-start(f32[32,4096]{1,0:T(8,128)} %get-tuple-element.22) | copy-start | bytes 1572868
  16.3 27.7 %copy-start.9 = (f32[32,4096]{1,0:T(8,128)S(1)}, f32[32,4096]{1,0:T(8,128)}, u32[]{:S(2)}) copy-start(f32[32,4096]{1,0:T(8,128)} %get-tuple-element.26) | copy-start | bytes 1572868
  16.3 29.7 %copy-start.3 = (f32[32,4096]{1,0:T(8,128)S(1)}, f32[32,4096]{1,0:T(8,128)}, u32[]{:S(2)}) copy-start(f32[32,4096]{1,0:T(8,128)} %get-tuple-element.23) | copy-start | bytes 1572868
  16.3 17.5 %collective-permute-start.7 = (f32[32,4096]{1,0:T(8,128)}, f32[32,4096]{1,0:T(8,128)S(1)}, u32[]{:S(2)}, u32[]{:S(2)}) collective-permute-start(f32[32,4096]{1,0:T(8,128)} %get-tuple-element.28), channel_id=1, source_target_pairs={{0,60},{4,56},{8,52},{12,48},{16,44},{20,40},{24,36},{28,32},{32,2... | collective-permute-start | bytes 1572872 | tf_op jit(solution)/shard_map/ppermute | solution.py:385
  22.3 27.0 %copy-start.2 = (f32[32,4096]{1,0:T(8,128)S(1)}, f32[32,4096]{1,0:T(8,128)}, u32[]{:S(2)}) copy-start(f32[32,4096]{1,0:T(8,128)} %get-tuple-element.27) | copy-start | bytes 1572868
  22.4 23.7 %collective-permute-start.3 = (f32[32,4096]{1,0:T(8,128)S(1)}, f32[32,4096]{1,0:T(8,128)S(1)}, u32[]{:S(2)}, u32[]{:S(2)}) collective-permute-start(f32[32,4096]{1,0:T(8,128)S(1)} %pad_maximum_fusion), channel_id=1, source_target_pairs={{0,2},{4,6},{8,10},{12,14},{16,18},{20,22},{24,26},{28,30},{32,34}... | collective-permute-start | bytes 1572872 | tf_op jit(solution)/shard_map/ppermute | solution.py:385
  33.9 15.4 %collective-permute-start.9 = (f32[32,4096]{1,0:T(8,128)S(1)}, f32[32,4096]{1,0:T(8,128)S(1)}, u32[]{:S(2)}, u32[]{:S(2)}) collective-permute-start(f32[32,4096]{1,0:T(8,128)S(1)} %pad_maximum_fusion.1), channel_id=1, source_target_pairs={{0,194},{4,198},{8,202},{12,206},{16,210},{20,214},{24,218},{28,22... | collective-permute-start | bytes 1572872 | tf_op jit(solution)/shard_map/ppermute | solution.py:385
  39.4 17.3 %collective-permute-start = (f32[32,4096]{1,0:T(8,128)S(1)}, f32[32,4096]{1,0:T(8,128)S(1)}, u32[]{:S(2)}, u32[]{:S(2)}) collective-permute-start(f32[32,4096]{1,0:T(8,128)S(1)} %copy-done.10), channel_id=1, source_target_pairs={{0,60},{4,56},{8,52},{12,48},{16,44},{20,40},{24,36},{28,32},{32,1... | collective-permute-start | bytes 1572872 | tf_op jit(solution)/shard_map/ppermute | solution.py:385
  44.1 25.9 %collective-permute-start.6 = (f32[32,4096]{1,0:T(8,128)S(1)}, f32[32,4096]{1,0:T(8,128)S(1)}, u32[]{:S(2)}, u32[]{:S(2)}) collective-permute-start(f32[32,4096]{1,0:T(8,128)S(1)} %copy-done.9), channel_id=1, source_target_pairs={{0,60},{4,56},{8,52},{12,48},{16,44},{20,40},{24,36},{28,32},{32,2... | collective-permute-start | bytes 1572872 | tf_op jit(solution)/shard_map/ppermute | solution.py:385
  46.1 13.4 %collective-permute-start.4 = (f32[32,4096]{1,0:T(8,128)S(1)}, f32[32,4096]{1,0:T(8,128)S(1)}, u32[]{:S(2)}, u32[]{:S(2)}) collective-permute-start(f32[32,4096]{1,0:T(8,128)S(1)} %add.32), channel_id=1, source_target_pairs={{0,2},{4,6},{8,10},{12,14},{16,18},{20,22},{24,26},{28,30},{32,34}... | collective-permute-start | bytes 1572872 | tf_op jit(solution)/shard_map/ppermute | solution.py:385
  49.4 20.6 %collective-permute-start.10 = (f32[32,4096]{1,0:T(8,128)S(1)}, f32[32,4096]{1,0:T(8,128)S(1)}, u32[]{:S(2)}, u32[]{:S(2)}) collective-permute-start(f32[32,4096]{1,0:T(8,128)S(1)} %add.35), channel_id=1, source_target_pairs={{0,194},{4,198},{8,202},{12,206},{16,210},{20,214},{24,218},{28,22... | collective-permute-start | bytes 1572872 | tf_op jit(solution)/shard_map/ppermute | solution.py:385
  59.6 19.9 %collective-permute-start.5 = (f32[32,4096]{1,0:T(8,128)S(1)}, f32[32,4096]{1,0:T(8,128)S(1)}, u32[]{:S(2)}, u32[]{:S(2)}) collective-permute-start(f32[32,4096]{1,0:T(8,128)S(1)} %add.33), channel_id=1, source_target_pairs={{0,2},{4,6},{8,10},{12,14},{16,18},{20,22},{24,26},{28,30},{32,34}... | collective-permute-start | bytes 1572872 | tf_op jit(solution)/shard_map/ppermute | solution.py:385
  70.0 13.1 %collective-permute-start.11 = (f32[32,4096]{1,0:T(8,128)S(1)}, f32[32,4096]{1,0:T(8,128)S(1)}, u32[]{:S(2)}, u32[]{:S(2)}) collective-permute-start(f32[32,4096]{1,0:T(8,128)S(1)} %add.36), channel_id=1, source_target_pairs={{0,194},{4,198},{8,202},{12,206},{16,210},{20,214},{24,218},{28,22... | collective-permute-start | bytes 1572872 | tf_op jit(solution)/shard_map/ppermute | solution.py:385
  79.5 3.5 %copy-start.4 = (f32[32,4096]{1,0:T(8,128)}, f32[32,4096]{1,0:T(8,128)S(1)}, u32[]{:S(2)}) copy-start(f32[32,4096]{1,0:T(8,128)S(1)} %collective-permute-done.5.up_ref) | copy-start | bytes 1572868
  83.1 0.8 copy-start.5
  191.1 13.5 %collective-permute-start.13 = (f32[6,256,128]{2,1,0:T(8,128)}, f32[6,256,128]{2,1,0:T(8,128)S(1)}, u32[]{:S(2)}, u32[]{:S(2)}) collective-permute-start(f32[6,256,128]{2,1,0:T(8,128)} %get-tuple-element.32.first_ref), channel_id=1, source_target_pairs={{0,253},{6,251},{1,0},{7,6},{4,1},{2,7},{5,4},{3,2},{8,5},{14,3},{... | collective-permute-start | bytes 2359304 | tf_op jit(solution)/shard_map/ppermute | solution.py:428
  191.1 13.5 %collective-permute-start.12 = (f32[6,256,128]{2,1,0:T(8,128)}, f32[6,256,128]{2,1,0:T(8,128)S(1)}, u32[]{:S(2)}, u32[]{:S(2)}) collective-permute-start(f32[6,256,128]{2,1,0:T(8,128)} %get-tuple-element.33.second_ref), channel_id=1, source_target_pairs={{0,1},{6,7},{1,4},{7,2},{4,5},{2,3},{5,8},{3,14},{8,9},{14,15},{9,... | collective-permute-start | bytes 2359304 | tf_op jit(solution)/shard_map/ppermute | solution.py:427
  192.8 11.7 %collective-permute-start.16 = (f32[64,128]{1,0:T(8,128)}, f32[64,128]{1,0:T(8,128)S(1)}, u32[]{:S(2)}, u32[]{:S(2)}) collective-permute-start(f32[64,128]{1,0:T(8,128)} %get-tuple-element.34), channel_id=1, source_target_pairs={{0,251},{6,253},{1,6},{7,0},{4,7},{2,1},{5,2},{3,4},{8,3},{14,5},{... | collective-permute-start | bytes 98312 | tf_op jit(solution)/shard_map/ppermute | solution.py:429
  192.8 11.7 %collective-permute-start.15 = (f32[64,128]{1,0:T(8,128)}, f32[64,128]{1,0:T(8,128)S(1)}, u32[]{:S(2)}, u32[]{:S(2)}) collective-permute-start(f32[64,128]{1,0:T(8,128)} %get-tuple-element.34), channel_id=1, source_target_pairs={{0,7},{6,1},{1,2},{7,4},{4,3},{2,5},{5,14},{3,8},{8,15},{14,9},{9,... | collective-permute-start | bytes 98312 | tf_op jit(solution)/shard_map/ppermute | solution.py:429
  194.6 10.0 %collective-permute-start.14 = (f32[64,128]{1,0:T(8,128)}, f32[64,128]{1,0:T(8,128)S(1)}, u32[]{:S(2)}, u32[]{:S(2)}) collective-permute-start(f32[64,128]{1,0:T(8,128)} %get-tuple-element.34), channel_id=1, source_target_pairs={{0,6},{6,0},{1,7},{7,1},{4,2},{2,4},{5,3},{3,5},{8,14},{14,8},{9,1... | collective-permute-start | bytes 98312 | tf_op jit(solution)/shard_map/ppermute | solution.py:429
  204.6 0.6 copy-start.6
  204.6 0.6 copy-start.7
  204.6 0.6 copy-start.8
  204.6 0.9 copy-start
  204.6 1.1 copy-start.1
  211.4 14.7 %collective-permute-start.17 = (f32[2,256,128]{2,1,0:T(8,128)}, f32[2,256,128]{2,1,0:T(8,128)S(1)}, u32[]{:S(2)}, u32[]{:S(2)}) collective-permute-start(f32[2,256,128]{2,1,0:T(8,128)} %get-tuple-element.35), channel_id=1, source_target_pairs={{0,0},{1,2},{6,1},{7,3},{4,4},{5,6},{2,5},{3,7},{8,8},{9,10},{14,9... | collective-permute-start | bytes 786440 | tf_op jit(solution)/shard_map/ppermute | solution.py:441
  214.4 11.7 %collective-permute-start.18 = (f32[2,256,128]{2,1,0:T(8,128)}, f32[2,256,128]{2,1,0:T(8,128)S(1)}, u32[]{:S(2)}, u32[]{:S(2)}) collective-permute-start(f32[2,256,128]{2,1,0:T(8,128)} %get-tuple-element.36), channel_id=1, source_target_pairs={{0,1},{1,3},{6,0},{7,2},{4,5},{5,7},{2,4},{3,6},{8,9},{9,11},{14,8... | collective-permute-start | bytes 786440 | tf_op jit(solution)/shard_map/ppermute | solution.py:442

commit v7 on v6

--- a/solution.py
+++ b/solution.py
@@ -153,7 +153,9 @@
     return jnp.concatenate(parts, axis=0)
 
 
-def planes_kernel(cut_ref, kz_ref, own_ref, up_ref, down_ref, y_ref, x_ref, out_ref, sh, sl, radius):
+def planes_kernel(
+    cut_ref, kz_ref, own_ref, up_ref, down_ref, y_ref, x_ref, out_ref, sh, sl, radius, ready, done
+):
     alone = kz_ref[0] == 0
     for i in range(16):
         c, r = divmod(i, TILE_ROWS)
@@ -215,8 +217,12 @@
                 else:
                     halves = [jnp.where(upper, units[q], pltpu.roll(units[q + 2], 4, 1)) for q in range(2)]
                 goal = 2 * (2 * (odd_block ^ side) + side)
-                out_ref[:, goal, pair] = jnp.where(even_unit, halves[0], pltpu.roll(halves[1], 2, 1))
-                out_ref[:, goal + 1, pair] = jnp.where(even_unit, pltpu.roll(halves[0], 6, 1), halves[1])
+                ready[pair, :, goal] = jnp.where(even_unit, halves[0], pltpu.roll(halves[1], 2, 1))
+                ready[pair, :, goal + 1] = jnp.where(even_unit, pltpu.roll(halves[0], 6, 1), halves[1])
+        pltpu.make_async_copy(ready.at[pair], out_ref.at[:, :, pair], done.at[pair]).start()
+
+    for pair in range(BANDS // 2):
+        pltpu.make_async_copy(ready.at[pair], out_ref.at[:, :, pair], done.at[pair]).wait()
 
 
 def depth_kernel(come_ref, z_ref, low_half_ref, high_half_ref, first_ref, second_ref, edge_ref, edge):
@@ -292,7 +298,7 @@
             right = pltpu.roll(jnp.where(lane == 0, beyond, tall), LANES - 1, 1)
             wide = tall + left + right
             full = wide + pltpu.roll(wide, 1, 0) + pltpu.roll(wide, BOX - 1, 0)
-            weight = 1.0 / (full / 27.0 + error_floor)
+            weight = 1.0 / (full + 27.0 * error_floor)
             low = low + weight * low_half_ref[i, row]
             high = high + weight * high_half_ref[i, row]
             total = total + weight
@@ -396,11 +402,17 @@
     constants = [jnp.asarray(t) for t in tables()]
     sent = pl.pallas_call(
         planes_kernel,
-        out_shape=jax.ShapeDtypeStruct((SENDERS // 4, 8, BANDS // 2, 8, LANES), f32),
+        out_shape=pltpu.HBM((SENDERS // 4, 8, BANDS // 2, 8, LANES), f32),
         in_specs=[SMEM, SMEM] + [VMEM] * 5,
-        out_specs=VMEM,
-        scratch_shapes=[pltpu.VMEM((2 * BOX, BOX), bf16)] * 2 + [pltpu.VMEM((BOX, BOX), f32)],
+        out_specs=pl.BlockSpec(memory_space=pltpu.HBM),
+        scratch_shapes=[pltpu.VMEM((2 * BOX, BOX), bf16)] * 2
+        + [
+            pltpu.VMEM((BOX, BOX), f32),
+            pltpu.VMEM((BANDS // 2, SENDERS // 4, 8, 8, LANES), f32),
+            pltpu.SemaphoreType.DMA((BANDS // 2,)),
+        ],
         name="planes",
+        compiler_params=pltpu.CompilerParams(vmem_limit_bytes=16 * 2**20),
     )(cutoffs, plane, own, rise, sink, *constants[:2])
     gathered = lax.all_to_all(sent.reshape(2 * SENDERS, PER, LANES), everyone, split_axis=0, concat_axis=0, tiled=True)
     gathered = gathered.reshape(2 * SENDERS * PER, LANES)
@@ -423,6 +435,7 @@
         out_specs=(rows_spec, rows_spec, row_spec, row_spec, edge_spec),
         scratch_shapes=[pltpu.VMEM((BOX, LANES), f32)],
         name="depth",
+        compiler_params=pltpu.CompilerParams(vmem_limit_bytes=20 * 2**20),
     )(gathered, constants[2])
     before = lax.ppermute(second, everyone, row_pairs(1, 0))
     after = lax.ppermute(first, everyone, row_pairs(-1, 0))
@@ -437,6 +450,7 @@
         out_specs=(block_spec, block_spec),
         scratch_shapes=[pltpu.VMEM((2, 3, BOX, LANES), f32), pltpu.VMEM((2, BOX, LANES), f32)],
         name="blend",
+        compiler_params=pltpu.CompilerParams(vmem_limit_bytes=16 * 2**20),
     )(side_flag, low_half, high_half, first, second, before, after, *edges)
     near = lax.ppermute(near, everyone, home_pairs(0))
     far = lax.ppermute(far, everyone, home_pairs(1))

time: 228 us -> 222 us (0.974)
  Pallas kernels: 24 us -> 18.8 us
    pallas_call x1, Pallas kernels: 6.15 us -> 3.6 us  [on_device(): pl.pallas_call(depth_kernel, grid=(BANDS // 2,), out_shape=(rows_shape, r...]
  transfers between devices with their start and end apart: 19 -> 19, of which waited for: 10 -> 10; matrix products, arithmetic and copies ran while one was open for 0% -> 1% of each run, Pallas kernels for 0% -> 0%
where the time goes in v7:
time: 222 us; the launch traced here: 221 us
  blocking collectives  93.7 us (42%)
  waiting for transfers between devices  67.6 us (30%)
  starting transfers between devices  38.2 us (17%)
  Pallas kernels  18.8 us (8%)
    all_to_all x1, blocking collectives, on_device(): lax.all_to_all(sent.reshape(2 * SENDERS, PER, LANES), everyone, split_axi...  93.7 us
    ppermute x12, waiting for transfers between devices, send(): return lax.ppermute(part, here, pairs)  47.2 us
    ppermute x12, starting transfers between devices, send(): return lax.ppermute(part, here, pairs)  30.5 us
    ppermute x1, waiting for transfers between devices, on_device(): near = lax.ppermute(near, everyone, home_pairs(0))  11.2 us
    ppermute x3, waiting for transfers between devices, on_device(): edges = [lax.ppermute(edge, everyone, row_pairs(n, 1)) for n in (0, 1, -1)]  9.18 us
    pallas_call x1, Pallas kernels, on_device(): pl.pallas_call(planes_kernel, out_shape=pltpu.HBM((SENDERS // 4, 8, BANDS...  5.57 us
    pallas_call x1, Pallas kernels, on_device(): pl.pallas_call(place_kernel, grid=(2,), out_shape=tuple((jax.ShapeDtypeSt...  4.94 us
    pallas_call x1, Pallas kernels, on_device(): pl.pallas_call(blend_kernel, grid=(steps,), out_shape=(block_shape, block...  4.74 us
  transfers between devices with their start and end apart: 19, of which 10 were waited for; matrix products, arithmetic and copies ran while one was open for 1% of the time, Pallas kernels for 0%

profile of v7, /device:TPU:1, one launch (start us, length us, event | category | flops | bytes accessed | tf_op | source)
XLA Modules:
  0.0 221.1 jit_solution(4256866860837192941)
XLA Ops:
  0.0 4.9 %place.1 = (f32[32,4096]{1,0:T(8,128)}, f32[32,4096]{1,0:T(8,128)}, f32[16,4096]{1,0:T(8,128)}, f32[16,4096]{1,0:T(8,128)}, f32[32,4096]{1,0:T(8,128)}, /*index=...) custom-call(s32[1]{0:T(128)} %bitcast.1.slab_ref, s32[1]{0:T(128)} %bitcast.2.group_ref, ...), custom_call_target="tpu_custom_call" | custom-call | tf_op jit(solution)/shard_map/place/pallas_call | solution.py:368
  4.9 5.8 %collective-permute-start.1 = (f32[32,4096]{1,0:T(8,128)}, f32[32,4096]{1,0:T(8,128)S(1)}, u32[]{:S(2)}, u32[]{:S(2)}) collective-permute-start(f32[32,4096]{1,0:T(8,128)} %get-tuple-element.24), channel_id=1, source_target_pairs={{0,60},{4,56},{8,52},{12,48},{16,44},{20,40},{24,36},{28,32},{32,2... | collective-permute-start | bytes 1572872 | tf_op jit(solution)/shard_map/ppermute | solution.py:391
  10.7 1.6 collective-permute-start.2
  12.4 3.9 %collective-permute-start.8 = (f32[16,4096]{1,0:T(8,128)}, f32[16,4096]{1,0:T(8,128)S(1)}, u32[]{:S(2)}, u32[]{:S(2)}) collective-permute-start(f32[16,4096]{1,0:T(8,128)} %get-tuple-element.29), channel_id=1, source_target_pairs={{0,194},{4,198},{8,202},{12,206},{16,210},{20,214},{24,218},{28,22... | collective-permute-start | bytes 786440 | tf_op jit(solution)/shard_map/ppermute | solution.py:391
  16.3 0.0 copy-start.8
  16.3 0.0 copy-start.6
  16.3 0.2 collective-permute-start.7
  16.5 5.7 %collective-permute-done.2 = f32[16,4096]{1,0:T(8,128)S(1)} collective-permute-done((f32[16,4096]{1,0:T(8,128)}, f32[16,4096]{1,0:T(8,128)S(1)}, u32[]{:S(2)}, u32[]{:S(2)}) %collective-permute-start.2) | collective-permute-done | bytes 262176 | tf_op jit(solution)/shard_map/ppermute | solution.py:391
  22.2 0.0 collective-permute-done.1
  22.3 0.0 copy-start.5
  22.3 1.9 collective-permute-start.3
  24.3 0.0 collective-permute-done.8
  24.3 9.5 %collective-permute-done.7 = f32[32,4096]{1,0:T(8,128)S(1)} collective-permute-done((f32[32,4096]{1,0:T(8,128)}, f32[32,4096]{1,0:T(8,128)S(1)}, u32[]{:S(2)}, u32[]{:S(2)}) %collective-permute-start.7) | collective-permute-done | bytes 524320 | tf_op jit(solution)/shard_map/ppermute | solution.py:391
  33.9 5.5 %collective-permute-start.9 = (f32[32,4096]{1,0:T(8,128)S(1)}, f32[32,4096]{1,0:T(8,128)S(1)}, u32[]{:S(2)}, u32[]{:S(2)}) collective-permute-start(f32[32,4096]{1,0:T(8,128)S(1)} %pad_maximum_fusion.1), channel_id=1, source_target_pairs={{0,194},{4,198},{8,202},{12,206},{16,210},{20,214},{24,218},{28,22... | collective-permute-start | bytes 1572872 | tf_op jit(solution)/shard_map/ppermute | solution.py:391
  39.4 0.0 copy-done.8
  39.4 4.6 %collective-permute-start = (f32[32,4096]{1,0:T(8,128)S(1)}, f32[32,4096]{1,0:T(8,128)S(1)}, u32[]{:S(2)}, u32[]{:S(2)}) collective-permute-start(f32[32,4096]{1,0:T(8,128)S(1)} %copy-done.8), channel_id=1, source_target_pairs={{0,60},{4,56},{8,52},{12,48},{16,44},{20,40},{24,36},{28,32},{32,1... | collective-permute-start | bytes 1572872 | tf_op jit(solution)/shard_map/ppermute | solution.py:391
  44.0 0.0 copy-done.7
  44.1 1.9 collective-permute-start.6
  46.0 0.0 collective-permute-done.3
  46.0 0.0 copy-done.6
  46.0 0.1 add.32
  46.1 0.1 collective-permute-start.4
  46.2 3.1 %collective-permute-done.9 = f32[32,4096]{1,0:T(8,128)S(1)} collective-permute-done((f32[32,4096]{1,0:T(8,128)S(1)}, f32[32,4096]{1,0:T(8,128)S(1)}, u32[]{:S(2)}, u32[]{:S(2)}) %collective-permute-start.9) | collective-permute-done | bytes 524320 | tf_op jit(solution)/shard_map/ppermute | solution.py:391
  49.3 0.0 copy-done.5
  49.3 0.0 copy-start
  49.3 0.0 copy-start.2
  49.3 0.0 copy-start.4
  49.3 0.1 add.35
  49.4 3.5 %collective-permute-start.10 = (f32[32,4096]{1,0:T(8,128)S(1)}, f32[32,4096]{1,0:T(8,128)S(1)}, u32[]{:S(2)}, u32[]{:S(2)}) collective-permute-start(f32[32,4096]{1,0:T(8,128)S(1)} %add.35), channel_id=1, source_target_pairs={{0,194},{4,198},{8,202},{12,206},{16,210},{20,214},{24,218},{28,22... | collective-permute-start | bytes 1572872 | tf_op jit(solution)/shard_map/ppermute | solution.py:391
  52.9 3.8 %collective-permute-done = f32[32,4096]{1,0:T(8,128)S(1)} collective-permute-done((f32[32,4096]{1,0:T(8,128)S(1)}, f32[32,4096]{1,0:T(8,128)S(1)}, u32[]{:S(2)}, u32[]{:S(2)}) %collective-permute-start) | collective-permute-done | bytes 524320 | tf_op jit(solution)/shard_map/ppermute | solution.py:391
  56.7 2.8 %collective-permute-done.4 = f32[32,4096]{1,0:T(8,128)S(1)} collective-permute-done((f32[32,4096]{1,0:T(8,128)S(1)}, f32[32,4096]{1,0:T(8,128)S(1)}, u32[]{:S(2)}, u32[]{:S(2)}) %collective-permute-start.4) | collective-permute-done | bytes 524320 | tf_op jit(solution)/shard_map/ppermute | solution.py:391
  59.5 0.1 add.33
  59.6 0.1 collective-permute-start.5
  59.7 10.2 %collective-permute-done.6 = f32[32,4096]{1,0:T(8,128)S(1)} collective-permute-done((f32[32,4096]{1,0:T(8,128)S(1)}, f32[32,4096]{1,0:T(8,128)S(1)}, u32[]{:S(2)}, u32[]{:S(2)}) %collective-permute-start.6) | collective-permute-done | bytes 524320 | tf_op jit(solution)/shard_map/ppermute | solution.py:391
  69.9 0.0 collective-permute-done.10
  69.9 0.8 add.36
  70.8 1.3 collective-permute-start.11
  72.0 7.5 %collective-permute-done.5.up_ref = f32[32,4096]{1,0:T(8,128)S(1)} collective-permute-done((f32[32,4096]{1,0:T(8,128)S(1)}, f32[32,4096]{1,0:T(8,128)S(1)}, u32[]{:S(2)}, u32[]{:S(2)}) %collective-permute-start.5) | collective-permute-done | bytes 524320 | tf_op jit(solution)/shard_map/ppermute | solution.py:391
  79.5 4.4 %collective-permute-done.11.down_ref = f32[32,4096]{1,0:T(8,128)S(1)} collective-permute-done((f32[32,4096]{1,0:T(8,128)}, f32[32,4096]{1,0:T(8,128)S(1)}, u32[]{:S(2)}, u32[]{:S(2)}) %collective-permute-start.11) | collective-permute-done | bytes 524320 | tf_op jit(solution)/shard_map/ppermute | solution.py:391
  84.0 0.0 copy-done
  84.0 0.0 copy-done.1
  84.0 0.0 copy-done.2
  84.0 0.0 copy-done.4
  84.0 5.6 %planes.1 = f32[32,8,3,8,128]{4,3,2,1,0:T(8,128)} custom-call(s32[6]{0:T(128)S(1)} %copy-done.4, s32[1]{0:T(128)} %bitcast.kz_ref, f32[32,4096]{1,0:T(8,128)S(1)} %copy-done.2, f32[32,4096]{1,0:T(8,128)S(1)} %collective-permute-done.5.up_ref, f32[32,4096]{1,0:T(8,128)S(1)} %collective-permute-done.11.down_ref, bf16[2,2,256,256]{3,2,1,0:T(8,128)(2,1)S(1)} %copy-done.1, ...), custom_call_target="tpu_custom_call" | custom-call | tf_op jit(solution)/shard_map/planes/pallas_call | solution.py:403
  89.6 0.0 copy-start.3
  89.6 93.7 %all_to_all.5 = f32[256,24,128]{2,1,0:T(8,128)S(1)} all-to-all(f32[256,24,128]{2,1,0:T(8,128)} %bitcast.14), channel_id=1, replica_groups=mesh['particle'=4,'slab'=32,'half'=2] {'particle','slab','half'}, dimensions={0} | all-to-all | bytes 6291456 | tf_op jit(solution)/shard_map/all_to_all | solution.py:417
  183.3 0.0 copy-done.3
  183.3 3.6 %depth.1 = (f32[6,2,256,128]{3,2,1,0:T(8,128)S(1)}, f32[6,2,256,128]{3,2,1,0:T(8,128)S(1)}, f32[6,256,128]{2,1,0:T(8,128)}, f32[6,256,128]{2,1,0:T(8,128)}, f32[64,128]{1,0:T(8,128)S(1)}) custom-call(f32[6144,128]{1,0:T(8,128)S(1)} %bitcast.13, bf16[2,256,256]{2,1,0:T(8,128)(2,1)S(1)} %copy-done.3), custom_call_target="tpu_custom_call" | custom-call | tf_op jit(solution)/shard_map/depth/pallas_call | solution.py:427
  186.9 0.0 collective-permute-start.13
  186.9 1.7 collective-permute-start.12
  188.6 0.0 collective-permute-start.16
  188.6 1.7 collective-permute-start.15
  190.4 0.9 collective-permute-start.14
  191.3 9.2 %collective-permute-done.16.edge_after_ref = f32[64,128]{1,0:T(8,128)S(1)} collective-permute-done((f32[64,128]{1,0:T(8,128)S(1)}, f32[64,128]{1,0:T(8,128)S(1)}, u32[]{:S(2)}, u32[]{:S(2)}) %collective-permute-start.16) | collective-permute-done | bytes 32800 | tf_op jit(solution)/shard_map/ppermute | solution.py:442
  200.5 0.0 collective-permute-done.15.edge_before_ref
  200.5 0.0 collective-permute-done.14.edge_ref
  200.5 0.0 collective-permute-done.13.after_ref
  200.5 0.0 collective-permute-done.12.before_ref
  200.5 4.7 %blend.1 = (f32[2,256,128]{2,1,0:T(8,128)}, f32[2,256,128]{2,1,0:T(8,128)S(1)}) custom-call(s32[128]{0:T(128)S(1)} %compare_select_fusion.side_ref, f32[6,2,256,128]{3,2,1,0:T(8,128)S(1)} %get-tuple-element.30.low_half_ref, f32[6,2,256,128]{3,2,1,0:T(8,128)S(1)} %get-tuple-element.31.high_half_ref, f32[6,256,128]{2,1,0:T(8,128)} %get-tuple-element.32.first_ref, ...), custom_call_target="tpu_custom_call" | custom-call | tf_op jit(solution)/shard_map/blend/pallas_call | solution.py:445
  205.2 3.2 %collective-permute-start.17 = (f32[2,256,128]{2,1,0:T(8,128)}, f32[2,256,128]{2,1,0:T(8,128)S(1)}, u32[]{:S(2)}, u32[]{:S(2)}) collective-permute-start(f32[2,256,128]{2,1,0:T(8,128)} %get-tuple-element.35), channel_id=1, source_target_pairs={{0,0},{1,2},{6,1},{7,3},{4,4},{5,6},{2,5},{3,7},{8,8},{9,10},{14,9... | collective-permute-start | bytes 786440 | tf_op jit(solution)/shard_map/ppermute | solution.py:455
  208.5 0.1 collective-permute-start.18
  208.6 11.2 %collective-permute-done.17 = f32[2,256,128]{2,1,0:T(8,128)S(1)} collective-permute-done((f32[2,256,128]{2,1,0:T(8,128)}, f32[2,256,128]{2,1,0:T(8,128)S(1)}, u32[]{:S(2)}, u32[]{:S(2)}) %collective-permute-start.17) | collective-permute-done | bytes 262176 | tf_op jit(solution)/shard_map/ppermute | solution.py:455
  219.8 0.0 collective-permute-done.18
  219.9 1.2 copy.9
  (9 shorter events, 0.2 us)
Async XLA Ops:
  4.9 17.3 %collective-permute-start.1 = (f32[32,4096]{1,0:T(8,128)}, f32[32,4096]{1,0:T(8,128)S(1)}, u32[]{:S(2)}, u32[]{:S(2)}) collective-permute-start(f32[32,4096]{1,0:T(8,128)} %get-tuple-element.24), channel_id=1, source_target_pairs={{0,60},{4,56},{8,52},{12,48},{16,44},{20,40},{24,36},{28,32},{32,2... | collective-permute-start | bytes 1572872 | tf_op jit(solution)/shard_map/ppermute | solution.py:391
  10.7 11.5 %collective-permute-start.2 = (f32[16,4096]{1,0:T(8,128)}, f32[16,4096]{1,0:T(8,128)S(1)}, u32[]{:S(2)}, u32[]{:S(2)}) collective-permute-start(f32[16,4096]{1,0:T(8,128)} %get-tuple-element.25), channel_id=1, source_target_pairs={{0,2},{4,6},{8,10},{12,14},{16,18},{20,22},{24,26},{28,30},{32,34}... | collective-permute-start | bytes 786440 | tf_op jit(solution)/shard_map/ppermute | solution.py:391
  12.4 11.9 %collective-permute-start.8 = (f32[16,4096]{1,0:T(8,128)}, f32[16,4096]{1,0:T(8,128)S(1)}, u32[]{:S(2)}, u32[]{:S(2)}) collective-permute-start(f32[16,4096]{1,0:T(8,128)} %get-tuple-element.29), channel_id=1, source_target_pairs={{0,194},{4,198},{8,202},{12,206},{16,210},{20,214},{24,218},{28,22... | collective-permute-start | bytes 786440 | tf_op jit(solution)/shard_map/ppermute | solution.py:391
  16.3 23.1 %copy-start.8 = (f32[32,4096]{1,0:T(8,128)S(1)}, f32[32,4096]{1,0:T(8,128)}, u32[]{:S(2)}) copy-start(f32[32,4096]{1,0:T(8,128)} %get-tuple-element.22) | copy-start | bytes 1572868
  16.3 27.7 %copy-start.7 = (f32[32,4096]{1,0:T(8,128)S(1)}, f32[32,4096]{1,0:T(8,128)}, u32[]{:S(2)}) copy-start(f32[32,4096]{1,0:T(8,128)} %get-tuple-element.26) | copy-start | bytes 1572868
  16.3 29.7 %copy-start.6 = (f32[32,4096]{1,0:T(8,128)S(1)}, f32[32,4096]{1,0:T(8,128)}, u32[]{:S(2)}) copy-start(f32[32,4096]{1,0:T(8,128)} %get-tuple-element.23) | copy-start | bytes 1572868
  16.3 17.5 %collective-permute-start.7 = (f32[32,4096]{1,0:T(8,128)}, f32[32,4096]{1,0:T(8,128)S(1)}, u32[]{:S(2)}, u32[]{:S(2)}) collective-permute-start(f32[32,4096]{1,0:T(8,128)} %get-tuple-element.28), channel_id=1, source_target_pairs={{0,60},{4,56},{8,52},{12,48},{16,44},{20,40},{24,36},{28,32},{32,2... | collective-permute-start | bytes 1572872 | tf_op jit(solution)/shard_map/ppermute | solution.py:391
  22.3 27.0 %copy-start.5 = (f32[32,4096]{1,0:T(8,128)S(1)}, f32[32,4096]{1,0:T(8,128)}, u32[]{:S(2)}) copy-start(f32[32,4096]{1,0:T(8,128)} %get-tuple-element.27) | copy-start | bytes 1572868
  22.3 23.7 %collective-permute-start.3 = (f32[32,4096]{1,0:T(8,128)S(1)}, f32[32,4096]{1,0:T(8,128)S(1)}, u32[]{:S(2)}, u32[]{:S(2)}) collective-permute-start(f32[32,4096]{1,0:T(8,128)S(1)} %pad_maximum_fusion), channel_id=1, source_target_pairs={{0,2},{4,6},{8,10},{12,14},{16,18},{20,22},{24,26},{28,30},{32,34}... | collective-permute-start | bytes 1572872 | tf_op jit(solution)/shard_map/ppermute | solution.py:391
  33.9 15.4 %collective-permute-start.9 = (f32[32,4096]{1,0:T(8,128)S(1)}, f32[32,4096]{1,0:T(8,128)S(1)}, u32[]{:S(2)}, u32[]{:S(2)}) collective-permute-start(f32[32,4096]{1,0:T(8,128)S(1)} %pad_maximum_fusion.1), channel_id=1, source_target_pairs={{0,194},{4,198},{8,202},{12,206},{16,210},{20,214},{24,218},{28,22... | collective-permute-start | bytes 1572872 | tf_op jit(solution)/shard_map/ppermute | solution.py:391
  39.4 17.3 %collective-permute-start = (f32[32,4096]{1,0:T(8,128)S(1)}, f32[32,4096]{1,0:T(8,128)S(1)}, u32[]{:S(2)}, u32[]{:S(2)}) collective-permute-start(f32[32,4096]{1,0:T(8,128)S(1)} %copy-done.8), channel_id=1, source_target_pairs={{0,60},{4,56},{8,52},{12,48},{16,44},{20,40},{24,36},{28,32},{32,1... | collective-permute-start | bytes 1572872 | tf_op jit(solution)/shard_map/ppermute | solution.py:391
  44.1 25.9 %collective-permute-start.6 = (f32[32,4096]{1,0:T(8,128)S(1)}, f32[32,4096]{1,0:T(8,128)S(1)}, u32[]{:S(2)}, u32[]{:S(2)}) collective-permute-start(f32[32,4096]{1,0:T(8,128)S(1)} %copy-done.7), channel_id=1, source_target_pairs={{0,60},{4,56},{8,52},{12,48},{16,44},{20,40},{24,36},{28,32},{32,2... | collective-permute-start | bytes 1572872 | tf_op jit(solution)/shard_map/ppermute | solution.py:391
  46.1 13.4 %collective-permute-start.4 = (f32[32,4096]{1,0:T(8,128)S(1)}, f32[32,4096]{1,0:T(8,128)S(1)}, u32[]{:S(2)}, u32[]{:S(2)}) collective-permute-start(f32[32,4096]{1,0:T(8,128)S(1)} %add.32), channel_id=1, source_target_pairs={{0,2},{4,6},{8,10},{12,14},{16,18},{20,22},{24,26},{28,30},{32,34}... | collective-permute-start | bytes 1572872 | tf_op jit(solution)/shard_map/ppermute | solution.py:391
  49.3 34.7 %copy-start = (bf16[2,2,256,256]{3,2,1,0:T(8,128)(2,1)S(1)}, bf16[2,2,256,256]{3,2,1,0:T(8,128)(2,1)}, u32[]{:S(2)}) copy-start(bf16[2,2,256,256]{3,2,1,0:T(8,128)(2,1)} %constant.40.clone.x_ref) | copy-start | bytes 1572868
  49.3 34.7 %copy-start.1 = (bf16[2,2,256,256]{3,2,1,0:T(8,128)(2,1)S(1)}, bf16[2,2,256,256]{3,2,1,0:T(8,128)(2,1)}, u32[]{:S(2)}) copy-start(bf16[2,2,256,256]{3,2,1,0:T(8,128)(2,1)} %constant.39.clone.y_ref) | copy-start | bytes 1572868
  49.3 34.7 %copy-start.2 = (f32[32,4096]{1,0:T(8,128)S(1)}, f32[32,4096]{1,0:T(8,128)}, u32[]{:S(2)}) copy-start(f32[32,4096]{1,0:T(8,128)} %get-tuple-element.21.own_ref) | copy-start | bytes 1572868
  49.3 34.7 %copy-start.4 = (s32[6]{0:T(128)S(1)}, s32[6]{0:T(128)}, u32[]{:S(2)}) copy-start(s32[6]{0:T(128)} %cut_ref.1) | copy-start | bytes 76
  49.4 20.5 %collective-permute-start.10 = (f32[32,4096]{1,0:T(8,128)S(1)}, f32[32,4096]{1,0:T(8,128)S(1)}, u32[]{:S(2)}, u32[]{:S(2)}) collective-permute-start(f32[32,4096]{1,0:T(8,128)S(1)} %add.35), channel_id=1, source_target_pairs={{0,194},{4,198},{8,202},{12,206},{16,210},{20,214},{24,218},{28,22... | collective-permute-start | bytes 1572872 | tf_op jit(solution)/shard_map/ppermute | solution.py:391
  59.6 19.9 %collective-permute-start.5 = (f32[32,4096]{1,0:T(8,128)S(1)}, f32[32,4096]{1,0:T(8,128)S(1)}, u32[]{:S(2)}, u32[]{:S(2)}) collective-permute-start(f32[32,4096]{1,0:T(8,128)S(1)} %add.33), channel_id=1, source_target_pairs={{0,2},{4,6},{8,10},{12,14},{16,18},{20,22},{24,26},{28,30},{32,34}... | collective-permute-start | bytes 1572872 | tf_op jit(solution)/shard_map/ppermute | solution.py:391
  70.8 13.2 %collective-permute-start.11 = (f32[32,4096]{1,0:T(8,128)}, f32[32,4096]{1,0:T(8,128)S(1)}, u32[]{:S(2)}, u32[]{:S(2)}) collective-permute-start(f32[32,4096]{1,0:T(8,128)} %add.36), channel_id=1, source_target_pairs={{0,194},{4,198},{8,202},{12,206},{16,210},{20,214},{24,218},{28,22... | collective-permute-start | bytes 1572872 | tf_op jit(solution)/shard_map/ppermute | solution.py:391
  89.6 93.7 %copy-start.3 = (bf16[2,256,256]{2,1,0:T(8,128)(2,1)S(1)}, bf16[2,256,256]{2,1,0:T(8,128)(2,1)}, u32[]{:S(2)}) copy-start(bf16[2,256,256]{2,1,0:T(8,128)(2,1)} %constant.41.clone.z_ref) | copy-start | bytes 786436
  186.9 13.6 %collective-permute-start.13 = (f32[6,256,128]{2,1,0:T(8,128)}, f32[6,256,128]{2,1,0:T(8,128)}, u32[]{:S(2)}, u32[]{:S(2)}) collective-permute-start(f32[6,256,128]{2,1,0:T(8,128)} %get-tuple-element.32.first_ref), channel_id=1, source_target_pairs={{0,253},{6,251},{1,0},{7,6},{4,1},{2,7},{5,4},{3,2},{8,5},{14,3},{... | collective-permute-start | bytes 2359304 | tf_op jit(solution)/shard_map/ppermute | solution.py:441
  186.9 13.6 %collective-permute-start.12 = (f32[6,256,128]{2,1,0:T(8,128)}, f32[6,256,128]{2,1,0:T(8,128)}, u32[]{:S(2)}, u32[]{:S(2)}) collective-permute-start(f32[6,256,128]{2,1,0:T(8,128)} %get-tuple-element.33.second_ref), channel_id=1, source_target_pairs={{0,1},{6,7},{1,4},{7,2},{4,5},{2,3},{5,8},{3,14},{8,9},{14,15},{9,... | collective-permute-start | bytes 2359304 | tf_op jit(solution)/shard_map/ppermute | solution.py:440
  188.6 11.9 %collective-permute-start.16 = (f32[64,128]{1,0:T(8,128)S(1)}, f32[64,128]{1,0:T(8,128)S(1)}, u32[]{:S(2)}, u32[]{:S(2)}) collective-permute-start(f32[64,128]{1,0:T(8,128)S(1)} %get-tuple-element.34), channel_id=1, source_target_pairs={{0,251},{6,253},{1,6},{7,0},{4,7},{2,1},{5,2},{3,4},{8,3},{14,5},{... | collective-permute-start | bytes 98312 | tf_op jit(solution)/shard_map/ppermute | solution.py:442
  188.6 11.9 %collective-permute-start.15 = (f32[64,128]{1,0:T(8,128)S(1)}, f32[64,128]{1,0:T(8,128)S(1)}, u32[]{:S(2)}, u32[]{:S(2)}) collective-permute-start(f32[64,128]{1,0:T(8,128)S(1)} %get-tuple-element.34), channel_id=1, source_target_pairs={{0,7},{6,1},{1,2},{7,4},{4,3},{2,5},{5,14},{3,8},{8,15},{14,9},{9,... | collective-permute-start | bytes 98312 | tf_op jit(solution)/shard_map/ppermute | solution.py:442
  190.4 10.1 %collective-permute-start.14 = (f32[64,128]{1,0:T(8,128)S(1)}, f32[64,128]{1,0:T(8,128)S(1)}, u32[]{:S(2)}, u32[]{:S(2)}) collective-permute-start(f32[64,128]{1,0:T(8,128)S(1)} %get-tuple-element.34), channel_id=1, source_target_pairs={{0,6},{6,0},{1,7},{7,1},{4,2},{2,4},{5,3},{3,5},{8,14},{14,8},{9,1... | collective-permute-start | bytes 98312 | tf_op jit(solution)/shard_map/ppermute | solution.py:442
  205.2 14.5 %collective-permute-start.17 = (f32[2,256,128]{2,1,0:T(8,128)}, f32[2,256,128]{2,1,0:T(8,128)S(1)}, u32[]{:S(2)}, u32[]{:S(2)}) collective-permute-start(f32[2,256,128]{2,1,0:T(8,128)} %get-tuple-element.35), channel_id=1, source_target_pairs={{0,0},{1,2},{6,1},{7,3},{4,4},{5,6},{2,5},{3,7},{8,8},{9,10},{14,9... | collective-permute-start | bytes 786440 | tf_op jit(solution)/shard_map/ppermute | solution.py:455
  208.5 11.3 %collective-permute-start.18 = (f32[2,256,128]{2,1,0:T(8,128)S(1)}, f32[2,256,128]{2,1,0:T(8,128)S(1)}, u32[]{:S(2)}, u32[]{:S(2)}) collective-permute-start(f32[2,256,128]{2,1,0:T(8,128)S(1)} %get-tuple-element.36), channel_id=1, source_target_pairs={{0,1},{1,3},{6,0},{7,2},{4,5},{5,7},{2,4},{3,6},{8,9},{9,11},{14,8... | collective-permute-start | bytes 786440 | tf_op jit(solution)/shard_map/ppermute | solution.py:456

commit v8 on v7

--- a/solution.py
+++ b/solution.py
@@ -43,10 +43,10 @@
     for odd in range(2):
         turn = angles(near, near % BLOCKS * TILE_ROWS + near // BLOCKS * 2 + odd)
         cosine, sine = np.cos(turn), np.sin(turn)
-        along_y.append(np.stack(split(np.block([[cosine, -sine], [sine, cosine]]))))
+        along_y.append(np.stack(split(np.concatenate([cosine, sine], axis=1))))
         turn = angles(2 * near + odd, near)
         cosine, sine = np.cos(turn), np.sin(turn)
-        along_x.append(np.stack(split(np.block([[cosine, sine], [-sine, cosine]]))))
+        along_x.append(np.stack(split(np.concatenate([cosine, sine], axis=1))))
     along_y, along_x = np.stack(along_y), np.stack(along_x)
     sender = np.arange(SENDERS)
     group, slab = sender // SLABS, sender % SLABS
@@ -72,7 +72,7 @@
 
 
 def place_kernel(slab_ref, group_ref, index_ref, bin_ref, gain_ref, tile_ref, *refs):
-    outs, (kept_mark, sent_mark, sent_mark_first, turn, moved, saved) = refs[:9], refs[9:]
+    outs, (kept_mark, sent_mark, sent_mark_first, turn, moved, saved) = refs[:15], refs[15:]
     step = pl.program_id(0)
     slab, group = slab_ref[0], group_ref[0]
     depth, late = group * 2 + slab % 2, slab // (SLABS // 2)
@@ -140,7 +140,7 @@
             if r == 0:
                 alone = jnp.where(first & (step == 1), last_sent[i * BLOCKS : (i + 1) * BLOCKS], 0.0)
             parts.append(jnp.where((slab == SLABS // 2) & (sent_line[i] == 0), alone, part))
-        parts[2:3] = [parts[2][: BLOCKS // 2], parts[2][BLOCKS // 2 :]]
+        parts = parts[:1] + [part[start : start + BLOCKS // 2] for part in parts[1:] for start in (0, BLOCKS // 2)]
         for out_ref, part in zip(outs, parts):
             out_ref[:, cols] = part
 
@@ -154,14 +154,21 @@
 
 
 def planes_kernel(
-    cut_ref, kz_ref, own_ref, up_ref, down_ref, y_ref, x_ref, out_ref, sh, sl, radius, ready, done
+    cut_ref, kz_ref, own_ref, up_a_ref, up_b_ref, down_a_ref, down_b_ref, few_y_ref, few_x_ref, out_ref, sh, sl, radius, ready, done, y_ref, x_ref
 ):
+    for odd in range(2):
+        for part in range(2):
+            cosine, sine = few_y_ref[odd, part, :, :HALF], few_y_ref[odd, part, :, HALF:]
+            y_ref[odd, part] = above(beside(cosine, -sine), beside(sine, cosine))
+            cosine, sine = few_x_ref[odd, part, :, :HALF], few_x_ref[odd, part, :, HALF:]
+            x_ref[odd, part] = above(beside(cosine, sine), beside(-sine, cosine))
     alone = kz_ref[0] == 0
     for i in range(16):
         c, r = divmod(i, TILE_ROWS)
         cols = pl.ds(i * BOX, BOX)
         rows = pl.ds(r % 2 * BOX + c * HALF + r // 2 * BLOCKS, BLOCKS)
-        whole = own_ref[:, cols] + up_ref[:, cols] + down_ref[:, cols]
+        whole = above(up_a_ref[:, cols] + down_a_ref[:, cols], up_b_ref[:, cols] + down_b_ref[:, cols])
+        whole = own_ref[:, cols] + whole
         if i == TILE_ROWS:
             last = whole[0:1, 0:1]
         sh[rows, :], sl[rows, :] = two(whole)
@@ -364,8 +371,8 @@
     _, particles, touched, _ = tiles.shape
     entries = particles * touched
     late = (slab_pos >= SLABS // 2).astype(jnp.int32)
-    heights = [BLOCKS, BLOCKS, BLOCKS // 2, BLOCKS // 2] + [BLOCKS] * 5
-    own, ahead, far_a, far_b, behind, *sent = pl.pallas_call(
+    heights = [BLOCKS] + [BLOCKS // 2] * 14
+    own, *halves = pl.pallas_call(
         place_kernel,
         grid=(2,),
         out_shape=tuple(jax.ShapeDtypeStruct((h, tile_width), f32) for h in heights),
@@ -385,35 +392,42 @@
     )(slab_pos.reshape(1), group_pos.reshape(1), tile_index[0].T, pose_bin, bin_gain, tiles[0])
     here = ("particle", "slab")
     up, down = ring_pairs(1), ring_pairs(-1)
-    cut = BLOCKS // 2
 
     def send(part, pairs):
         return lax.ppermute(part, here, pairs)
 
-    come = [send(sent[i], mirror_pairs(e)) for i, e in enumerate((3, -3, 1, -1))]
-    rise, sink = send(far_a, up), send(far_b, down)
-    rise = jnp.concatenate([come[0][:cut] + rise, come[0][cut:]], axis=0)
-    sink = jnp.concatenate([come[1][:cut], come[1][cut:] + sink], axis=0)
-    rise, sink = send(rise, up), send(sink, down)
-    rise, sink = send(ahead + rise, up), send(behind + sink, down)
-    rise, sink = send(come[2] + rise, up), send(come[3] + sink, down)
+    ahead, far, behind, *sent = [halves[i : i + 2] for i in range(0, 14, 2)]
+    come = [[send(sent[i][half], mirror_pairs(e)) for half in range(2)] for i, e in enumerate((3, -3, 1, -1))]
+    rise, sink = [], []
+    for half in range(2):
+        for way, done, (first, own_part, last), pairs in (
+            ("rise", rise, (come[0], ahead, come[2]), up),
+            ("sink", sink, (come[1], behind, come[3]), down),
+        ):
+            part = first[half]
+            if (way == "rise") == (half == 0):
+                part = part + send(far[half], pairs)
+            part = send(part, pairs)
+            part = send(own_part[half] + part, pairs)
+            done.append(send(last[half] + part, pairs))
     plane = (slab_pos * 8 + group_pos * 2 + late).reshape(1)
 
     constants = [jnp.asarray(t) for t in tables()]
     sent = pl.pallas_call(
         planes_kernel,
         out_shape=pltpu.HBM((SENDERS // 4, 8, BANDS // 2, 8, LANES), f32),
-        in_specs=[SMEM, SMEM] + [VMEM] * 5,
+        in_specs=[SMEM, SMEM] + [VMEM] * 7,
         out_specs=pl.BlockSpec(memory_space=pltpu.HBM),
         scratch_shapes=[pltpu.VMEM((2 * BOX, BOX), bf16)] * 2
         + [
             pltpu.VMEM((BOX, BOX), f32),
             pltpu.VMEM((BANDS // 2, SENDERS // 4, 8, 8, LANES), f32),
             pltpu.SemaphoreType.DMA((BANDS // 2,)),
-        ],
+        ]
+        + [pltpu.VMEM((2, 2, BOX, BOX), bf16)] * 2,
         name="planes",
         compiler_params=pltpu.CompilerParams(vmem_limit_bytes=16 * 2**20),
-    )(cutoffs, plane, own, rise, sink, *constants[:2])
+    )(cutoffs, plane, own, *rise, *sink, *constants[:2])
     gathered = lax.all_to_all(sent.reshape(2 * SENDERS, PER, LANES), everyone, split_axis=0, concat_axis=0, tiled=True)
     gathered = gathered.reshape(2 * SENDERS * PER, LANES)
     side_flag = jnp.where(jnp.arange(LANES, dtype=jnp.int32) == 0, side_pos, 0)

time: 222 us -> 216 us (0.973)
  waiting for transfers between devices: 67.6 us -> 37.3 us
  starting transfers between devices: 38.2 us -> 63.1 us
    ppermute x12 -> x22, waiting for transfers between devices: 47.2 us -> 16.9 us  [send(): return lax.ppermute(part, here, pairs)]
    ppermute x12 -> x22, starting transfers between devices: 30.5 us -> 55.3 us  [send(): return lax.ppermute(part, here, pairs)]
  transfers between devices with their start and end apart: 19 -> 29, of which waited for: 10 -> 9; matrix products, arithmetic and copies ran while one was open for 1% -> 1% of each run, Pallas kernels for 0% -> 0%
where the time goes in v8:
time: 216 us; the launch traced here: 215 us
  blocking collectives  92.8 us (43%)
  starting transfers between devices  63.1 us (29%)
  waiting for transfers between devices  37.3 us (17%)
  Pallas kernels  19 us (9%)
    all_to_all x1, blocking collectives, on_device(): lax.all_to_all(sent.reshape(2 * SENDERS, PER, LANES), everyone, split_axi...  92.8 us
    ppermute x22, starting transfers between devices, send(): return lax.ppermute(part, here, pairs)  55.3 us
    ppermute x22, waiting for transfers between devices, send(): return lax.ppermute(part, here, pairs)  16.9 us
    ppermute x1, waiting for transfers between devices, on_device(): near = lax.ppermute(near, everyone, home_pairs(0))  11.2 us
    ppermute x3, waiting for transfers between devices, on_device(): edges = [lax.ppermute(edge, everyone, row_pairs(n, 1)) for n in (0, 1, -1)]  9.17 us
    pallas_call x1, Pallas kernels, on_device(): pl.pallas_call(planes_kernel, out_shape=pltpu.HBM((SENDERS // 4, 8, BANDS...  5.66 us
    pallas_call x1, Pallas kernels, on_device(): pl.pallas_call(place_kernel, grid=(2,), out_shape=tuple((jax.ShapeDtypeSt...  4.98 us
    pallas_call x1, Pallas kernels, on_device(): pl.pallas_call(blend_kernel, grid=(steps,), out_shape=(block_shape, block...  4.74 us
  transfers between devices with their start and end apart: 29, of which 9 were waited for; matrix products, arithmetic and copies ran while one was open for 1% of the time, Pallas kernels for 0%

profile of v8, /device:TPU:1, one launch (start us, length us, event | category | flops | bytes accessed | tf_op | source)
XLA Modules:
  0.0 215.0 jit_solution(16286835768322081756)
XLA Ops:
  0.0 5.0 %place.1 = (f32[32,4096]{1,0:T(8,128)}, f32[16,4096]{1,0:T(8,128)}, f32[16,4096]{1,0:T(8,128)}, f32[16,4096]{1,0:T(8,128)}, f32[16,4096]{1,0:T(8,128)}, /*index=...) custom-call(s32[1]{0:T(128)} %bitcast.1.slab_ref, ...), custom_call_target="tpu_custom_call" | custom-call | tf_op jit(solution)/shard_map/place/pallas_call | solution.py:375
  5.0 5.8 %collective-permute-start.1 = (f32[16,4096]{1,0:T(8,128)}, f32[16,4096]{1,0:T(8,128)S(1)}, u32[]{:S(2)}, u32[]{:S(2)}) collective-permute-start(f32[16,4096]{1,0:T(8,128)} %get-tuple-element.30), channel_id=1, source_target_pairs={{0,60},{4,56},{8,52},{12,48},{16,44},{20,40},{24,36},{28,32},{32,2... | collective-permute-start | bytes 786440 | tf_op jit(solution)/shard_map/ppermute | solution.py:397
  10.9 1.6 collective-permute-start.2
  12.5 0.1 collective-permute-start.7
  12.6 4.7 %collective-permute-start.12 = (f32[16,4096]{1,0:T(8,128)}, f32[16,4096]{1,0:T(8,128)S(1)}, u32[]{:S(2)}, u32[]{:S(2)}) collective-permute-start(f32[16,4096]{1,0:T(8,128)} %get-tuple-element.37), channel_id=1, source_target_pairs={{0,60},{4,56},{8,52},{12,48},{16,44},{20,40},{24,36},{28,32},{32,2... | collective-permute-start | bytes 786440 | tf_op jit(solution)/shard_map/ppermute | solution.py:397
  17.3 0.1 collective-permute-start.17
  17.4 0.0 collective-permute-done.1
  17.4 5.1 %collective-permute-start.18 = (f32[16,4096]{1,0:T(8,128)}, f32[16,4096]{1,0:T(8,128)S(1)}, u32[]{:S(2)}, u32[]{:S(2)}) collective-permute-start(f32[16,4096]{1,0:T(8,128)} %get-tuple-element.41), channel_id=1, source_target_pairs={{0,194},{4,198},{8,202},{12,206},{16,210},{20,214},{24,218},{28,22... | collective-permute-start | bytes 786440 | tf_op jit(solution)/shard_map/ppermute | solution.py:397
  22.5 0.0 collective-permute-done.2
  22.6 0.1 collective-permute-start.3
  22.7 0.0 collective-permute-done.7
  22.7 1.6 collective-permute-start.8
  24.3 4.0 %collective-permute-done.12 = f32[16,4096]{1,0:T(8,128)S(1)} collective-permute-done((f32[16,4096]{1,0:T(8,128)}, f32[16,4096]{1,0:T(8,128)S(1)}, u32[]{:S(2)}, u32[]{:S(2)}) %collective-permute-start.12) | collective-permute-done | bytes 262176 | tf_op jit(solution)/shard_map/ppermute | solution.py:397
  28.3 5.6 %collective-permute-start.13 = (f32[16,4096]{1,0:T(8,128)S(1)}, f32[16,4096]{1,0:T(8,128)S(1)}, u32[]{:S(2)}, u32[]{:S(2)}) collective-permute-start(f32[16,4096]{1,0:T(8,128)S(1)} %collective-permute-done.12), channel_id=1, source_target_pairs={{0,194},{4,198},{8,202},{12,206},{16,210},{20,214},{24,218},{28,22... | collective-permute-start | bytes 786440 | tf_op jit(solution)/shard_map/ppermute | solution.py:397
  33.9 0.0 collective-permute-done.17
  33.9 0.0 collective-permute-done.18
  34.0 5.7 %collective-permute-start.19 = (f32[16,4096]{1,0:T(8,128)S(1)}, f32[16,4096]{1,0:T(8,128)S(1)}, u32[]{:S(2)}, u32[]{:S(2)}) collective-permute-start(f32[16,4096]{1,0:T(8,128)S(1)} %add.50), channel_id=1, source_target_pairs={{0,194},{4,198},{8,202},{12,206},{16,210},{20,214},{24,218},{28,22... | collective-permute-start | bytes 786440 | tf_op jit(solution)/shard_map/ppermute | solution.py:397
  39.6 4.5 %collective-permute-start = (f32[16,4096]{1,0:T(8,128)}, f32[16,4096]{1,0:T(8,128)S(1)}, u32[]{:S(2)}, u32[]{:S(2)}) collective-permute-start(f32[16,4096]{1,0:T(8,128)} %get-tuple-element.28), channel_id=1, source_target_pairs={{0,60},{4,56},{8,52},{12,48},{16,44},{20,40},{24,36},{28,32},{32,1... | collective-permute-start | bytes 786440 | tf_op jit(solution)/shard_map/ppermute | solution.py:397
  44.1 0.0 collective-permute-done.3
  44.1 1.6 collective-permute-start.6
  45.7 1.0 add.44
  46.7 0.1 collective-permute-start.4
  46.9 2.2 %collective-permute-start.11 = (f32[16,4096]{1,0:T(8,128)S(1)}, f32[16,4096]{1,0:T(8,128)S(1)}, u32[]{:S(2)}, u32[]{:S(2)}) collective-permute-start(f32[16,4096]{1,0:T(8,128)S(1)} %copy-done.9), channel_id=1, source_target_pairs={{0,60},{4,56},{8,52},{12,48},{16,44},{20,40},{24,36},{28,32},{32,2... | collective-permute-start | bytes 786440 | tf_op jit(solution)/shard_map/ppermute | solution.py:397
  49.1 0.0 copy-start
  49.1 0.0 copy-start.1
  49.1 0.0 copy-start.2
  49.1 0.0 copy-start.4
  49.1 0.1 collective-permute-start.9
  49.3 2.4 %collective-permute-done = f32[16,4096]{1,0:T(8,128)S(1)} collective-permute-done((f32[16,4096]{1,0:T(8,128)}, f32[16,4096]{1,0:T(8,128)S(1)}, u32[]{:S(2)}, u32[]{:S(2)}) %collective-permute-start) | collective-permute-done | bytes 262176 | tf_op jit(solution)/shard_map/ppermute | solution.py:397
  51.6 2.5 %collective-permute-start.14 = (f32[16,4096]{1,0:T(8,128)S(1)}, f32[16,4096]{1,0:T(8,128)S(1)}, u32[]{:S(2)}, u32[]{:S(2)}) collective-permute-start(f32[16,4096]{1,0:T(8,128)S(1)} %add.48), channel_id=1, source_target_pairs={{0,194},{4,198},{8,202},{12,206},{16,210},{20,214},{24,218},{28,22... | collective-permute-start | bytes 786440 | tf_op jit(solution)/shard_map/ppermute | solution.py:397
  54.2 3.7 %collective-permute-done.6 = f32[16,4096]{1,0:T(8,128)S(1)} collective-permute-done((f32[16,4096]{1,0:T(8,128)}, f32[16,4096]{1,0:T(8,128)S(1)}, u32[]{:S(2)}, u32[]{:S(2)}) %collective-permute-start.6) | collective-permute-done | bytes 262176 | tf_op jit(solution)/shard_map/ppermute | solution.py:397
  57.9 2.2 %collective-permute-start.16 = (f32[16,4096]{1,0:T(8,128)S(1)}, f32[16,4096]{1,0:T(8,128)S(1)}, u32[]{:S(2)}, u32[]{:S(2)}) collective-permute-start(f32[16,4096]{1,0:T(8,128)S(1)} %copy-done.8), channel_id=1, source_target_pairs={{0,60},{4,56},{8,52},{12,48},{16,44},{20,40},{24,36},{28,32},{32,2... | collective-permute-start | bytes 786440 | tf_op jit(solution)/shard_map/ppermute | solution.py:397
  60.0 0.0 collective-permute-done.4
  60.0 4.0 %collective-permute-start.20 = (f32[16,4096]{1,0:T(8,128)S(1)}, f32[16,4096]{1,0:T(8,128)S(1)}, u32[]{:S(2)}, u32[]{:S(2)}) collective-permute-start(f32[16,4096]{1,0:T(8,128)S(1)} %add.51), channel_id=1, source_target_pairs={{0,194},{4,198},{8,202},{12,206},{16,210},{20,214},{24,218},{28,22... | collective-permute-start | bytes 786440 | tf_op jit(solution)/shard_map/ppermute | solution.py:397
  64.1 0.1 collective-permute-start.5
  64.2 0.5 collective-permute-done.11
  64.8 0.0 collective-permute-start.10
  64.8 0.0 collective-permute-done.14
  64.8 2.7 %collective-permute-start.15 = (f32[16,4096]{1,0:T(8,128)S(1)}, f32[16,4096]{1,0:T(8,128)S(1)}, u32[]{:S(2)}, u32[]{:S(2)}) collective-permute-start(f32[16,4096]{1,0:T(8,128)S(1)} %add.49), channel_id=1, source_target_pairs={{0,194},{4,198},{8,202},{12,206},{16,210},{20,214},{24,218},{28,22... | collective-permute-start | bytes 786440 | tf_op jit(solution)/shard_map/ppermute | solution.py:397
  67.5 0.2 collective-permute-done.16
  67.8 4.8 %collective-permute-start.21 = (f32[16,4096]{1,0:T(8,128)S(1)}, f32[16,4096]{1,0:T(8,128)S(1)}, u32[]{:S(2)}, u32[]{:S(2)}) collective-permute-start(f32[16,4096]{1,0:T(8,128)S(1)} %add.52), channel_id=1, source_target_pairs={{0,194},{4,198},{8,202},{12,206},{16,210},{20,214},{24,218},{28,22... | collective-permute-start | bytes 786440 | tf_op jit(solution)/shard_map/ppermute | solution.py:397
  72.6 0.0 collective-permute-done.5.up_a_ref
  72.6 2.3 %collective-permute-done.10.up_b_ref = f32[16,4096]{1,0:T(8,128)S(1)} collective-permute-done((f32[16,4096]{1,0:T(8,128)S(1)}, f32[16,4096]{1,0:T(8,128)S(1)}, u32[]{:S(2)}, u32[]{:S(2)}) %collective-permute-start.10) | collective-permute-done | bytes 262176 | tf_op jit(solution)/shard_map/ppermute | solution.py:397
  74.9 0.0 collective-permute-done.15.down_a_ref
  74.9 3.8 %collective-permute-done.21.down_b_ref = f32[16,4096]{1,0:T(8,128)S(1)} collective-permute-done((f32[16,4096]{1,0:T(8,128)S(1)}, f32[16,4096]{1,0:T(8,128)S(1)}, u32[]{:S(2)}, u32[]{:S(2)}) %collective-permute-start.21) | collective-permute-done | bytes 262176 | tf_op jit(solution)/shard_map/ppermute | solution.py:397
  78.7 5.7 %planes.1 = f32[32,8,3,8,128]{4,3,2,1,0:T(8,128)} custom-call(s32[6]{0:T(128)S(1)} %copy-done.4, s32[1]{0:T(128)} %bitcast.kz_ref, f32[32,4096]{1,0:T(8,128)S(1)} %copy-done, f32[16,4096]{1,0:T(8,128)S(1)} %collective-permute-done.5.up_a_ref, f32[16,4096]{1,0:T(8,128)S(1)} %collective-permute-done.10.up_b_ref, ...), custom_call_target="tpu_custom_call" | custom-call | tf_op jit(solution)/shard_map/planes/pallas_call | solution.py:416
  84.4 0.0 copy-start.3
  84.4 92.8 %all_to_all.5 = f32[256,24,128]{2,1,0:T(8,128)S(1)} all-to-all(f32[256,24,128]{2,1,0:T(8,128)} %bitcast.14), channel_id=1, replica_groups=mesh['particle'=4,'slab'=32,'half'=2] {'particle','slab','half'}, dimensions={0} | all-to-all | bytes 6291456 | tf_op jit(solution)/shard_map/all_to_all | solution.py:431
  177.2 3.6 %depth.1 = (f32[6,2,256,128]{3,2,1,0:T(8,128)S(1)}, f32[6,2,256,128]{3,2,1,0:T(8,128)S(1)}, f32[6,256,128]{2,1,0:T(8,128)}, f32[6,256,128]{2,1,0:T(8,128)}, f32[64,128]{1,0:T(8,128)S(1)}) custom-call(f32[6144,128]{1,0:T(8,128)S(1)} %bitcast.13, bf16[2,256,256]{2,1,0:T(8,128)(2,1)S(1)} %copy-done.3), custom_call_target="tpu_custom_call" | custom-call | tf_op jit(solution)/shard_map/depth/pallas_call | solution.py:441
  180.8 0.0 collective-permute-start.23
  180.8 1.7 collective-permute-start.22
  182.5 0.0 collective-permute-start.26
  182.6 1.7 collective-permute-start.25
  184.3 0.9 collective-permute-start.24
  185.2 9.2 %collective-permute-done.26.edge_after_ref = f32[64,128]{1,0:T(8,128)S(1)} collective-permute-done((f32[64,128]{1,0:T(8,128)S(1)}, f32[64,128]{1,0:T(8,128)S(1)}, u32[]{:S(2)}, u32[]{:S(2)}) %collective-permute-start.26) | collective-permute-done | bytes 32800 | tf_op jit(solution)/shard_map/ppermute | solution.py:456
  194.4 0.0 collective-permute-done.25.edge_before_ref
  194.4 0.0 collective-permute-done.24.edge_ref
  194.4 0.0 collective-permute-done.23.after_ref
  194.4 4.7 %blend.1 = (f32[2,256,128]{2,1,0:T(8,128)}, f32[2,256,128]{2,1,0:T(8,128)S(1)}) custom-call(s32[128]{0:T(128)S(1)} %compare_select_fusion.side_ref, f32[6,2,256,128]{3,2,1,0:T(8,128)S(1)} %get-tuple-element.42.low_half_ref, f32[6,2,256,128]{3,2,1,0:T(8,128)S(1)} %get-tuple-element.43.high_half_ref, f32[6,256,128]{2,1,0:T(8,128)} %get-tuple-element.44.first_ref, ...), custom_call_target="tpu_custom_call" | custom-call | tf_op jit(solution)/shard_map/blend/pallas_call | solution.py:459
  199.2 3.2 %collective-permute-start.27 = (f32[2,256,128]{2,1,0:T(8,128)}, f32[2,256,128]{2,1,0:T(8,128)S(1)}, u32[]{:S(2)}, u32[]{:S(2)}) collective-permute-start(f32[2,256,128]{2,1,0:T(8,128)} %get-tuple-element.47), channel_id=1, source_target_pairs={{0,0},{1,2},{6,1},{7,3},{4,4},{5,6},{2,5},{3,7},{8,8},{9,10},{14,9... | collective-permute-start | bytes 786440 | tf_op jit(solution)/shard_map/ppermute | solution.py:469
  202.4 0.1 collective-permute-start.28
  202.5 11.2 %collective-permute-done.27 = f32[2,256,128]{2,1,0:T(8,128)S(1)} collective-permute-done((f32[2,256,128]{2,1,0:T(8,128)}, f32[2,256,128]{2,1,0:T(8,128)S(1)}, u32[]{:S(2)}, u32[]{:S(2)}) %collective-permute-start.27) | collective-permute-done | bytes 262176 | tf_op jit(solution)/shard_map/ppermute | solution.py:469
  213.7 0.0 collective-permute-done.28
  213.8 1.2 copy.9
  (33 shorter events, 0.4 us)
Async XLA Ops:
  5.0 41.8 %copy-start.7 = (f32[16,4096]{1,0:T(8,128)S(1)}, f32[16,4096]{1,0:T(8,128)}, u32[]{:S(2)}) copy-start(f32[16,4096]{1,0:T(8,128)} %get-tuple-element.33) | copy-start | bytes 786436
  5.0 41.9 %copy-start.9 = (f32[16,4096]{1,0:T(8,128)S(1)}, f32[16,4096]{1,0:T(8,128)}, u32[]{:S(2)}) copy-start(f32[16,4096]{1,0:T(8,128)} %get-tuple-element.35) | copy-start | bytes 786436
  5.0 44.0 %copy-start.6 = (f32[16,4096]{1,0:T(8,128)S(1)}, f32[16,4096]{1,0:T(8,128)}, u32[]{:S(2)}) copy-start(f32[16,4096]{1,0:T(8,128)} %get-tuple-element.36) | copy-start | bytes 786436
  5.0 44.2 %copy-start.5 = (f32[16,4096]{1,0:T(8,128)S(1)}, f32[16,4096]{1,0:T(8,128)}, u32[]{:S(2)}) copy-start(f32[16,4096]{1,0:T(8,128)} %get-tuple-element.39) | copy-start | bytes 786436
  5.0 12.4 %collective-permute-start.1 = (f32[16,4096]{1,0:T(8,128)}, f32[16,4096]{1,0:T(8,128)S(1)}, u32[]{:S(2)}, u32[]{:S(2)}) collective-permute-start(f32[16,4096]{1,0:T(8,128)} %get-tuple-element.30), channel_id=1, source_target_pairs={{0,60},{4,56},{8,52},{12,48},{16,44},{20,40},{24,36},{28,32},{32,2... | collective-permute-start | bytes 786440 | tf_op jit(solution)/shard_map/ppermute | solution.py:397
  10.9 11.7 %collective-permute-start.2 = (f32[16,4096]{1,0:T(8,128)}, f32[16,4096]{1,0:T(8,128)S(1)}, u32[]{:S(2)}, u32[]{:S(2)}) collective-permute-start(f32[16,4096]{1,0:T(8,128)} %get-tuple-element.31), channel_id=1, source_target_pairs={{0,2},{4,6},{8,10},{12,14},{16,18},{20,22},{24,26},{28,30},{32,34}... | collective-permute-start | bytes 786440 | tf_op jit(solution)/shard_map/ppermute | solution.py:397
  12.5 10.2 %collective-permute-start.7 = (f32[16,4096]{1,0:T(8,128)}, f32[16,4096]{1,0:T(8,128)S(1)}, u32[]{:S(2)}, u32[]{:S(2)}) collective-permute-start(f32[16,4096]{1,0:T(8,128)} %get-tuple-element.34), channel_id=1, source_target_pairs={{0,60},{4,56},{8,52},{12,48},{16,44},{20,40},{24,36},{28,32},{32,2... | collective-permute-start | bytes 786440 | tf_op jit(solution)/shard_map/ppermute | solution.py:397
  12.6 15.7 %collective-permute-start.12 = (f32[16,4096]{1,0:T(8,128)}, f32[16,4096]{1,0:T(8,128)S(1)}, u32[]{:S(2)}, u32[]{:S(2)}) collective-permute-start(f32[16,4096]{1,0:T(8,128)} %get-tuple-element.37), channel_id=1, source_target_pairs={{0,60},{4,56},{8,52},{12,48},{16,44},{20,40},{24,36},{28,32},{32,2... | collective-permute-start | bytes 786440 | tf_op jit(solution)/shard_map/ppermute | solution.py:397
  17.3 16.6 %collective-permute-start.17 = (f32[16,4096]{1,0:T(8,128)}, f32[16,4096]{1,0:T(8,128)S(1)}, u32[]{:S(2)}, u32[]{:S(2)}) collective-permute-start(f32[16,4096]{1,0:T(8,128)} %get-tuple-element.40), channel_id=1, source_target_pairs={{0,60},{4,56},{8,52},{12,48},{16,44},{20,40},{24,36},{28,32},{32,2... | collective-permute-start | bytes 786440 | tf_op jit(solution)/shard_map/ppermute | solution.py:397
  17.4 16.5 %collective-permute-start.18 = (f32[16,4096]{1,0:T(8,128)}, f32[16,4096]{1,0:T(8,128)S(1)}, u32[]{:S(2)}, u32[]{:S(2)}) collective-permute-start(f32[16,4096]{1,0:T(8,128)} %get-tuple-element.41), channel_id=1, source_target_pairs={{0,194},{4,198},{8,202},{12,206},{16,210},{20,214},{24,218},{28,22... | collective-permute-start | bytes 786440 | tf_op jit(solution)/shard_map/ppermute | solution.py:397
  22.6 35.3 %copy-start.8 = (f32[16,4096]{1,0:T(8,128)S(1)}, f32[16,4096]{1,0:T(8,128)}, u32[]{:S(2)}) copy-start(f32[16,4096]{1,0:T(8,128)} %get-tuple-element.38) | copy-start | bytes 786436
  22.6 21.6 %collective-permute-start.3 = (f32[16,4096]{1,0:T(8,128)S(1)}, f32[16,4096]{1,0:T(8,128)S(1)}, u32[]{:S(2)}, u32[]{:S(2)}) collective-permute-start(f32[16,4096]{1,0:T(8,128)S(1)} %add.43), channel_id=1, source_target_pairs={{0,2},{4,6},{8,10},{12,14},{16,18},{20,22},{24,26},{28,30},{32,34}... | collective-permute-start | bytes 786440 | tf_op jit(solution)/shard_map/ppermute | solution.py:397
  22.7 24.0 %collective-permute-start.8 = (f32[16,4096]{1,0:T(8,128)S(1)}, f32[16,4096]{1,0:T(8,128)S(1)}, u32[]{:S(2)}, u32[]{:S(2)}) collective-permute-start(f32[16,4096]{1,0:T(8,128)S(1)} %collective-permute-done.7), channel_id=1, source_target_pairs={{0,2},{4,6},{8,10},{12,14},{16,18},{20,22},{24,26},{28,30},{32,34}... | collective-permute-start | bytes 786440 | tf_op jit(solution)/shard_map/ppermute | solution.py:397
  28.3 18.6 %collective-permute-start.13 = (f32[16,4096]{1,0:T(8,128)S(1)}, f32[16,4096]{1,0:T(8,128)S(1)}, u32[]{:S(2)}, u32[]{:S(2)}) collective-permute-start(f32[16,4096]{1,0:T(8,128)S(1)} %collective-permute-done.12), channel_id=1, source_target_pairs={{0,194},{4,198},{8,202},{12,206},{16,210},{20,214},{24,218},{28,22... | collective-permute-start | bytes 786440 | tf_op jit(solution)/shard_map/ppermute | solution.py:397
  34.0 15.2 %collective-permute-start.19 = (f32[16,4096]{1,0:T(8,128)S(1)}, f32[16,4096]{1,0:T(8,128)S(1)}, u32[]{:S(2)}, u32[]{:S(2)}) collective-permute-start(f32[16,4096]{1,0:T(8,128)S(1)} %add.50), channel_id=1, source_target_pairs={{0,194},{4,198},{8,202},{12,206},{16,210},{20,214},{24,218},{28,22... | collective-permute-start | bytes 786440 | tf_op jit(solution)/shard_map/ppermute | solution.py:397
  39.6 12.0 %collective-permute-start = (f32[16,4096]{1,0:T(8,128)}, f32[16,4096]{1,0:T(8,128)S(1)}, u32[]{:S(2)}, u32[]{:S(2)}) collective-permute-start(f32[16,4096]{1,0:T(8,128)} %get-tuple-element.28), channel_id=1, source_target_pairs={{0,60},{4,56},{8,52},{12,48},{16,44},{20,40},{24,36},{28,32},{32,1... | collective-permute-start | bytes 786440 | tf_op jit(solution)/shard_map/ppermute | solution.py:397
  44.1 13.7 %collective-permute-start.6 = (f32[16,4096]{1,0:T(8,128)}, f32[16,4096]{1,0:T(8,128)S(1)}, u32[]{:S(2)}, u32[]{:S(2)}) collective-permute-start(f32[16,4096]{1,0:T(8,128)} %get-tuple-element.32), channel_id=1, source_target_pairs={{0,60},{4,56},{8,52},{12,48},{16,44},{20,40},{24,36},{28,32},{32,1... | collective-permute-start | bytes 786440 | tf_op jit(solution)/shard_map/ppermute | solution.py:397
  46.7 13.3 %collective-permute-start.4 = (f32[16,4096]{1,0:T(8,128)S(1)}, f32[16,4096]{1,0:T(8,128)S(1)}, u32[]{:S(2)}, u32[]{:S(2)}) collective-permute-start(f32[16,4096]{1,0:T(8,128)S(1)} %add.44), channel_id=1, source_target_pairs={{0,2},{4,6},{8,10},{12,14},{16,18},{20,22},{24,26},{28,30},{32,34}... | collective-permute-start | bytes 786440 | tf_op jit(solution)/shard_map/ppermute | solution.py:397
  46.9 17.9 %collective-permute-start.11 = (f32[16,4096]{1,0:T(8,128)S(1)}, f32[16,4096]{1,0:T(8,128)S(1)}, u32[]{:S(2)}, u32[]{:S(2)}) collective-permute-start(f32[16,4096]{1,0:T(8,128)S(1)} %copy-done.9), channel_id=1, source_target_pairs={{0,60},{4,56},{8,52},{12,48},{16,44},{20,40},{24,36},{28,32},{32,2... | collective-permute-start | bytes 786440 | tf_op jit(solution)/shard_map/ppermute | solution.py:397
  49.1 29.7 %copy-start = (f32[32,4096]{1,0:T(8,128)S(1)}, f32[32,4096]{1,0:T(8,128)}, u32[]{:S(2)}) copy-start(f32[32,4096]{1,0:T(8,128)} %get-tuple-element.27.own_ref) | copy-start | bytes 1572868
  49.1 29.6 %copy-start.1 = (bf16[2,2,128,256]{3,2,1,0:T(8,128)(2,1)S(1)}, bf16[2,2,128,256]{3,2,1,0:T(8,128)(2,1)}, u32[]{:S(2)}) copy-start(bf16[2,2,128,256]{3,2,1,0:T(8,128)(2,1)} %constant.40.clone.few_x_ref) | copy-start | bytes 786436
  49.1 29.6 %copy-start.2 = (bf16[2,2,128,256]{3,2,1,0:T(8,128)(2,1)S(1)}, bf16[2,2,128,256]{3,2,1,0:T(8,128)(2,1)}, u32[]{:S(2)}) copy-start(bf16[2,2,128,256]{3,2,1,0:T(8,128)(2,1)} %constant.39.clone.few_y_ref) | copy-start | bytes 786436
  49.1 29.6 %copy-start.4 = (s32[6]{0:T(128)S(1)}, s32[6]{0:T(128)}, u32[]{:S(2)}) copy-start(s32[6]{0:T(128)} %cut_ref.1) | copy-start | bytes 76
  49.1 14.9 %collective-permute-start.9 = (f32[16,4096]{1,0:T(8,128)S(1)}, f32[16,4096]{1,0:T(8,128)S(1)}, u32[]{:S(2)}, u32[]{:S(2)}) collective-permute-start(f32[16,4096]{1,0:T(8,128)S(1)} %add.46), channel_id=1, source_target_pairs={{0,2},{4,6},{8,10},{12,14},{16,18},{20,22},{24,26},{28,30},{32,34}... | collective-permute-start | bytes 786440 | tf_op jit(solution)/shard_map/ppermute | solution.py:397
  51.6 13.1 %collective-permute-start.14 = (f32[16,4096]{1,0:T(8,128)S(1)}, f32[16,4096]{1,0:T(8,128)S(1)}, u32[]{:S(2)}, u32[]{:S(2)}) collective-permute-start(f32[16,4096]{1,0:T(8,128)S(1)} %add.48), channel_id=1, source_target_pairs={{0,194},{4,198},{8,202},{12,206},{16,210},{20,214},{24,218},{28,22... | collective-permute-start | bytes 786440 | tf_op jit(solution)/shard_map/ppermute | solution.py:397
  57.9 9.9 %collective-permute-start.16 = (f32[16,4096]{1,0:T(8,128)S(1)}, f32[16,4096]{1,0:T(8,128)S(1)}, u32[]{:S(2)}, u32[]{:S(2)}) collective-permute-start(f32[16,4096]{1,0:T(8,128)S(1)} %copy-done.8), channel_id=1, source_target_pairs={{0,60},{4,56},{8,52},{12,48},{16,44},{20,40},{24,36},{28,32},{32,2... | collective-permute-start | bytes 786440 | tf_op jit(solution)/shard_map/ppermute | solution.py:397
  60.0 7.7 %collective-permute-start.20 = (f32[16,4096]{1,0:T(8,128)S(1)}, f32[16,4096]{1,0:T(8,128)S(1)}, u32[]{:S(2)}, u32[]{:S(2)}) collective-permute-start(f32[16,4096]{1,0:T(8,128)S(1)} %add.51), channel_id=1, source_target_pairs={{0,194},{4,198},{8,202},{12,206},{16,210},{20,214},{24,218},{28,22... | collective-permute-start | bytes 786440 | tf_op jit(solution)/shard_map/ppermute | solution.py:397
  64.1 8.5 %collective-permute-start.5 = (f32[16,4096]{1,0:T(8,128)S(1)}, f32[16,4096]{1,0:T(8,128)S(1)}, u32[]{:S(2)}, u32[]{:S(2)}) collective-permute-start(f32[16,4096]{1,0:T(8,128)S(1)} %add.45), channel_id=1, source_target_pairs={{0,2},{4,6},{8,10},{12,14},{16,18},{20,22},{24,26},{28,30},{32,34}... | collective-permute-start | bytes 786440 | tf_op jit(solution)/shard_map/ppermute | solution.py:397
  64.8 10.2 %collective-permute-start.10 = (f32[16,4096]{1,0:T(8,128)S(1)}, f32[16,4096]{1,0:T(8,128)S(1)}, u32[]{:S(2)}, u32[]{:S(2)}) collective-permute-start(f32[16,4096]{1,0:T(8,128)S(1)} %add.47), channel_id=1, source_target_pairs={{0,2},{4,6},{8,10},{12,14},{16,18},{20,22},{24,26},{28,30},{32,34}... | collective-permute-start | bytes 786440 | tf_op jit(solution)/shard_map/ppermute | solution.py:397
  64.8 10.1 %collective-permute-start.15 = (f32[16,4096]{1,0:T(8,128)S(1)}, f32[16,4096]{1,0:T(8,128)S(1)}, u32[]{:S(2)}, u32[]{:S(2)}) collective-permute-start(f32[16,4096]{1,0:T(8,128)S(1)} %add.49), channel_id=1, source_target_pairs={{0,194},{4,198},{8,202},{12,206},{16,210},{20,214},{24,218},{28,22... | collective-permute-start | bytes 786440 | tf_op jit(solution)/shard_map/ppermute | solution.py:397
  67.8 11.0 %collective-permute-start.21 = (f32[16,4096]{1,0:T(8,128)S(1)}, f32[16,4096]{1,0:T(8,128)S(1)}, u32[]{:S(2)}, u32[]{:S(2)}) collective-permute-start(f32[16,4096]{1,0:T(8,128)S(1)} %add.52), channel_id=1, source_target_pairs={{0,194},{4,198},{8,202},{12,206},{16,210},{20,214},{24,218},{28,22... | collective-permute-start | bytes 786440 | tf_op jit(solution)/shard_map/ppermute | solution.py:397
  84.4 92.8 %copy-start.3 = (bf16[2,256,256]{2,1,0:T(8,128)(2,1)S(1)}, bf16[2,256,256]{2,1,0:T(8,128)(2,1)}, u32[]{:S(2)}) copy-start(bf16[2,256,256]{2,1,0:T(8,128)(2,1)} %constant.41.clone.z_ref) | copy-start | bytes 786436
  180.8 13.6 %collective-permute-start.23 = (f32[6,256,128]{2,1,0:T(8,128)}, f32[6,256,128]{2,1,0:T(8,128)}, u32[]{:S(2)}, u32[]{:S(2)}) collective-permute-start(f32[6,256,128]{2,1,0:T(8,128)} %get-tuple-element.44.first_ref), channel_id=1, source_target_pairs={{0,253},{6,251},{1,0},{7,6},{4,1},{2,7},{5,4},{3,2},{8,5},{14,3},{... | collective-permute-start | bytes 2359304 | tf_op jit(solution)/shard_map/ppermute | solution.py:455
  180.8 13.6 %collective-permute-start.22 = (f32[6,256,128]{2,1,0:T(8,128)}, f32[6,256,128]{2,1,0:T(8,128)}, u32[]{:S(2)}, u32[]{:S(2)}) collective-permute-start(f32[6,256,128]{2,1,0:T(8,128)} %get-tuple-element.45.second_ref), channel_id=1, source_target_pairs={{0,1},{6,7},{1,4},{7,2},{4,5},{2,3},{5,8},{3,14},{8,9},{14,15},{9,... | collective-permute-start | bytes 2359304 | tf_op jit(solution)/shard_map/ppermute | solution.py:454
  182.5 11.9 %collective-permute-start.26 = (f32[64,128]{1,0:T(8,128)S(1)}, f32[64,128]{1,0:T(8,128)S(1)}, u32[]{:S(2)}, u32[]{:S(2)}) collective-permute-start(f32[64,128]{1,0:T(8,128)S(1)} %get-tuple-element.46), channel_id=1, source_target_pairs={{0,251},{6,253},{1,6},{7,0},{4,7},{2,1},{5,2},{3,4},{8,3},{14,5},{... | collective-permute-start | bytes 98312 | tf_op jit(solution)/shard_map/ppermute | solution.py:456
  182.6 11.9 %collective-permute-start.25 = (f32[64,128]{1,0:T(8,128)S(1)}, f32[64,128]{1,0:T(8,128)S(1)}, u32[]{:S(2)}, u32[]{:S(2)}) collective-permute-start(f32[64,128]{1,0:T(8,128)S(1)} %get-tuple-element.46), channel_id=1, source_target_pairs={{0,7},{6,1},{1,2},{7,4},{4,3},{2,5},{5,14},{3,8},{8,15},{14,9},{9,... | collective-permute-start | bytes 98312 | tf_op jit(solution)/shard_map/ppermute | solution.py:456
  184.3 10.1 %collective-permute-start.24 = (f32[64,128]{1,0:T(8,128)S(1)}, f32[64,128]{1,0:T(8,128)S(1)}, u32[]{:S(2)}, u32[]{:S(2)}) collective-permute-start(f32[64,128]{1,0:T(8,128)S(1)} %get-tuple-element.46), channel_id=1, source_target_pairs={{0,6},{6,0},{1,7},{7,1},{4,2},{2,4},{5,3},{3,5},{8,14},{14,8},{9,1... | collective-permute-start | bytes 98312 | tf_op jit(solution)/shard_map/ppermute | solution.py:456
  199.2 14.6 %collective-permute-start.27 = (f32[2,256,128]{2,1,0:T(8,128)}, f32[2,256,128]{2,1,0:T(8,128)S(1)}, u32[]{:S(2)}, u32[]{:S(2)}) collective-permute-start(f32[2,256,128]{2,1,0:T(8,128)} %get-tuple-element.47), channel_id=1, source_target_pairs={{0,0},{1,2},{6,1},{7,3},{4,4},{5,6},{2,5},{3,7},{8,8},{9,10},{14,9... | collective-permute-start | bytes 786440 | tf_op jit(solution)/shard_map/ppermute | solution.py:469
  202.4 11.3 %collective-permute-start.28 = (f32[2,256,128]{2,1,0:T(8,128)S(1)}, f32[2,256,128]{2,1,0:T(8,128)S(1)}, u32[]{:S(2)}, u32[]{:S(2)}) collective-permute-start(f32[2,256,128]{2,1,0:T(8,128)S(1)} %get-tuple-element.48), channel_id=1, source_target_pairs={{0,1},{1,3},{6,0},{7,2},{4,5},{5,7},{2,4},{3,6},{8,9},{9,11},{14,8... | collective-permute-start | bytes 786440 | tf_op jit(solution)/shard_map/ppermute | solution.py:470
